TPU v7x, 256 devices: a whole 4x4x8 slice. The times are simulated.
256 devices in a mesh: site: 8 (over x, y_lo), blk: 32 (over y_hi, z, core).
Axes of the slice: x: 4, y: 4 (y_hi: 2, y_lo: 2; y = y_hi * 2 + y_lo), z: 8, core: 2. Of those that a mesh axis runs over, the one named last changes fastest.
Arguments:
- corner: bfloat16 [8, 768, 768], P('site', 'blk'), may hold values from -6 to 6
- edge: bfloat16 [8, 768, 64, 768], P('site', 'blk'), may hold values from -0.02734375 to 0.02734375
- proj_left: bfloat16 [8, 768, 64, 768], P('site', 'blk'), may hold values from -0.21875 to 0.21875
- proj_right: bfloat16 [8, 768, 64, 768], P('site', 'blk'), may hold values from -0.21875 to 0.21875
- charge: int32 [8, 768], P('site'), may hold values from 0 to 15, never falling along the last dimension, each value on 1 to 96 neighbouring positions
- cot_left: float32 [8, 768, 768], P('site', 'blk'), may hold values from -2 to 2
- cot_right: float32 [8, 768, 768], P('site', 'blk'), may hold values from -2 to 2
Outputs:
- new_left: bfloat16 [8, 768, 768], P('site', 'blk')
- new_right: bfloat16 [8, 768, 768], P('site', 'blk')
- grad_left: bfloat16 [8, 768, 64, 768], P('site', 'blk')
- grad_right: bfloat16 [8, 768, 64, 768], P('site', 'blk')
Inputs may be any that keep to these rules, and one draw needn't show every extreme that they name: `charge`: sector labels never fall along the bond index; each sector holds 1 to 96 indices.
All inputs are finite; a program needn't handle non-finite values.
Results may differ from a plain program's by a relative error of at most 0.0059.
Values may be sent and summed in bfloat16 or wider, within the bound.
No kernel may reach another device: no remote copies, remote signals or barrier semaphores. Data moves between devices by JAX's collectives and lax.ppermute only.
A program may use at most 64 MiB of HBM per device.

v0:
```python
import jax
import jax.numpy as jnp
from jax import lax
from jax.sharding import PartitionSpec as P

ITERS = 2


def shifted(block, axis, distance):
    devices = range(lax.axis_size(axis))
    route = [((i - distance) % len(devices), i) for i in devices]
    return lax.ppermute(block, axis, route)


def in_one_piece(arrays, axis, dim, along):
    widths = [a.shape[along] for a in arrays]
    both = jnp.concatenate(arrays, axis=along)
    whole = lax.all_gather(both, axis, axis=dim, tiled=True)
    return tuple(jnp.split(whole, [sum(widths[:k]) for k in range(1, len(widths))], axis=along))


def contract_first(left, right):
    return lax.dot_general(
        left, right, (((0,), (0,)), ((), ())), preferred_element_type=jnp.float32
    )


def contract_last(left, right):
    return lax.dot_general(
        left, right, (((1,), (1,)), ((), ())), preferred_element_type=jnp.float32
    )


def body(corner, edge, proj_left, proj_right, charge, cot_left, cot_right):
    rows = corner.shape[1]
    width = corner.shape[2]
    depth = edge.shape[2]
    first_row = lax.axis_index("blk") * rows
    labels = charge[0]
    own_labels = lax.dynamic_slice_in_dim(labels, first_row, rows, 0)
    mask = (own_labels[:, None] == labels[None, :]).astype(jnp.float32)
    here = corner[0]
    prev_corner = shifted(here, "site", 1)
    next_corner = shifted(here, "site", -1)
    edge_flat = edge[0].reshape(rows * depth, width)
    left_flat = proj_left[0].reshape(rows * depth, width)
    right_flat = proj_right[0].reshape(rows * depth, width)

    def partial_term(flat_proj):
        return contract_first(edge_flat, flat_proj)

    summed = lax.psum((partial_term(left_flat), partial_term(right_flat)), "blk")
    enl_left = summed[0].astype(jnp.bfloat16)
    enl_right = summed[1].astype(jnp.bfloat16)
    new_left = (mask * jnp.dot(prev_corner, enl_left, preferred_element_type=jnp.float32)).astype(
        jnp.bfloat16
    )
    new_right = (mask * jnp.dot(next_corner, enl_right, preferred_element_type=jnp.float32)).astype(
        jnp.bfloat16
    )
    adj_left = cot_left[0]
    adj_right = cot_right[0]
    for step in range(ITERS):
        w_left = (mask * adj_left).astype(jnp.bfloat16)
        w_right = (mask * adj_right).astype(jnp.bfloat16)
        back_left = contract_last(w_left, enl_left)
        back_right = contract_last(w_right, enl_right)
        adj_left = cot_left[0] + shifted(back_left, "site", -1)
        adj_right = cot_right[0] + shifted(back_right, "site", 1)
    w_left = (mask * adj_left).astype(jnp.bfloat16)
    w_right = (mask * adj_right).astype(jnp.bfloat16)
    full_prev, full_next, full_wl, full_wr = in_one_piece(
        (prev_corner, next_corner, w_left, w_right), "blk", 0, 1
    )
    mid_whole_left = contract_first(full_prev, full_wl).astype(jnp.bfloat16)
    mid_whole_right = contract_first(full_next, full_wr).astype(jnp.bfloat16)
    grad_flat_left = jnp.dot(edge_flat, mid_whole_left, preferred_element_type=jnp.float32)
    grad_flat_right = jnp.dot(edge_flat, mid_whole_right, preferred_element_type=jnp.float32)
    grad_left = grad_flat_left.astype(jnp.bfloat16).reshape(1, rows, depth, width)
    grad_right = grad_flat_right.astype(jnp.bfloat16).reshape(1, rows, depth, width)
    return (new_left[None], new_right[None], grad_left, grad_right)


def solution(mesh):
    placed = (
        P("site", "blk", None),
        P("site", "blk", None, None),
        P("site", "blk", None, None),
        P("site", "blk", None, None),
        P("site", None),
        P("site", "blk", None),
        P("site", "blk", None),
    )
    return jax.shard_map(
        body,
        mesh=mesh,
        in_specs=placed,
        out_specs=(
            P("site", "blk", None),
            P("site", "blk", None),
            P("site", "blk", None, None),
            P("site", "blk", None, None),
        ),
        check_vma=False,
    )
```

profile of v0, /device:TPU:1, one launch (start us, length us, event | category | flops | bytes accessed | tf_op | source)
XLA Modules:
  0.0 312.5 jit_solution(9137581595843107648)
XLA Ops:
  7.2 0.0 all-gather.2.cloned.1.call-start
  7.2 0.8 reduce
  8.1 0.8 dynamic-slice_bitcast_fusion
  8.9 5.3 %fusion.8 = f32[768,768]{1,0:T(8,128)} fusion(bf16[1,24,64,768]{3,2,1,0:T(8,128)(2,1)} %param.9, bf16[1,24,64,768]{3,2,1,0:T(8,128)(2,1)S(1)} %copy-done), kind=kOutput, calls=%fused_computation.10 | convolution fusion | flops 1811939328 | bytes 7077888 | tf_op jit(solution)/shard_map/dot_general | solution.py:23
  14.1 3.5 %fusion.13 = f32[768,768]{1,0:T(8,128)} fusion(bf16[1,24,64,768]{3,2,1,0:T(8,128)(2,1)S(1)} %copy-done.2, bf16[1,24,64,768]{3,2,1,0:T(8,128)(2,1)S(1)} %copy-done), kind=kOutput, calls=%fused_computation.11 | convolution fusion | flops 1811939328 | bytes 7077888 | tf_op jit(solution)/shard_map/dot_general | solution.py:23
  17.6 156.5 %all-reduce.2 = (bf16[768,768]{1,0:T(8,128)(2,1)}, bf16[768,768]{1,0:T(8,128)(2,1)S(1)}) all-reduce(f32[768,768]{1,0:T(8,128)} %fusion.8, f32[768,768]{1,0:T(8,128)} %fusion.13), channel_id=1, replica_groups=mesh['site'=8,'blk'=32] {'blk'}, use_global_device_ids=true, to_apply=%region_0.0 | all-reduce | flops 1179648 | bytes 7077888 | tf_op jit(solution)/shard_map/psum | solution.py:52
  174.1 1.9 fusion.48
  176.0 2.6 collective-permute-start.2
  178.6 1.3 fusion.44
  179.9 0.0 collective-permute-start.4
  180.0 0.1 collective-permute-done.2
  180.0 0.4 fusion.46
  180.5 4.0 %collective-permute-start.3 = (f32[24,768]{1,0:T(8,128)S(1)}, f32[24,768]{1,0:T(8,128)S(1)}, u32[]{:S(2)}, u32[]{:S(2)}) collective-permute-start(f32[24,768]{1,0:T(8,128)S(1)} %fusion.46), channel_id=1, source_target_pairs={{32,0},{64,32},{96,64},{128,96},{160,128},{192,160},{224,192},{0,2... | collective-permute-start | bytes 221192 | tf_op jit(solution)/shard_map/ppermute | solution.py:12
  184.4 0.8 collective-permute-done.4
  185.3 0.4 fusion.42
  185.7 0.0 collective-permute-start.5
  185.7 0.1 collective-permute-start
  185.8 3.6 %collective-permute-start.1 = (bf16[24,768]{1,0:T(8,128)(2,1)S(1)}, bf16[24,768]{1,0:T(8,128)(2,1)S(1)}, u32[]{:S(2)}, u32[]{:S(2)}) collective-permute-start(bf16[24,768]{1,0:T(8,128)(2,1)S(1)} %bitcast.88), channel_id=1, source_target_pairs={{32,0},{64,32},{96,64},{128,96},{160,128},{192,160},{224,192},{0,2... | collective-permute-start | bytes 110600 | tf_op jit(solution)/shard_map/ppermute | solution.py:12
  189.4 1.7 collective-permute-done.5
  191.1 0.1 fusion.38
  191.1 0.4 collective-permute-done
  191.5 0.6 copy-done.6
  192.1 0.0 copy-done.5
  192.1 0.7 pad_maximum_fusion
  192.8 0.0 all-gather.2.cloned.1.call-update
  192.8 2.2 fusion.26
  195.0 1.7 fusion.27
  196.7 88.5 %all-gather.2.cloned.1.call-done = bf16[768,3072]{1,0:T(8,128)(2,1)} async-done(((bf16[24,3072]{1,0:T(8,128)(2,1)}), bf16[768,3072]{1,0:T(8,128)(2,1)}) %all-gather.2.cloned.1.call-update) | async-done | bytes 4718608 | tf_op jit(solution)/shard_map/all_gather | solution.py:18
  285.1 6.0 %fusion = bf16[1536,768]{0,1:T(8,128)(2,1)} fusion(bf16[1536,768]{1,0:T(8,128)(2,1)S(1)} %bitcast.83, bf16[768,3072]{1,0:T(8,128)(2,1)} %all-gather.2.cloned.1.call-done), kind=kOutput, calls=%fused_computation.2 | convolution fusion | flops 2719678464 | bytes 7077888 | tf_op jit(solution)/shard_map/dot_general | solution.py:77
  291.1 4.3 %copy.13 = bf16[1536,768]{1,0:T(8,128)(2,1)} copy(bf16[1536,768]{0,1:T(8,128)(2,1)} %fusion) | data formatting | bytes 4718592 | tf_op jit(solution)/shard_map/convert_element_type | solution.py:79
  295.4 6.0 %fusion.1 = bf16[1536,768]{0,1:T(8,128)(2,1)} fusion(bf16[1536,768]{1,0:T(8,128)(2,1)S(1)} %bitcast.84, bf16[768,3072]{1,0:T(8,128)(2,1)} %all-gather.2.cloned.1.call-done), kind=kOutput, calls=%fused_computation.3 | convolution fusion | flops 2719678464 | bytes 7077888 | tf_op jit(solution)/shard_map/dot_general | solution.py:78
  301.4 4.3 %copy.14 = bf16[1536,768]{1,0:T(8,128)(2,1)} copy(bf16[1536,768]{0,1:T(8,128)(2,1)} %fusion.1) | data formatting | bytes 4718592 | tf_op jit(solution)/shard_map/convert_element_type | solution.py:80
  (16 shorter events, 0.0 us)
Async XLA Ops:
  7.2 1.7 copy-start
  7.2 278.0 %all-gather.2.cloned.1.call-start = ((), (), s32[]{:S(2)}) async-start(), calls=%async_computation | async-start | bytes 4866048 | tf_op jit(solution)/shard_map/all_gather | solution.py:18
  8.9 5.3 %copy-start.2 = (bf16[1,24,64,768]{3,2,1,0:T(8,128)(2,1)S(1)}, bf16[1,24,64,768]{3,2,1,0:T(8,128)(2,1)}, u32[]{:S(2)}) copy-start(bf16[1,24,64,768]{3,2,1,0:T(8,128)(2,1)} %param.10) | copy-start | bytes 7077892
  174.1 5.9 %copy-start.1 = (bf16[768,768]{1,0:T(8,128)(2,1)S(1)}, bf16[768,768]{1,0:T(8,128)(2,1)}, u32[]{:S(2)}) copy-start(bf16[768,768]{1,0:T(8,128)(2,1)} %get-tuple-element.8) | copy-start | bytes 3538948
  174.1 5.9 %copy-start.3 = (f32[1,24,768]{2,1,0:T(8,128)S(1)}, f32[1,24,768]{2,1,0:T(8,128)}, u32[]{:S(2)}) copy-start(f32[1,24,768]{2,1,0:T(8,128)} %param.12) | copy-start | bytes 221188
  174.1 11.2 %copy-start.4 = (f32[1,24,768]{2,1,0:T(8,128)S(1)}, f32[1,24,768]{2,1,0:T(8,128)}, u32[]{:S(2)}) copy-start(f32[1,24,768]{2,1,0:T(8,128)} %param.13) | copy-start | bytes 221188
  176.0 9.8 %copy-start.7 = (bf16[1,24,768]{2,1,0:T(8,128)(2,1)S(1)}, bf16[1,24,768]{2,1,0:T(8,128)(2,1)}, u32[]{:S(2)}) copy-start(bf16[1,24,768]{2,1,0:T(8,128)(2,1)} %param.7) | copy-start | bytes 110596
  176.0 4.0 %collective-permute-start.2 = (f32[24,768]{1,0:T(8,128)S(1)}, f32[24,768]{1,0:T(8,128)S(1)}, u32[]{:S(2)}, u32[]{:S(2)}) collective-permute-start(f32[24,768]{1,0:T(8,128)S(1)} %fusion.48), channel_id=1, source_target_pairs={{32,0},{64,32},{96,64},{128,96},{160,128},{192,160},{224,192},{0,2... | collective-permute-start | bytes 221192 | tf_op jit(solution)/shard_map/ppermute | solution.py:12
  179.9 5.3 %collective-permute-start.4 = (f32[24,768]{1,0:T(8,128)S(1)}, f32[24,768]{1,0:T(8,128)S(1)}, u32[]{:S(2)}, u32[]{:S(2)}) collective-permute-start(f32[24,768]{1,0:T(8,128)S(1)} %fusion.44), channel_id=1, source_target_pairs={{224,0},{0,32},{32,64},{64,96},{96,128},{128,160},{160,192},{192,2... | collective-permute-start | bytes 221192 | tf_op jit(solution)/shard_map/ppermute | solution.py:12
  180.5 8.9 %collective-permute-start.3 = (f32[24,768]{1,0:T(8,128)S(1)}, f32[24,768]{1,0:T(8,128)S(1)}, u32[]{:S(2)}, u32[]{:S(2)}) collective-permute-start(f32[24,768]{1,0:T(8,128)S(1)} %fusion.46), channel_id=1, source_target_pairs={{32,0},{64,32},{96,64},{128,96},{160,128},{192,160},{224,192},{0,2... | collective-permute-start | bytes 221192 | tf_op jit(solution)/shard_map/ppermute | solution.py:12
  185.7 5.3 %collective-permute-start.5 = (f32[24,768]{1,0:T(8,128)S(1)}, f32[24,768]{1,0:T(8,128)S(1)}, u32[]{:S(2)}, u32[]{:S(2)}) collective-permute-start(f32[24,768]{1,0:T(8,128)S(1)} %fusion.42), channel_id=1, source_target_pairs={{224,0},{0,32},{32,64},{64,96},{96,128},{128,160},{160,192},{192,2... | collective-permute-start | bytes 221192 | tf_op jit(solution)/shard_map/ppermute | solution.py:12
  185.7 5.8 %collective-permute-start = (bf16[24,768]{1,0:T(8,128)(2,1)S(1)}, bf16[24,768]{1,0:T(8,128)(2,1)S(1)}, u32[]{:S(2)}, u32[]{:S(2)}) collective-permute-start(bf16[24,768]{1,0:T(8,128)(2,1)S(1)} %bitcast.87), channel_id=1, source_target_pairs={{224,0},{0,32},{32,64},{64,96},{96,128},{128,160},{160,192},{192,2... | collective-permute-start | bytes 110600 | tf_op jit(solution)/shard_map/ppermute | solution.py:12
  185.8 5.7 %collective-permute-start.1 = (bf16[24,768]{1,0:T(8,128)(2,1)S(1)}, bf16[24,768]{1,0:T(8,128)(2,1)S(1)}, u32[]{:S(2)}, u32[]{:S(2)}) collective-permute-start(bf16[24,768]{1,0:T(8,128)(2,1)S(1)} %bitcast.88), channel_id=1, source_target_pairs={{32,0},{64,32},{96,64},{128,96},{160,128},{192,160},{224,192},{0,2... | collective-permute-start | bytes 110600 | tf_op jit(solution)/shard_map/ppermute | solution.py:12
  191.5 0.6 copy-start.6
  191.5 0.6 copy-start.5
Sparse Core Ops, SparseCore 0:
  192.9 92.1 all-gather.1
where the time goes:
time: 313 us
  blocking collectives  156 us (50%)
  waiting for transfers between devices  91.4 us (29%)
  matrix products  28.7 us (9%)
  between operations  14.1 us (5%)
  starting transfers between devices  10.3 us (3%)
  local copies, waits for them, and re-layouts  9.96 us (3%)
    psum x1, blocking collectives, body(): lax.psum((partial_term(left_flat), partial_term(right_flat)), 'blk')  156 us
    all_gather x1, waiting for transfers between devices, in_one_piece(): whole = lax.all_gather(both, axis, axis=dim, tiled=True)  88.5 us
    ppermute x6, starting transfers between devices, shifted(): return lax.ppermute(block, axis, route)  10.3 us
    dot_general x2, matrix products, contract_first(): lax.dot_general(left, right, (((0,), (0,)), ((), ())), preferred_element_...  8.75 us
  transfers between devices with their start and end apart: 7, of which 5 were waited for; matrix products, arithmetic and copies ran while one was open for 2% of the time, Pallas kernels for 0%

commit v1 on v0

v1 whole, which is shorter than its diff:
```python
import jax
import jax.numpy as jnp
from jax import lax
from jax.sharding import PartitionSpec as P

ITERS = 2
SECTORS = 16
FOLD = 128
WIDE = 384
F32 = jnp.float32
BF16 = jnp.bfloat16


def contract_first(left, right):
    return lax.dot_general(left, right, (((0,), (0,)), ((), ())), preferred_element_type=F32)


def contract_last(left, right):
    return lax.dot_general(left, right, (((1,), (1,)), ((), ())), preferred_element_type=F32)


def fold_lanes(x, width):
    pieces = [x[:, at : at + width] for at in range(0, x.shape[1], width)]
    total = pieces[0]
    for piece in pieces[1:]:
        total = total + piece
    return total


def body(corner, edge, proj_left, proj_right, charge, cot_left, cot_right):
    sites = lax.axis_size("site")
    members = lax.axis_size("blk")
    rows, chi = corner.shape[1], corner.shape[2]
    depth = edge.shape[2]
    chips = members // 2
    pair_rows = 2 * rows
    blk = lax.axis_index("blk")
    first = blk % 2 == 0
    chip = blk // 2
    groups = [[2 * q + core for q in range(chips)] for core in range(2)]

    def swap_cores(x):
        return lax.ppermute(x, "blk", [(i, i ^ 1) for i in range(members)])

    def site_move(x, distance, cross):
        route = []
        for s in range(sites):
            for i in range(members):
                target = i ^ 1 if cross else i
                sign = 1 if target % 2 == 0 else -1
                route.append((s * members + i, ((s + sign * distance) % sites) * members + target))
        return lax.ppermute(x, ("site", "blk"), route)

    def exchange(x):
        return lax.all_to_all(x, "blk", 0, 0, tiled=True, axis_index_groups=groups)

    def spread(x):
        return jnp.broadcast_to(x[None], (chips,) + x.shape)

    def pick(a, b):
        return jnp.where(first, a, b)

    def weave(own, other):
        halves = jnp.stack([pick(own, other), pick(other, own)], axis=1)
        return halves.reshape(chi, own.shape[-1])

    label = charge[0]
    label_to = site_move(charge, 1, False)[0]
    row_label = lax.dynamic_slice_in_dim(label, blk * rows, rows, 0)
    row_mask = row_label[:, None] == label[None, :]
    here = corner[0]
    start_left = fold_lanes(jnp.where(row_mask, cot_left[0], 0.0), FOLD).astype(BF16)
    start_right = fold_lanes(jnp.where(row_mask, cot_right[0], 0.0), FOLD).astype(BF16)
    early = exchange(spread(jnp.concatenate([here, start_left, start_right], axis=1)))

    edge_flat = edge[0].reshape(rows * depth, chi)
    part_left = contract_first(edge_flat, proj_left[0].reshape(rows * depth, chi))
    part_right = contract_first(edge_flat, proj_right[0].reshape(rows * depth, chi))
    other_part = swap_cores(pick(part_right, part_left).astype(BF16))
    part = pick(part_left, part_right) + other_part.astype(F32)
    part_bf = part.astype(BF16)

    sector = jnp.arange(SECTORS, dtype=jnp.int32)
    in_sector = label_to[None, :] == sector[:, None]
    least = jnp.min(jnp.where(in_sector, label[None, :], SECTORS), axis=1)
    most = jnp.max(jnp.where(in_sector, label[None, :], -1), axis=1)
    low = jnp.sum(jnp.where(label_to[:, None] == sector[None, :], least[None, :], 0), axis=1)
    high = jnp.sum(jnp.where(label_to[:, None] == sector[None, :], most[None, :], 0), axis=1)
    reach = (label[None, :] >= low[:, None]) & (label[None, :] <= high[:, None])
    narrow = fold_lanes(jnp.where(reach, part, 0.0), WIDE).astype(BF16)
    got = exchange(narrow.reshape(chips, pair_rows, WIDE))
    enl = jnp.sum(got.astype(F32), axis=0).astype(BF16)

    half = early[:, :, :chi]
    near = weave(site_move(half, 1, False), site_move(half, 1, True))
    early_left = early[:, :, chi : chi + FOLD]
    early_right = early[:, :, chi + FOLD :]
    w0 = weave(pick(early_left, early_right), swap_cores(pick(early_right, early_left)))

    same = label[:, None] == label[None, :]
    mine = lax.dynamic_slice_in_dim(label, chip * pair_rows, pair_rows, 0)
    mine_to = lax.dynamic_slice_in_dim(label_to, chip * pair_rows, pair_rows, 0)
    at_lane = (chip * pair_rows + jnp.arange(pair_rows, dtype=jnp.int32)) % FOLD
    select = (at_lane[:, None] == jnp.arange(FOLD, dtype=jnp.int32)[None, :]).astype(BF16)
    turned = contract_last(select, w0)
    cot_turned = fold_lanes(jnp.where(mine[:, None] == label[None, :], turned, 0.0), FOLD).astype(BF16)
    cot_to = site_move(cot_turned, 1, False).astype(F32)
    mask_to = mine_to[:, None] == label_to[None, :]

    def next_w(back):
        adj = cot_to + fold_lanes(jnp.where(mask_to, back, 0.0), FOLD)
        return site_move(adj.astype(BF16), -1, False)

    wide_mask = same[:, :WIDE] | same[:, WIDE:]
    w0_wide = jnp.where(wide_mask, jnp.concatenate([w0] * (WIDE // FOLD), axis=1), 0.0)
    w1 = next_w(contract_last(enl, w0_wide))
    w1_all = exchange(spread(w1)).reshape(chi, FOLD)
    w1_open = jnp.where(same, jnp.concatenate([w1_all] * (chi // FOLD), axis=1), 0.0)
    w1_fold = w1_open[:WIDE] + w1_open[WIDE:]
    w2 = next_w(jnp.dot(enl, w1_fold, preferred_element_type=F32))

    new_part = jnp.dot(near, part_bf, preferred_element_type=F32)
    new_part = fold_lanes(jnp.where(same, new_part, 0.0), FOLD).astype(BF16)
    last = exchange(
        jnp.concatenate([spread(w2), new_part.reshape(chips, pair_rows, FOLD)], axis=2)
    )
    w2_all = last[:, :, :FOLD].reshape(chi, FOLD)
    new_sum = jnp.sum(last[:, :, FOLD:].astype(F32), axis=0)
    new_own = pick(new_sum[:rows], new_sum[rows:])
    new_other = swap_cores(pick(new_sum[rows:], new_sum[:rows]))

    def open_new(x):
        return jnp.where(row_mask, jnp.concatenate([x] * (chi // FOLD), axis=1), 0.0).astype(BF16)

    new_left = open_new(pick(new_own, new_other))
    new_right = open_new(pick(new_other, new_own))

    w2_open = jnp.where(same, jnp.concatenate([w2_all] * (chi // FOLD), axis=1), 0.0)
    mid = jnp.dot(w2_open, near, preferred_element_type=F32).astype(BF16)
    mid_other = swap_cores(mid)
    grad_left = contract_last(edge_flat, pick(mid, mid_other)).astype(BF16)
    grad_right = contract_last(edge_flat, pick(mid_other, mid)).astype(BF16)
    return (
        new_left[None],
        new_right[None],
        grad_left.reshape(1, rows, depth, chi),
        grad_right.reshape(1, rows, depth, chi),
    )


def solution(mesh):
    row = P("site", "blk", None)
    flat = P("site", "blk", None, None)
    return jax.shard_map(
        body,
        mesh=mesh,
        in_specs=(row, flat, flat, flat, P("site", None), row, row),
        out_specs=(row, row, flat, flat),
        check_vma=False,
    )
```

time: 313 us -> 167 us (0.53)
  blocking collectives: 156 us -> 16.3 us
  waiting for transfers between devices: 91.4 us -> 50.9 us
  starting transfers between devices: 10.3 us -> 41.5 us
  between operations: 14.1 us -> 1.13 us
  other arithmetic: 1.6 us -> 14.2 us
  local copies, waits for them, and re-layouts: 9.96 us -> 17.1 us
  matrix products: 28.7 us -> 25 us
    psum x1 -> x0, blocking collectives: 156 us -> none  [body(): lax.psum((partial_term(left_flat), partial_term(right_flat)), 'blk')]
    all_gather x1 -> x0, waiting for transfers between devices: 88.5 us -> none  [in_one_piece(): whole = lax.all_gather(both, axis, axis=dim, tiled=True)]
    ppermute x6 -> x10, waiting for transfers between devices: 2.9 us -> 35.6 us  [the longest x6 34 us: site_move(): return lax.ppermute(x, ('site', 'blk'), route)]
    all_to_all x0 -> x3, starting transfers between devices: none -> 24.3 us  [exchange(): return lax.all_to_all(x, 'blk', 0, 0, tiled=True, axis_index_groups=groups)]
    all_to_all x0 -> x1, blocking collectives: none -> 16.3 us  [exchange(): return lax.all_to_all(x, 'blk', 0, 0, tiled=True, axis_index_groups=groups)]
    all_to_all x0 -> x3, waiting for transfers between devices: none -> 15.2 us  [exchange(): return lax.all_to_all(x, 'blk', 0, 0, tiled=True, axis_index_groups=groups)]
    dot_general x4 -> x3, matrix products: 15.8 us -> 7.02 us  [the longest x1 5.65 us: body(): new_part = jnp.dot(near, part_bf, preferred_element_type=F32)]
    ppermute x6 -> x10, starting transfers between devices: 10.3 us -> 17.2 us  [the longest x4 10.1 us: swap_cores(): return lax.ppermute(x, 'blk', [(i, i ^ 1) for i in range(members)])]
  transfers between devices with their start and end apart: 7 -> 13, of which waited for: 5 -> 7; matrix products, arithmetic and copies ran while one was open for 2% -> 16% of each run, Pallas kernels for 0% -> 0%
where the time goes in v1:
time: 167 us; the launch traced here: 166 us
  waiting for transfers between devices  50.9 us (30%)
  starting transfers between devices  41.5 us (25%)
  matrix products  25 us (15%)
  local copies, waits for them, and re-layouts  17.1 us (10%)
  blocking collectives  16.3 us (10%)
  other arithmetic  14.2 us (9%)
    ppermute x6, waiting for transfers between devices, site_move(): return lax.ppermute(x, ('site', 'blk'), route)  34 us
    all_to_all x3, starting transfers between devices, exchange(): return lax.all_to_all(x, 'blk', 0, 0, tiled=True, axis_index_groups=groups)  24.3 us
    all_to_all x1, blocking collectives, exchange(): return lax.all_to_all(x, 'blk', 0, 0, tiled=True, axis_index_groups=groups)  16.3 us
    all_to_all x3, waiting for transfers between devices, exchange(): return lax.all_to_all(x, 'blk', 0, 0, tiled=True, axis_index_groups=groups)  15.2 us
    dot_general x4, matrix products, contract_last(): lax.dot_general(left, right, (((1,), (1,)), ((), ())), preferred_element_...  10.1 us
    ppermute x4, starting transfers between devices, swap_cores(): return lax.ppermute(x, 'blk', [(i, i ^ 1) for i in range(members)])  10.1 us
    dot_general x2, matrix products, contract_first(): lax.dot_general(left, right, (((0,), (0,)), ((), ())), preferred_element_...  7.89 us
    ppermute x6, starting transfers between devices, site_move(): return lax.ppermute(x, ('site', 'blk'), route)  7.07 us
  transfers between devices with their start and end apart: 13, of which 7 were waited for; matrix products, arithmetic and copies ran while one was open for 16% of the time, Pallas kernels for 0%

profile of v1, /device:TPU:1, one launch (start us, length us, event | category | flops | bytes accessed | tf_op | source)
XLA Modules:
  0.0 166.0 jit_solution(13842026974874316880)
XLA Ops:
  0.7 1.6 copy-done
  2.3 3.9 %fusion.6 = f32[768,768,1]{1,0,2:T(8,128)S(1)} fusion(bf16[1,24,64,768]{3,2,1,0:T(8,128)(2,1)} %param.9, bf16[1,24,64,768]{3,2,1,0:T(8,128)(2,1)S(1)} %copy-done), kind=kOutput, calls=%fused_computation.10 | convolution fusion | flops 1811939328 | bytes 7077888 | tf_op jit(solution)/shard_map/dot_general | solution.py:15
  6.2 4.0 %fusion.3 = (bf16[768,768]{1,0:T(8,128)(2,1)}, f32[768,768,1]{1,0,2:T(8,128)}) fusion(f32[768,768,1]{1,0,2:T(8,128)S(1)} %fusion.6, pred[]{:T(512)S(6)} %eq.132, bf16[1,24,64,768]{3,2,1,0:T(8,128)(2,1)S(1)} %copy-done.14, bf16[1,24,64,768]{3,2,1,0:T(8,128)(2,1)S(1)} %copy-done), kind=kOutput, calls=%fused_computation.7 | convolution fusion | flops 1812529152 | bytes 10616833 | tf_op jit(solution)/shard_map/dot_general | solution.py:15
  10.2 3.2 %collective-permute-start.3 = (bf16[768,768]{1,0:T(8,128)(2,1)}, bf16[768,768]{1,0:T(8,128)(2,1)S(1)}, u32[]{:S(2)}, u32[]{:S(2)}) collective-permute-start(bf16[768,768]{1,0:T(8,128)(2,1)} %get-tuple-element.26), channel_id=1, source_target_pairs={{0,1},{1,0},{2,3},{3,2},{4,5},{5,4},{6,7},{7,6},{8,9},{9,8},{10,11... | collective-permute-start | bytes 3538952 | tf_op jit(solution)/shard_map/ppermute | solution.py:43
  13.5 1.0 compare_select_fusion.5
  16.3 9.3 %all-to-all-start = ((bf16[16,24,1024]{2,1,0:T(8,128)(2,1)}), bf16[16,24,1024]{2,1,0:T(8,128)(2,1)}, u32[]{:S(2)}, u32[]{:S(2)}) async-start(bf16[16,24,1024]{2,1,0:T(8,128)(2,1)} %broadcast_in_dim.98), calls=%async_computation | async-start | bytes 1572864 | tf_op jit(solution)/shard_map/all_to_all | solution.py:55
  25.6 2.7 %collective-permute-start.2 = (s32[1,768]{1,0:T(1,128)S(1)}, s32[1,768]{1,0:T(1,128)S(1)}, u32[]{:S(2)}, u32[]{:S(2)}) collective-permute-start(s32[1,768]{1,0:T(1,128)S(1)} %copy-done.10), channel_id=1, source_target_pairs={{0,32},{1,225},{2,34},{3,227},{4,36},{5,229},{6,38},{7,231},{8,40}... | collective-permute-start | bytes 9224 | tf_op jit(solution)/shard_map/ppermute | solution.py:52
  28.3 1.2 broadcast_compare_fusion
  30.4 3.4 %and_select_fusion = f32[768,768]{1,0:T(8,128)S(1)} fusion(s32[768]{0:T(1024)S(1)} %reduce.1, s32[768]{0:T(1024)S(1)} %get-tuple-element.11, s32[768]{0:T(1024)S(1)} %get-tuple-element.10, bf16[768,768]{1,0:T(8,128)(2,1)S(1)} %collective-permute-done.3, f32[768,768,1]{1,0,2:T(8,128)} %get-tuple-element.27, f32[768,768,1]{1,0,2:T(8,128)} %copy-done.1, ...), kind=kLoop, calls=%fused_computation.14 | loop fusion | flops 4128768 | bytes 8266753 | tf_op jit(solution)/shard_map/jit(_where)/select_n | solution.py:90
  34.7 11.9 %all-to-all-done = bf16[16,24,1024]{2,1,0:T(8,128)(2,1)} async-done(((bf16[16,24,1024]{2,1,0:T(8,128)(2,1)}), bf16[16,24,1024]{2,1,0:T(8,128)(2,1)}, u32[]{:S(2)}, u32[]{:S(2)}) %all-to-all-start) | async-done | bytes 786464 | tf_op jit(solution)/shard_map/all_to_all | solution.py:55
  46.6 6.6 %all-to-all-start.1 = ((bf16[16,48,384]{2,1,0:T(8,128)(2,1)}), bf16[16,48,384]{2,1,0:T(8,128)(2,1)S(1)}, u32[]{:S(2)}, u32[]{:S(2)}) async-start(bf16[16,48,384]{2,1,0:T(8,128)(2,1)} %bitcast.108), calls=%async_computation.1 | async-start | bytes 1179648 | tf_op jit(solution)/shard_map/all_to_all | solution.py:55
  55.7 1.1 slice.236
  56.8 2.7 %collective-permute-start.6 = (bf16[16,24,768]{2,1,0:T(8,128)(2,1)S(1)}, bf16[16,24,768]{2,1,0:T(8,128)(2,1)S(1)}, u32[]{:S(2)}, u32[]{:S(2)}) collective-permute-start(bf16[16,24,768]{2,1,0:T(8,128)(2,1)S(1)} %slice.236), channel_id=1, source_target_pairs={{0,32},{1,225},{2,34},{3,227},{4,36},{5,229},{6,38},{7,231},{8,40}... | collective-permute-start | bytes 1769480 | tf_op jit(solution)/shard_map/ppermute | solution.py:52
  61.4 1.6 collective-permute-start.1
  62.9 25.6 %collective-permute-done.6 = bf16[16,24,768]{2,1,0:T(8,128)(2,1)S(1)} collective-permute-done((bf16[16,24,768]{2,1,0:T(8,128)(2,1)S(1)}, bf16[16,24,768]{2,1,0:T(8,128)(2,1)S(1)}, u32[]{:S(2)}, u32[]{:S(2)}) %collective-permute-start.6) | collective-permute-done | bytes 589856 | tf_op jit(solution)/shard_map/ppermute | solution.py:52
  88.6 1.0 collective-permute-done.7
  91.2 1.7 %convolution_select_fusion.1 = f32[48,768]{1,0:T(8,128)S(1)} fusion(bf16[48,384]{1,0:T(8,128)(2,1)} %reduce_sum.41, pred[768,768]{1,0:T(32,128)(4,1)} %broadcast_compare_fusion, bf16[768,128]{1,0:T(8,128)(2,1)} %bitcast.111, s32[768]{0:T(1024)} %copy-done.8, s32[48]{0:T(128)} %fusion.39), kind=kOutput, calls=%fused_computation.33 | convolution fusion | flops 30744576 | bytes 974016 | tf_op jit(solution)/shard_map/dot_general | solution.py:19
  93.0 1.1 pad_maximum_fusion
  94.2 3.5 %collective-permute-done.4 = bf16[48,128]{1,0:T(8,128)(2,1)S(1)} collective-permute-done((bf16[48,128]{1,0:T(8,128)(2,1)S(1)}, bf16[48,128]{1,0:T(8,128)(2,1)S(1)}, u32[]{:S(2)}, u32[]{:S(2)}) %collective-permute-start.4) | collective-permute-done | bytes 12320 | tf_op jit(solution)/shard_map/ppermute | solution.py:52
  98.4 8.5 %all-to-all-start.2 = ((bf16[16,48,128]{2,1,0:T(8,128)(2,1)}), bf16[16,48,128]{2,1,0:T(8,128)(2,1)S(1)}, u32[]{:S(2)}, u32[]{:S(2)}) async-start(bf16[16,48,128]{2,1,0:T(8,128)(2,1)} %broadcast_in_dim.108), calls=%async_computation.2 | async-start | bytes 393216 | tf_op jit(solution)/shard_map/all_to_all | solution.py:55
  106.8 5.7 %compare_select_fusion.1 = f32[768,768]{1,0:T(8,128)} fusion(bf16[768,768]{1,0:T(8,128)(2,1)} %bitcast.104, s32[768]{0:T(1024)S(1)} %reduce.1, f32[768,768,1]{1,0,2:T(8,128)} %get-tuple-element.27, f32[768,768,1]{1,0,2:T(8,128)} %copy-done.1, bf16[768,768]{1,0:T(8,128)(2,1)} %copy-done.4, pred[]{:T(512)S(6)} %eq.132), kind=kOutput, calls=%fused_computation.16 | convolution fusion | flops 909508608 | bytes 9440257 | tf_op jit(solution)/shard_map/dot_general | solution.py:122
  112.5 3.3 %all-to-all-done.2 = bf16[16,48,128]{2,1,0:T(8,128)(2,1)S(1)} async-done(((bf16[16,48,128]{2,1,0:T(8,128)(2,1)}), bf16[16,48,128]{2,1,0:T(8,128)(2,1)S(1)}, u32[]{:S(2)}, u32[]{:S(2)}) %all-to-all-start.2) | async-done | bytes 196640 | tf_op jit(solution)/shard_map/all_to_all | solution.py:55
  118.0 3.9 %collective-permute-done.5 = bf16[48,128]{1,0:T(8,128)(2,1)S(1)} collective-permute-done((bf16[48,128]{1,0:T(8,128)(2,1)S(1)}, bf16[48,128]{1,0:T(8,128)(2,1)S(1)}, u32[]{:S(2)}, u32[]{:S(2)}) %collective-permute-start.5) | collective-permute-done | bytes 12320 | tf_op jit(solution)/shard_map/ppermute | solution.py:52
  121.9 16.3 %all_to_all.20 = bf16[16,48,256]{2,1,0:T(8,128)(2,1)S(1)} all-to-all(bf16[16,48,256]{2,1,0:T(8,128)(2,1)S(1)} %pad_maximum_fusion.1), channel_id=1, replica_groups={{0,2,4,6,8,10,12,14,16,18,20,22,24,26,28,30},{1,3,5,7,9,11,13,15,17,19,..., dimensions={0} | all-to-all | bytes 786432 | tf_op jit(solution)/shard_map/all_to_all | solution.py:55
  138.6 5.1 %collective-permute-start.8 = (bf16[24,128]{1,0:T(8,128)(2,1)S(1)}, bf16[24,128]{1,0:T(8,128)(2,1)S(1)}, u32[]{:S(2)}, u32[]{:S(2)}) collective-permute-start(bf16[24,128]{1,0:T(8,128)(2,1)S(1)} %slice_select_fusion), channel_id=1, source_target_pairs={{0,1},{1,0},{2,3},{3,2},{4,5},{5,4},{6,7},{7,6},{8,9},{9,8},{10,11... | collective-permute-start | bytes 18440 | tf_op jit(solution)/shard_map/ppermute | solution.py:43
  143.7 1.2 convolution_convert_fusion.2
  146.7 1.6 collective-permute-done.9
  148.3 1.1 copy-done.15
  149.3 3.4 %fusion.1 = bf16[1536,768]{0,1:T(8,128)(2,1)} fusion(bf16[1536,768]{1,0:T(8,128)(2,1)S(1)} %bitcast.91, bf16[768,768]{1,0:T(8,128)(2,1)S(1)} %collective-permute-done.9, bf16[768,768]{1,0:T(8,128)(2,1)S(1)} %convolution_convert_fusion.2, pred[]{:T(512)S(6)} %eq.132), kind=kOutput, calls=%fused_computation.3 | convolution fusion | flops 1813708800 | bytes 7077889 | tf_op jit(solution)/shard_map/dot_general | solution.py:19
  152.8 4.3 %copy.21 = bf16[1536,768]{1,0:T(8,128)(2,1)} copy(bf16[1536,768]{0,1:T(8,128)(2,1)} %fusion.1) | data formatting | bytes 4718592 | tf_op jit(solution)/shard_map/convert_element_type | solution.py:142
  157.0 4.7 %fusion = bf16[1536,768]{0,1:T(8,128)(2,1)} fusion(bf16[1536,768]{1,0:T(8,128)(2,1)S(1)} %bitcast.90, bf16[768,768]{1,0:T(8,128)(2,1)S(1)} %convolution_convert_fusion.2, bf16[768,768]{1,0:T(8,128)(2,1)} %copy-done.15, pred[]{:T(512)S(6)} %eq.132), kind=kOutput, calls=%fused_computation.2 | convolution fusion | flops 1813708800 | bytes 7077889 | tf_op jit(solution)/shard_map/dot_general | solution.py:19
  161.8 4.3 %copy.20 = bf16[1536,768]{1,0:T(8,128)(2,1)} copy(bf16[1536,768]{0,1:T(8,128)(2,1)} %fusion) | data formatting | bytes 4718592 | tf_op jit(solution)/shard_map/convert_element_type | solution.py:141
  (98 shorter events, 14.6 us)
Async XLA Ops:
  0.6 1.7 %copy-start = (bf16[1,24,64,768]{3,2,1,0:T(8,128)(2,1)S(1)}, bf16[1,24,64,768]{3,2,1,0:T(8,128)(2,1)}, u32[]{:S(2)}) copy-start(bf16[1,24,64,768]{3,2,1,0:T(8,128)(2,1)} %param.8) | copy-start | bytes 7077892
  2.3 3.9 %copy-start.14 = (bf16[1,24,64,768]{3,2,1,0:T(8,128)(2,1)S(1)}, bf16[1,24,64,768]{3,2,1,0:T(8,128)(2,1)}, u32[]{:S(2)}) copy-start(bf16[1,24,64,768]{3,2,1,0:T(8,128)(2,1)} %param.10) | copy-start | bytes 7077892
  6.2 4.0 %copy-start.1 = (f32[768,768,1]{1,0,2:T(8,128)}, f32[768,768,1]{1,0,2:T(8,128)S(1)}, u32[]{:S(2)}) copy-start(f32[768,768,1]{1,0,2:T(8,128)S(1)} %fusion.6) | copy-start | bytes 7077892
  6.2 7.2 %copy-start.10 = (s32[1,768]{1,0:T(1,128)S(1)}, s32[1,768]{1,0:T(1,128)}, u32[]{:S(2)}) copy-start(s32[1,768]{1,0:T(1,128)} %param.11) | copy-start | bytes 9220
  10.2 20.1 %collective-permute-start.3 = (bf16[768,768]{1,0:T(8,128)(2,1)}, bf16[768,768]{1,0:T(8,128)(2,1)S(1)}, u32[]{:S(2)}, u32[]{:S(2)}) collective-permute-start(bf16[768,768]{1,0:T(8,128)(2,1)} %get-tuple-element.26), channel_id=1, source_target_pairs={{0,1},{1,0},{2,3},{3,2},{4,5},{5,4},{6,7},{7,6},{8,9},{9,8},{10,11... | collective-permute-start | bytes 3538952 | tf_op jit(solution)/shard_map/ppermute | solution.py:43
  13.5 1.0 copy-start.11
  16.3 30.3 %all-to-all-start = ((bf16[16,24,1024]{2,1,0:T(8,128)(2,1)}), bf16[16,24,1024]{2,1,0:T(8,128)(2,1)}, u32[]{:S(2)}, u32[]{:S(2)}) async-start(bf16[16,24,1024]{2,1,0:T(8,128)(2,1)} %broadcast_in_dim.98), calls=%async_computation | async-start | bytes 1572864 | tf_op jit(solution)/shard_map/all_to_all | solution.py:55
  25.6 4.5 %collective-permute-start.2 = (s32[1,768]{1,0:T(1,128)S(1)}, s32[1,768]{1,0:T(1,128)S(1)}, u32[]{:S(2)}, u32[]{:S(2)}) collective-permute-start(s32[1,768]{1,0:T(1,128)S(1)} %copy-done.10), channel_id=1, source_target_pairs={{0,32},{1,225},{2,34},{3,227},{4,36},{5,229},{6,38},{7,231},{8,40}... | collective-permute-start | bytes 9224 | tf_op jit(solution)/shard_map/ppermute | solution.py:52
  30.1 3.6 %copy-start.8 = (s32[768]{0:T(1024)}, s32[768]{0:T(1024)S(1)}, u32[]{:S(2)}) copy-start(s32[768]{0:T(1024)S(1)} %reduce.2) | copy-start | bytes 9220
  30.3 3.4 %copy-start.4 = (bf16[768,768]{1,0:T(8,128)(2,1)}, bf16[768,768]{1,0:T(8,128)(2,1)S(1)}, u32[]{:S(2)}) copy-start(bf16[768,768]{1,0:T(8,128)(2,1)S(1)} %collective-permute-done.3) | copy-start | bytes 3538948
  46.6 43.9 %all-to-all-start.1 = ((bf16[16,48,384]{2,1,0:T(8,128)(2,1)}), bf16[16,48,384]{2,1,0:T(8,128)(2,1)S(1)}, u32[]{:S(2)}, u32[]{:S(2)}) async-start(bf16[16,48,384]{2,1,0:T(8,128)(2,1)} %bitcast.108), calls=%async_computation.1 | async-start | bytes 1179648 | tf_op jit(solution)/shard_map/all_to_all | solution.py:55
  54.1 5.3 %collective-permute-start = (bf16[16,24,128]{2,1,0:T(8,128)(2,1)S(1)}, bf16[16,24,128]{2,1,0:T(8,128)(2,1)S(1)}, u32[]{:S(2)}, u32[]{:S(2)}) collective-permute-start(bf16[16,24,128]{2,1,0:T(8,128)(2,1)S(1)} %broadcast_select_fusion), channel_id=1, source_target_pairs={{0,1},{1,0},{2,3},{3,2},{4,5},{5,4},{6,7},{7,6},{8,9},{9,8},{10,11... | collective-permute-start | bytes 294920 | tf_op jit(solution)/shard_map/ppermute | solution.py:43
  55.7 4.8 %copy-start.13 = (s32[48]{0:T(128)S(1)}, s32[48]{0:T(128)}, u32[]{:S(2)}) copy-start(s32[48]{0:T(128)} %fusion.38) | copy-start | bytes 580
  56.8 31.8 %collective-permute-start.6 = (bf16[16,24,768]{2,1,0:T(8,128)(2,1)S(1)}, bf16[16,24,768]{2,1,0:T(8,128)(2,1)S(1)}, u32[]{:S(2)}, u32[]{:S(2)}) collective-permute-start(bf16[16,24,768]{2,1,0:T(8,128)(2,1)S(1)} %slice.236), channel_id=1, source_target_pairs={{0,32},{1,225},{2,34},{3,227},{4,36},{5,229},{6,38},{7,231},{8,40}... | collective-permute-start | bytes 1769480 | tf_op jit(solution)/shard_map/ppermute | solution.py:52
  59.5 30.1 %collective-permute-start.7 = (bf16[16,24,768]{2,1,0:T(8,128)(2,1)S(1)}, bf16[16,24,768]{2,1,0:T(8,128)(2,1)S(1)}, u32[]{:S(2)}, u32[]{:S(2)}) collective-permute-start(bf16[16,24,768]{2,1,0:T(8,128)(2,1)S(1)} %slice.236), channel_id=1, source_target_pairs={{0,225},{1,32},{2,227},{3,34},{4,229},{5,36},{6,231},{7,38},{8,233... | collective-permute-start | bytes 1769480 | tf_op jit(solution)/shard_map/ppermute | solution.py:52
  60.5 28.1 %copy-start.6 = (bf16[16,2,24,128]{3,2,1,0:T(8,128)(2,1)}, bf16[16,2,24,128]{3,2,1,0:T(8,128)(2,1)S(1)}, u32[]{:S(2)}) copy-start(bf16[16,2,24,128]{3,2,1,0:T(8,128)(2,1)S(1)} %copy.18) | copy-start | bytes 589828
  61.4 31.5 %collective-permute-start.1 = (bf16[48,128]{1,0:T(8,128)(2,1)}, bf16[48,128]{1,0:T(8,128)(2,1)S(1)}, u32[]{:S(2)}, u32[]{:S(2)}) collective-permute-start(bf16[48,128]{1,0:T(8,128)(2,1)} %fusion.33), channel_id=1, source_target_pairs={{0,32},{1,225},{2,34},{3,227},{4,36},{5,229},{6,38},{7,231},{8,40}... | collective-permute-start | bytes 36872 | tf_op jit(solution)/shard_map/ppermute | solution.py:52
  91.2 1.9 %copy-start.5 = (bf16[16,1,24,768]{3,2,1,0:T(8,128)(2,1)S(1)}, bf16[16,1,24,768]{3,2,1,0:T(8,128)(2,1)}, u32[]{:S(2)}) copy-start(bf16[16,1,24,768]{3,2,1,0:T(8,128)(2,1)} %get-tuple-element.17) | copy-start | bytes 1769476
  92.9 4.7 %collective-permute-start.4 = (bf16[48,128]{1,0:T(8,128)(2,1)S(1)}, bf16[48,128]{1,0:T(8,128)(2,1)S(1)}, u32[]{:S(2)}, u32[]{:S(2)}) collective-permute-start(bf16[48,128]{1,0:T(8,128)(2,1)S(1)} %fusion.31), channel_id=1, source_target_pairs={{0,224},{1,33},{2,226},{3,35},{4,228},{5,37},{6,230},{7,39},{8,232... | collective-permute-start | bytes 36872 | tf_op jit(solution)/shard_map/ppermute | solution.py:52
  98.4 17.4 %all-to-all-start.2 = ((bf16[16,48,128]{2,1,0:T(8,128)(2,1)}), bf16[16,48,128]{2,1,0:T(8,128)(2,1)S(1)}, u32[]{:S(2)}, u32[]{:S(2)}) async-start(bf16[16,48,128]{2,1,0:T(8,128)(2,1)} %broadcast_in_dim.108), calls=%async_computation.2 | async-start | bytes 393216 | tf_op jit(solution)/shard_map/all_to_all | solution.py:55
  116.1 0.8 copy-start.7
  116.2 0.7 copy-start.9
  116.2 0.7 copy-start.16
  116.2 1.7 %copy-start.2 = (f32[768,768]{1,0:T(8,128)S(1)}, f32[768,768]{1,0:T(8,128)}, u32[]{:S(2)}) copy-start(f32[768,768]{1,0:T(8,128)} %compare_select_fusion.1) | copy-start | bytes 7077892
  117.1 4.7 %collective-permute-start.5 = (bf16[48,128]{1,0:T(8,128)(2,1)S(1)}, bf16[48,128]{1,0:T(8,128)(2,1)S(1)}, u32[]{:S(2)}, u32[]{:S(2)}) collective-permute-start(bf16[48,128]{1,0:T(8,128)(2,1)S(1)} %fusion.32), channel_id=1, source_target_pairs={{0,224},{1,33},{2,226},{3,35},{4,228},{5,37},{6,230},{7,39},{8,232... | collective-permute-start | bytes 36872 | tf_op jit(solution)/shard_map/ppermute | solution.py:52
  138.3 5.5 %copy-start.3 = (bf16[16,2,24,768]{3,2,1,0:T(8,128)(2,1)S(1)}, bf16[16,2,24,768]{3,2,1,0:T(8,128)(2,1)}, u32[]{:S(2)}) copy-start(bf16[16,2,24,768]{3,2,1,0:T(8,128)(2,1)} %pad_maximum_fusion) | copy-start | bytes 3538948
  138.6 7.3 %copy-start.12 = (s32[24]{0:T(128)S(1)}, s32[24]{0:T(128)}, u32[]{:S(2)}) copy-start(s32[24]{0:T(128)} %copy-done.11) | copy-start | bytes 292
  138.6 7.2 %collective-permute-start.8 = (bf16[24,128]{1,0:T(8,128)(2,1)S(1)}, bf16[24,128]{1,0:T(8,128)(2,1)S(1)}, u32[]{:S(2)}, u32[]{:S(2)}) collective-permute-start(bf16[24,128]{1,0:T(8,128)(2,1)S(1)} %slice_select_fusion), channel_id=1, source_target_pairs={{0,1},{1,0},{2,3},{3,2},{4,5},{5,4},{6,7},{7,6},{8,9},{9,8},{10,11... | collective-permute-start | bytes 18440 | tf_op jit(solution)/shard_map/ppermute | solution.py:43
  144.9 3.4 %collective-permute-start.9 = (bf16[768,768]{1,0:T(8,128)(2,1)S(1)}, bf16[768,768]{1,0:T(8,128)(2,1)S(1)}, u32[]{:S(2)}, u32[]{:S(2)}) collective-permute-start(bf16[768,768]{1,0:T(8,128)(2,1)S(1)} %convolution_convert_fusion.2), channel_id=1, source_target_pairs={{0,1},{1,0},{2,3},{3,2},{4,5},{5,4},{6,7},{7,6},{8,9},{9,8},{10,11... | collective-permute-start | bytes 3538952 | tf_op jit(solution)/shard_map/ppermute | solution.py:43
  148.3 1.1 copy-start.15

commit v2 on v1

v2 whole, which is shorter than its diff:
```python
import jax
import jax.numpy as jnp
from jax import lax
from jax.experimental import pallas as pl
from jax.experimental.pallas import tpu as pltpu
from jax.sharding import PartitionSpec as P

SECTORS = 16
FOLD = 128
WIDE = 384
F32 = jnp.float32
BF16 = jnp.bfloat16
VMEM = pl.BlockSpec(memory_space=pltpu.VMEM)
ANY = pl.BlockSpec(memory_space=pl.ANY)


def contract_first(left, right):
    return lax.dot_general(left, right, (((0,), (0,)), ((), ())), preferred_element_type=F32)


def contract_last(left, right):
    return lax.dot_general(left, right, (((1,), (1,)), ((), ())), preferred_element_type=F32)


def fold_lanes(x, width):
    pieces = [x[:, at : at + width] for at in range(0, x.shape[1], width)]
    total = pieces[0]
    for piece in pieces[1:]:
        total = total + piece
    return total


def near_tiles(i, tiles):
    return max(0, i - 1), min(tiles, i + 2)


def sum_kernel(got_ref, out_ref):
    total = got_ref[0, :, :WIDE].astype(F32)
    for q in range(1, got_ref.shape[0]):
        total = total + got_ref[q, :, :WIDE].astype(F32)
    out_ref[...] = jnp.broadcast_to(total.astype(BF16)[None], out_ref.shape)


def fold_back(enl_ref, operand, contract, to_row_ref, to_col_ref, out_ref):
    tiles = out_ref.shape[0] // FOLD
    for i in range(tiles):
        low, high = near_tiles(i, tiles)
        rows = slice(FOLD * i, FOLD * (i + 1))
        back = contract(enl_ref[rows, :], operand(FOLD * low, FOLD * high))
        total = jnp.zeros((FOLD, FOLD), F32)
        for q in range(low, high):
            same = to_col_ref[rows, :] == to_row_ref[:, FOLD * q : FOLD * (q + 1)]
            total = total + jnp.where(same, back[:, FOLD * (q - low) : FOLD * (q - low + 1)], 0.0)
        out_ref[rows, :] = total.astype(out_ref.dtype)


def first_kernel(w_ref, enl_ref, row_ref, col_ref, to_row_ref, to_col_ref, out_ref, open_ref):
    w = w_ref[...].astype(F32)
    for q in range(WIDE // FOLD):
        same = col_ref[...] == row_ref[:, FOLD * q : FOLD * (q + 1)]
        again = col_ref[...] == row_ref[:, WIDE + FOLD * q : WIDE + FOLD * (q + 1)]
        open_ref[:, FOLD * q : FOLD * (q + 1)] = jnp.where(same | again, w, 0.0).astype(BF16)
    fold_back(
        enl_ref, lambda at, to: open_ref[at:to, :], contract_last, to_row_ref, to_col_ref, out_ref
    )


def second_kernel(cot_ref, back_ref, enl_ref, row_ref, col_ref, to_row_ref, to_col_ref, out_ref, open_ref):
    w = (cot_ref[...].astype(F32) + back_ref[...].astype(F32)).astype(BF16).astype(F32)
    for q in range(out_ref.shape[0] // FOLD):
        lanes = slice(FOLD * q, FOLD * (q + 1))
        total = jnp.where(col_ref[:WIDE, :] == row_ref[:, lanes], w[:WIDE], 0.0)
        total = total + jnp.where(col_ref[WIDE:, :] == row_ref[:, lanes], w[WIDE:], 0.0)
        open_ref[:, lanes] = total.astype(BF16)

    def product(left, right):
        return jnp.dot(left, right, preferred_element_type=F32)

    fold_back(
        enl_ref, lambda at, to: open_ref[:, at:to], product, to_row_ref, to_col_ref, out_ref
    )


SLOTS = 4
STEP = 256


def grad_kernel(
    edge_ref, near_ref, near_other_ref, w_ref, w_other_ref, row_ref, col_ref, left_ref, right_ref,
    open_ref, mid_ref, stage_ref, sems,
):
    core = lax.rem(lax.axis_index("blk"), 2)
    chi = near_ref.shape[0]
    tiles = chi // FOLD
    steps = edge_ref.shape[0] // STEP
    for side, (near, w) in enumerate(((near_ref, w_ref), (near_other_ref, w_other_ref))):
        for i in range(tiles):
            low, high = near_tiles(i, tiles)
            rows = slice(FOLD * i, FOLD * (i + 1))
            x = w[rows, :].astype(F32)
            for q in range(low, high):
                same = col_ref[rows, :] == row_ref[:, FOLD * q : FOLD * (q + 1)]
                open_ref[:, FOLD * (q - low) : FOLD * (q - low + 1)] = jnp.where(same, x, 0.0).astype(BF16)
            mid_ref[rows, :] = jnp.dot(
                open_ref[:, : FOLD * (high - low)],
                near[FOLD * low : FOLD * high, :],
                preferred_element_type=F32,
            ).astype(BF16)
        for n in range(steps):
            at = side * steps + n
            slot = at % SLOTS
            rows = pl.ds(STEP * n, STEP)
            if at >= SLOTS:
                pltpu.make_async_copy(stage_ref.at[slot], left_ref.at[rows], sems.at[slot]).wait()
            stage_ref[slot] = contract_last(edge_ref[STEP * n : STEP * (n + 1), :], mid_ref[...]).astype(BF16)

            @pl.when(core == side)
            def _():
                pltpu.make_async_copy(stage_ref.at[slot], left_ref.at[rows], sems.at[slot]).start()

            @pl.when(core != side)
            def _():
                pltpu.make_async_copy(stage_ref.at[slot], right_ref.at[rows], sems.at[slot]).start()

    for slot in range(SLOTS):
        pltpu.make_async_copy(stage_ref.at[slot], left_ref.at[pl.ds(0, STEP)], sems.at[slot]).wait()


def call(kernel, out_shape, in_specs, scratch, name, flops, moved, out_specs=VMEM):
    return pl.pallas_call(
        kernel,
        out_shape=out_shape,
        in_specs=in_specs,
        out_specs=out_specs,
        scratch_shapes=scratch,
        name=name,
        cost_estimate=pl.CostEstimate(flops=flops, bytes_accessed=moved, transcendentals=0),
        compiler_params=pltpu.CompilerParams(vmem_limit_bytes=24 << 20),
    )


def body(corner, edge, proj_left, proj_right, charge, cot_left, cot_right):
    sites = lax.axis_size("site")
    members = lax.axis_size("blk")
    rows, chi = corner.shape[1], corner.shape[2]
    depth = edge.shape[2]
    chips = members // 2
    pair_rows = 2 * rows
    blk = lax.axis_index("blk")
    first = blk % 2 == 0
    groups = [[2 * q + core for q in range(chips)] for core in range(2)]

    def swap_cores(x):
        return lax.ppermute(x, "blk", [(i, i ^ 1) for i in range(members)])

    def site_move(x, distance, cross):
        route = []
        for s in range(sites):
            for i in range(members):
                target = i ^ 1 if cross else i
                sign = 1 if target % 2 == 0 else -1
                route.append((s * members + i, ((s + sign * distance) % sites) * members + target))
        return lax.ppermute(x, ("site", "blk"), route)

    def exchange(x):
        return lax.all_to_all(x, "blk", 0, 0, tiled=True, axis_index_groups=groups)

    def spread(x):
        return jnp.broadcast_to(x[None], (chips,) + x.shape)

    def pick(a, b):
        return jnp.where(first, a, b)

    def weave(own, other):
        halves = jnp.stack([pick(own, other), pick(other, own)], axis=1)
        return halves.reshape(chi, own.shape[-1])

    row_label_all = charge
    label = charge[0]
    to_row = site_move(charge, 1, False)
    label_to = to_row[0]
    col = label[:, None]
    to_col = label_to[:, None]
    row_label = lax.dynamic_slice_in_dim(label, blk * rows, rows, 0)
    row_mask = row_label[:, None] == label[None, :]
    here = corner[0]
    start_left = fold_lanes(jnp.where(row_mask, cot_left[0], 0.0), FOLD).astype(BF16)
    start_right = fold_lanes(jnp.where(row_mask, cot_right[0], 0.0), FOLD).astype(BF16)
    tall = jnp.concatenate([here[:, :WIDE], here[:, WIDE:]], axis=0)
    start = jnp.concatenate([tall, jnp.concatenate([start_left, start_right], axis=0)], axis=1)

    edge_flat = edge[0].reshape(rows * depth, chi)
    part_left = contract_first(edge_flat, proj_left[0].reshape(rows * depth, chi))
    part_right = contract_first(edge_flat, proj_right[0].reshape(rows * depth, chi))
    other_part = swap_cores(pick(part_right, part_left).astype(BF16))
    part = pick(part_left, part_right) + other_part.astype(F32)
    part_bf = part.astype(BF16)

    sector = jnp.arange(SECTORS, dtype=jnp.int32)
    in_sector = label_to[None, :] == sector[:, None]
    least = jnp.min(jnp.where(in_sector, label[None, :], SECTORS), axis=1)
    most = jnp.max(jnp.where(in_sector, label[None, :], -1), axis=1)
    low = jnp.sum(jnp.where(label_to[:, None] == sector[None, :], least[None, :], 0), axis=1)
    high = jnp.sum(jnp.where(label_to[:, None] == sector[None, :], most[None, :], 0), axis=1)
    reach = (label[None, :] >= low[:, None]) & (label[None, :] <= high[:, None])
    narrow = fold_lanes(jnp.where(reach, part, 0.0), WIDE).astype(BF16)
    got = exchange(jnp.concatenate([narrow.reshape(chips, pair_rows, WIDE), spread(start)], axis=2))

    summed = call(
        sum_kernel, jax.ShapeDtypeStruct((chips, pair_rows, WIDE), BF16), [VMEM], [], "sum_enl", 0, 2 << 20
    )(got)
    enl = exchange(summed).reshape(chi, WIDE)

    half = jnp.concatenate([got[:, :rows, WIDE : 2 * WIDE], got[:, rows:, WIDE : 2 * WIDE]], axis=2)
    near = weave(site_move(half, 1, False), site_move(half, 1, True))
    near_other = swap_cores(near)
    early_left = got[:, :rows, 2 * WIDE :]
    early_right = got[:, rows:, 2 * WIDE :]
    w0 = weave(pick(early_left, early_right), swap_cores(pick(early_right, early_left)))

    same = label[:, None] == label[None, :]
    w0_open = jnp.where(same, jnp.concatenate([w0] * (chi // FOLD), axis=1), 0.0)
    cot = jnp.transpose(jnp.sum(w0_open.reshape(chi // FOLD, FOLD, chi), axis=0))

    packed = jax.ShapeDtypeStruct((chi, FOLD), BF16)
    back1 = call(
        first_kernel, packed, [VMEM] * 6, [pltpu.VMEM((chi, WIDE), BF16)], "first_back", chi * chi * WIDE, 2 << 20
    )(w0, enl, row_label_all, col, to_row, to_col)
    back1_at = site_move(back1, -1, False)

    near_part, back1_tie = lax.optimization_barrier((part_bf, back1))
    new_part = jnp.dot(near, near_part, preferred_element_type=F32)
    new_part = fold_lanes(jnp.where(same, new_part, 0.0), FOLD).astype(BF16)
    new_got = exchange(new_part.reshape(chips, pair_rows, FOLD))

    back2 = call(
        second_kernel, packed, [VMEM] * 7, [pltpu.VMEM((WIDE, chi), BF16)], "second_back", chi * chi * WIDE, 2 << 20
    )(cot, back1_at, enl, row_label_all, col, to_row, to_col)
    w2 = (cot.astype(F32) + site_move(back2, -1, False).astype(F32)).astype(BF16)
    w2_other = swap_cores(w2)

    new_sum = jnp.sum(new_got.astype(F32), axis=0)
    new_own = pick(new_sum[:rows], new_sum[rows:])
    new_other = swap_cores(pick(new_sum[rows:], new_sum[:rows]))

    def open_new(x):
        return jnp.where(row_mask, jnp.concatenate([x] * (chi // FOLD), axis=1), 0.0).astype(BF16)

    new_left = open_new(pick(new_own, new_other))
    new_right = open_new(pick(new_other, new_own))

    flat = jax.ShapeDtypeStruct((rows * depth, chi), BF16)
    grad_left, grad_right = call(
        grad_kernel,
        (flat, flat),
        [VMEM] * 7,
        [
            pltpu.VMEM((FOLD, WIDE), BF16),
            pltpu.VMEM((chi, chi), BF16),
            pltpu.VMEM((SLOTS, STEP, chi), BF16),
            pltpu.SemaphoreType.DMA((SLOTS,)),
        ],
        "grads",
        4 * rows * depth * chi * chi,
        8 << 20,
        (ANY, ANY),
    )(edge_flat, near, near_other, w2, w2_other, row_label_all, col)
    return (
        new_left[None],
        new_right[None],
        grad_left.reshape(1, rows, depth, chi),
        grad_right.reshape(1, rows, depth, chi),
    )


def solution(mesh):
    row = P("site", "blk", None)
    flat = P("site", "blk", None, None)
    return jax.shard_map(
        body,
        mesh=mesh,
        in_specs=(row, flat, flat, flat, P("site", None), row, row),
        out_specs=(row, row, flat, flat),
        check_vma=False,
    )
```

time: 167 us -> 156 us (0.934)
  blocking collectives: 16.3 us -> 0 us
  waiting for transfers between devices: 50.9 us -> 66.9 us
  matrix products: 25 us -> 10.9 us
  Pallas kernels: 0 us -> 13.8 us
  local copies, waits for them, and re-layouts: 17.1 us -> 10.8 us
  starting transfers between devices: 41.5 us -> 35.4 us
    all_to_all x3, waiting for transfers between devices: 15.2 us -> 35.7 us  [exchange(): return lax.all_to_all(x, 'blk', 0, 0, tiled=True, axis_index_groups=groups)]
    all_to_all x1 -> x0, blocking collectives: 16.3 us -> none  [exchange(): return lax.all_to_all(x, 'blk', 0, 0, tiled=True, axis_index_groups=groups)]
    dot_general x7 -> x1, matrix products: 17.1 us -> 2.35 us  [body(): new_part = jnp.dot(near, near_part, preferred_element_type=F32)]
    pallas_call x0 -> x4, Pallas kernels: none -> 13.8 us  [the longest x1 9.46 us: body(): call(grad_kernel, (flat, flat), [VMEM] * 7, [pltpu.VMEM((FOLD, WIDE), BF1...]
    convert_element_type x2 -> x0, local copies, waits for them, and re-layouts: 8.53 us -> none  [the longest x1 4.27 us: body(): grad_left = contract_last(edge_flat, pick(mid, mid_other)).astype(BF16)]
    all_to_all x3, starting transfers between devices: 24.3 us -> 20.5 us  [exchange(): return lax.all_to_all(x, 'blk', 0, 0, tiled=True, axis_index_groups=groups)]
    select_n x3 -> x0, other arithmetic: 3.7 us -> none  [the longest x1 3.36 us: body(): narrow = fold_lanes(jnp.where(reach, part, 0.0), WIDE).astype(BF16)]
    convert_element_type x3 -> x2, other arithmetic: 0.65 us -> 4.04 us  [the longest x1 3.98 us: body(): part_bf = part.astype(BF16)]
  transfers between devices with their start and end apart: 13 -> 13, of which waited for: 7 -> 8; matrix products, arithmetic and copies ran while one was open for 16% -> 9% of each run, Pallas kernels for 0% -> 2%
where the time goes in v2:
time: 156 us; the launch traced here: 154 us
  waiting for transfers between devices  66.9 us (43%)
  starting transfers between devices  35.4 us (23%)
  other arithmetic  14.8 us (9%)
  Pallas kernels  13.8 us (9%)
  matrix products  10.9 us (7%)
  local copies, waits for them, and re-layouts  10.8 us (7%)
    all_to_all x3, waiting for transfers between devices, exchange(): return lax.all_to_all(x, 'blk', 0, 0, tiled=True, axis_index_groups=groups)  35.7 us
    ppermute x5, waiting for transfers between devices, site_move(): return lax.ppermute(x, ('site', 'blk'), route)  30.7 us
    all_to_all x3, starting transfers between devices, exchange(): return lax.all_to_all(x, 'blk', 0, 0, tiled=True, axis_index_groups=groups)  20.5 us
    pallas_call x1, Pallas kernels, body(): call(grad_kernel, (flat, flat), [VMEM] * 7, [pltpu.VMEM((FOLD, WIDE), BF1...  9.46 us
    ppermute x5, starting transfers between devices, swap_cores(): return lax.ppermute(x, 'blk', [(i, i ^ 1) for i in range(members)])  8.67 us
    dot_general x2, matrix products, contract_first(): lax.dot_general(left, right, (((0,), (0,)), ((), ())), preferred_element_...  8.53 us
    ppermute x5, starting transfers between devices, site_move(): return lax.ppermute(x, ('site', 'blk'), route)  6.26 us
    unnamed x43, local copies, waits for them, and re-layouts  5.48 us
  transfers between devices with their start and end apart: 13, of which 8 were waited for; matrix products, arithmetic and copies ran while one was open for 9% of the time, Pallas kernels for 2%

profile of v2, /device:TPU:1, one launch (start us, length us, event | category | flops | bytes accessed | tf_op | source)
XLA Modules:
  0.0 153.8 jit_solution(17543745166431847671)
XLA Ops:
  0.7 4.6 %fusion.4 = f32[768,768,1]{1,0,2:T(8,128)S(1)} fusion(bf16[1,24,64,768]{3,2,1,0:T(8,128)(2,1)} %param.9, bf16[1,24,64,768]{3,2,1,0:T(8,128)(2,1)} %param.8), kind=kOutput, calls=%fused_computation.6 | convolution fusion | flops 1811939328 | bytes 7077888 | tf_op jit(solution)/shard_map/dot_general | solution.py:18
  5.4 3.9 %fusion.1 = (bf16[768,768]{1,0:T(8,128)(2,1)}, f32[768,768,1]{1,0,2:T(8,128)}) fusion(f32[768,768,1]{1,0,2:T(8,128)S(1)} %fusion.4, pred[]{:T(512)S(6)} %eq.98, bf16[1,24,64,768]{3,2,1,0:T(8,128)(2,1)S(1)} %copy-done, bf16[1,24,64,768]{3,2,1,0:T(8,128)(2,1)S(1)} %copy-done.3), kind=kOutput, calls=%fused_computation.3 | convolution fusion | flops 1812529152 | bytes 10616833 | tf_op jit(solution)/shard_map/dot_general | solution.py:18
  9.3 3.2 %collective-permute-start.1 = (bf16[768,768]{1,0:T(8,128)(2,1)}, bf16[768,768]{1,0:T(8,128)(2,1)}, u32[]{:S(2)}, u32[]{:S(2)}) collective-permute-start(bf16[768,768]{1,0:T(8,128)(2,1)} %get-tuple-element.34), channel_id=1, source_target_pairs={{0,1},{1,0},{2,3},{3,2},{4,5},{5,4},{6,7},{7,6},{8,9},{9,8},{10,11... | collective-permute-start | bytes 3538952 | tf_op jit(solution)/shard_map/ppermute | solution.py:154
  12.5 1.8 %collective-permute-start = (s32[1,768]{1,0:T(1,128)S(1)}, s32[1,768]{1,0:T(1,128)S(1)}, u32[]{:S(2)}, u32[]{:S(2)}) collective-permute-start(s32[1,768]{1,0:T(1,128)S(1)} %copy-done.9), channel_id=1, source_target_pairs={{0,32},{1,225},{2,34},{3,227},{4,36},{5,229},{6,38},{7,231},{8,40}... | collective-permute-start | bytes 9224 | tf_op jit(solution)/shard_map/ppermute | solution.py:163
  15.3 4.0 %fusion.11 = (bf16[768,768]{1,0:T(8,128)(2,1)}, f32[768,768]{1,0:T(8,128)S(1)}) fusion(bf16[768,768]{1,0:T(8,128)(2,1)} %collective-permute-done.1, f32[768,768,1]{1,0,2:T(8,128)} %get-tuple-element.35, f32[768,768,1]{1,0,2:T(8,128)} %copy-done.10, pred[]{:T(512)S(6)} %eq.98, s32[768]{0:T(1024)S(1)} %get-tuple-element.13, s32[768]{0:T(1024)S(1)} %get-tuple-element.12, ...), kind=kLoop, calls=%fused_computation.29 | loop fusion | flops 4718592 | bytes 9446401 | tf_op jit(solution)/shard_map/convert_element_type | solution.py:197
  19.5 1.2 pad_maximum_fusion
  20.7 10.7 %all-to-all-start = ((bf16[16,48,896]{2,1,0:T(8,128)(2,1)}), bf16[16,48,896]{2,1,0:T(8,128)(2,1)}, u32[]{:S(2)}, u32[]{:S(2)}) async-start(bf16[16,48,896]{2,1,0:T(8,128)(2,1)} %pad_maximum_fusion), calls=%async_computation | async-start | bytes 2752512 | tf_op jit(solution)/shard_map/all_to_all | solution.py:166
  32.5 32.2 %all-to-all-done.got_ref = bf16[16,48,896]{2,1,0:T(8,128)(2,1)} async-done(((bf16[16,48,896]{2,1,0:T(8,128)(2,1)}), bf16[16,48,896]{2,1,0:T(8,128)(2,1)}, u32[]{:S(2)}, u32[]{:S(2)}) %all-to-all-start) | async-done | bytes 1376288 | tf_op jit(solution)/shard_map/all_to_all | solution.py:166
  65.7 3.3 %collective-permute-start.4 = (bf16[16,24,128]{2,1,0:T(8,128)(2,1)S(1)}, bf16[16,24,128]{2,1,0:T(8,128)(2,1)}, u32[]{:S(2)}, u32[]{:S(2)}) collective-permute-start(bf16[16,24,128]{2,1,0:T(8,128)(2,1)S(1)} %broadcast_select_fusion), channel_id=1, source_target_pairs={{0,1},{1,0},{2,3},{3,2},{4,5},{5,4},{6,7},{7,6},{8,9},{9,8},{10,11... | collective-permute-start | bytes 294920 | tf_op jit(solution)/shard_map/ppermute | solution.py:154
  69.1 1.1 fusion.16
  71.0 3.1 %collective-permute-start.2 = (bf16[16,24,768]{2,1,0:T(8,128)(2,1)}, bf16[16,24,768]{2,1,0:T(8,128)(2,1)}, u32[]{:S(2)}, u32[]{:S(2)}) collective-permute-start(bf16[16,24,768]{2,1,0:T(8,128)(2,1)} %pad_maximum_fusion.2), channel_id=1, source_target_pairs={{0,32},{1,225},{2,34},{3,227},{4,36},{5,229},{6,38},{7,231},{8,40}... | collective-permute-start | bytes 1769480 | tf_op jit(solution)/shard_map/ppermute | solution.py:163
  74.1 1.4 sum_enl.1
  76.4 5.5 %all-to-all-start.1 = ((bf16[16,48,384]{2,1,0:T(8,128)(2,1)}), bf16[16,48,384]{2,1,0:T(8,128)(2,1)S(1)}, u32[]{:S(2)}, u32[]{:S(2)}) async-start(bf16[16,48,384]{2,1,0:T(8,128)(2,1)} %copy-done.5), calls=%async_computation.1 | async-start | bytes 1179648 | tf_op jit(solution)/shard_map/all_to_all | solution.py:166
  81.9 1.0 select_bitcast_fusion.3
  83.2 19.3 %collective-permute-done.2 = bf16[16,24,768]{2,1,0:T(8,128)(2,1)} collective-permute-done((bf16[16,24,768]{2,1,0:T(8,128)(2,1)}, bf16[16,24,768]{2,1,0:T(8,128)(2,1)}, u32[]{:S(2)}, u32[]{:S(2)}) %collective-permute-start.2) | collective-permute-done | bytes 589856 | tf_op jit(solution)/shard_map/ppermute | solution.py:163
  102.5 2.5 %collective-permute-done.3 = bf16[16,24,768]{2,1,0:T(8,128)(2,1)} collective-permute-done((bf16[16,24,768]{2,1,0:T(8,128)(2,1)}, bf16[16,24,768]{2,1,0:T(8,128)(2,1)}, u32[]{:S(2)}, u32[]{:S(2)}) %collective-permute-start.3) | collective-permute-done | bytes 589856 | tf_op jit(solution)/shard_map/ppermute | solution.py:163
  105.0 1.3 select_bitcast_fusion.1
  106.4 1.1 copy.30
  107.5 1.0 copy-done.1
  109.8 2.4 %compare_select_fusion.1 = f32[768,768]{1,0:T(8,128)S(1)} fusion(bf16[768,768]{1,0:T(8,128)(2,1)S(1)} %bitcast.90, bf16[768,768]{1,0:T(8,128)(2,1)} %get-tuple-element.7, s32[768]{0:T(1024)S(1)} %reduce.1), kind=kOutput, calls=%fused_computation.12 | convolution fusion | flops 907149312 | bytes 4721664 | tf_op jit(solution)/shard_map/dot_general | solution.py:232
  112.9 4.4 %all-to-all-start.2 = ((bf16[16,48,128]{2,1,0:T(8,128)(2,1)}), bf16[16,48,128]{2,1,0:T(8,128)(2,1)}, u32[]{:S(2)}, u32[]{:S(2)}) async-start(bf16[16,48,128]{2,1,0:T(8,128)(2,1)} %bitcast.95), calls=%async_computation.2 | async-start | bytes 393216 | tf_op jit(solution)/shard_map/all_to_all | solution.py:166
  118.7 2.4 %fusion.8 = bf16[128,768]{1,0:T(8,128)(2,1)} fusion(bf16[6,128,768]{2,1,0:T(8,128)(2,1)} %constant_dynamic-update-slice_fusion.12, s32[768]{0:T(1024)S(1)} %reduce.1, s32[6,128]{1,0:T(8,128)S(1)} %bitcast.96), kind=kLoop, calls=%fused_computation.14 | loop fusion | flops 1671168 | bytes 1382400 | tf_op jit(solution)/shard_map/reduce_sum | solution.py:223
  121.0 1.1 copy.35
  122.2 1.2 collective-permute-start.7
  123.4 3.5 %all-to-all-done.2 = bf16[16,48,128]{2,1,0:T(8,128)(2,1)} async-done(((bf16[16,48,128]{2,1,0:T(8,128)(2,1)}), bf16[16,48,128]{2,1,0:T(8,128)(2,1)}, u32[]{:S(2)}, u32[]{:S(2)}) %all-to-all-start.2) | async-done | bytes 196640 | tf_op jit(solution)/shard_map/all_to_all | solution.py:166
  128.3 1.9 %collective-permute-done.7.back_ref = bf16[768,128]{1,0:T(8,128)(2,1)} collective-permute-done((bf16[768,128]{1,0:T(8,128)(2,1)}, bf16[768,128]{1,0:T(8,128)(2,1)}, u32[]{:S(2)}, u32[]{:S(2)}) %collective-permute-start.7) | collective-permute-done | bytes 196640 | tf_op jit(solution)/shard_map/ppermute | solution.py:163
  130.2 1.0 copy-done.2
  131.2 2.1 %second_back.1 = bf16[768,128]{1,0:T(8,128)(2,1)S(1)} custom-call(bf16[768,128]{1,0:T(8,128)(2,1)S(1)} %bitcast.88, bf16[768,128]{1,0:T(8,128)(2,1)} %collective-permute-done.7.back_ref, bf16[768,384]{1,0:T(8,128)(2,1)S(1)} %bitcast.86, s32[1,768]{1,0:T(1,128)S(1)} %copy-done.9, s32[768,1]{1,0:T(8,128)S(1)} %copy.32.col_ref, ...), custom_call_target="tpu_custom_call" | custom-call | flops 226492416 | bytes 2097152 | tf_op jit(solution)/shard_map/second_back/pallas_call | solution.py:236
  133.7 6.5 %collective-permute-done.8 = bf16[768,128]{1,0:T(8,128)(2,1)S(1)} collective-permute-done((bf16[768,128]{1,0:T(8,128)(2,1)S(1)}, bf16[768,128]{1,0:T(8,128)(2,1)S(1)}, u32[]{:S(2)}, u32[]{:S(2)}) %collective-permute-start.8) | collective-permute-done | bytes 196640 | tf_op jit(solution)/shard_map/ppermute | solution.py:163
  140.2 1.6 %collective-permute-start.9 = (bf16[768,128]{1,0:T(8,128)(2,1)S(1)}, bf16[768,128]{1,0:T(8,128)(2,1)S(1)}, u32[]{:S(2)}, u32[]{:S(2)}) collective-permute-start(bf16[768,128]{1,0:T(8,128)(2,1)S(1)} %add_convert_fusion.w_ref), channel_id=1, source_target_pairs={{0,1},{1,0},{2,3},{3,2},{4,5},{5,4},{6,7},{7,6},{8,9},{9,8},{10,11... | collective-permute-start | bytes 589832 | tf_op jit(solution)/shard_map/ppermute | solution.py:154
  142.9 1.3 copy-done.7
  144.2 9.5 %grads.1 = (bf16[1536,768]{1,0:T(8,128)(2,1)}, bf16[1536,768]{1,0:T(8,128)(2,1)}) custom-call(bf16[1536,768]{1,0:T(8,128)(2,1)S(1)} %bitcast.87, bf16[768,768]{1,0:T(8,128)(2,1)S(1)} %bitcast.91, bf16[768,768]{1,0:T(8,128)(2,1)} %collective-permute-done.6.near_other_ref, bf16[768,128]{1,0:T(8,128)(2,1)S(1)} %add_convert_fusion.w_ref, ...), custom_call_target="tpu_custom_call" | custom-call | flops 3623878656 | bytes 8388608 | tf_op jit(solution)/shard_map/grads/pallas_call | solution.py:253
  (79 shorter events, 11.6 us)
Async XLA Ops:
  0.6 4.7 %copy-start = (bf16[1,24,64,768]{3,2,1,0:T(8,128)(2,1)S(1)}, bf16[1,24,64,768]{3,2,1,0:T(8,128)(2,1)}, u32[]{:S(2)}) copy-start(bf16[1,24,64,768]{3,2,1,0:T(8,128)(2,1)} %param.10) | copy-start | bytes 7077892
  0.7 4.6 %copy-start.3 = (bf16[1,24,64,768]{3,2,1,0:T(8,128)(2,1)S(1)}, bf16[1,24,64,768]{3,2,1,0:T(8,128)(2,1)}, u32[]{:S(2)}) copy-start(bf16[1,24,64,768]{3,2,1,0:T(8,128)(2,1)} %param.8) | copy-start | bytes 7077892
  5.3 4.0 %copy-start.10 = (f32[768,768,1]{1,0,2:T(8,128)}, f32[768,768,1]{1,0,2:T(8,128)S(1)}, u32[]{:S(2)}) copy-start(f32[768,768,1]{1,0,2:T(8,128)S(1)} %fusion.4) | copy-start | bytes 7077892
  5.3 7.2 %copy-start.9 = (s32[1,768]{1,0:T(1,128)S(1)}, s32[1,768]{1,0:T(1,128)}, u32[]{:S(2)}) copy-start(s32[1,768]{1,0:T(1,128)} %row_ref.5) | copy-start | bytes 9220
  5.3 9.1 %copy-start.12 = (f32[1,24,768]{2,1,0:T(8,128)S(1)}, f32[1,24,768]{2,1,0:T(8,128)}, u32[]{:S(2)}) copy-start(f32[1,24,768]{2,1,0:T(8,128)} %param.12) | copy-start | bytes 221188
  5.3 9.0 %copy-start.13 = (f32[1,24,768]{2,1,0:T(8,128)S(1)}, f32[1,24,768]{2,1,0:T(8,128)}, u32[]{:S(2)}) copy-start(f32[1,24,768]{2,1,0:T(8,128)} %param.13) | copy-start | bytes 221188
  5.4 9.1 %copy-start.14 = (bf16[1,24,768]{2,1,0:T(8,128)(2,1)S(1)}, bf16[1,24,768]{2,1,0:T(8,128)(2,1)}, u32[]{:S(2)}) copy-start(bf16[1,24,768]{2,1,0:T(8,128)(2,1)} %param.7) | copy-start | bytes 110596
  9.3 6.0 %collective-permute-start.1 = (bf16[768,768]{1,0:T(8,128)(2,1)}, bf16[768,768]{1,0:T(8,128)(2,1)}, u32[]{:S(2)}, u32[]{:S(2)}) collective-permute-start(bf16[768,768]{1,0:T(8,128)(2,1)} %get-tuple-element.34), channel_id=1, source_target_pairs={{0,1},{1,0},{2,3},{3,2},{4,5},{5,4},{6,7},{7,6},{8,9},{9,8},{10,11... | collective-permute-start | bytes 3538952 | tf_op jit(solution)/shard_map/ppermute | solution.py:154
  12.5 2.5 %collective-permute-start = (s32[1,768]{1,0:T(1,128)S(1)}, s32[1,768]{1,0:T(1,128)S(1)}, u32[]{:S(2)}, u32[]{:S(2)}) collective-permute-start(s32[1,768]{1,0:T(1,128)S(1)} %copy-done.9), channel_id=1, source_target_pairs={{0,32},{1,225},{2,34},{3,227},{4,36},{5,229},{6,38},{7,231},{8,40}... | collective-permute-start | bytes 9224 | tf_op jit(solution)/shard_map/ppermute | solution.py:163
  20.7 44.0 %all-to-all-start = ((bf16[16,48,896]{2,1,0:T(8,128)(2,1)}), bf16[16,48,896]{2,1,0:T(8,128)(2,1)}, u32[]{:S(2)}, u32[]{:S(2)}) async-start(bf16[16,48,896]{2,1,0:T(8,128)(2,1)} %pad_maximum_fusion), calls=%async_computation | async-start | bytes 2752512 | tf_op jit(solution)/shard_map/all_to_all | solution.py:166
  65.7 16.1 %collective-permute-start.4 = (bf16[16,24,128]{2,1,0:T(8,128)(2,1)S(1)}, bf16[16,24,128]{2,1,0:T(8,128)(2,1)}, u32[]{:S(2)}, u32[]{:S(2)}) collective-permute-start(bf16[16,24,128]{2,1,0:T(8,128)(2,1)S(1)} %broadcast_select_fusion), channel_id=1, source_target_pairs={{0,1},{1,0},{2,3},{3,2},{4,5},{5,4},{6,7},{7,6},{8,9},{9,8},{10,11... | collective-permute-start | bytes 294920 | tf_op jit(solution)/shard_map/ppermute | solution.py:154
  71.0 31.4 %collective-permute-start.2 = (bf16[16,24,768]{2,1,0:T(8,128)(2,1)}, bf16[16,24,768]{2,1,0:T(8,128)(2,1)}, u32[]{:S(2)}, u32[]{:S(2)}) collective-permute-start(bf16[16,24,768]{2,1,0:T(8,128)(2,1)} %pad_maximum_fusion.2), channel_id=1, source_target_pairs={{0,32},{1,225},{2,34},{3,227},{4,36},{5,229},{6,38},{7,231},{8,40}... | collective-permute-start | bytes 1769480 | tf_op jit(solution)/shard_map/ppermute | solution.py:163
  74.1 30.8 %collective-permute-start.3 = (bf16[16,24,768]{2,1,0:T(8,128)(2,1)}, bf16[16,24,768]{2,1,0:T(8,128)(2,1)}, u32[]{:S(2)}, u32[]{:S(2)}) collective-permute-start(bf16[16,24,768]{2,1,0:T(8,128)(2,1)} %pad_maximum_fusion.2), channel_id=1, source_target_pairs={{0,225},{1,32},{2,227},{3,34},{4,229},{5,36},{6,231},{7,38},{8,233... | collective-permute-start | bytes 1769480 | tf_op jit(solution)/shard_map/ppermute | solution.py:163
  75.6 0.8 copy-start.5
  76.4 31.1 %all-to-all-start.1 = ((bf16[16,48,384]{2,1,0:T(8,128)(2,1)}), bf16[16,48,384]{2,1,0:T(8,128)(2,1)S(1)}, u32[]{:S(2)}, u32[]{:S(2)}) async-start(bf16[16,48,384]{2,1,0:T(8,128)(2,1)} %copy-done.5), calls=%async_computation.1 | async-start | bytes 1179648 | tf_op jit(solution)/shard_map/all_to_all | solution.py:166
  83.2 19.3 %copy-start.11 = (bf16[6,128,768]{2,1,0:T(8,128)(2,1)}, bf16[6,128,768]{2,1,0:T(8,128)(2,1)S(1)}, u32[]{:S(2)}) copy-start(bf16[6,128,768]{2,1,0:T(8,128)(2,1)S(1)} %constant_dynamic-update-slice_fusion.14) | copy-start | bytes 3538948
  107.5 1.0 copy-start.1
  108.5 1.3 copy-start.6
  109.4 2.8 %copy-start.8 = (bf16[768,128]{1,0:T(8,128)(2,1)}, bf16[768,128]{1,0:T(8,128)(2,1)S(1)}, u32[]{:S(2)}) copy-start(bf16[768,128]{1,0:T(8,128)(2,1)S(1)} %first_back.1) | copy-start | bytes 589828
  112.9 14.0 %all-to-all-start.2 = ((bf16[16,48,128]{2,1,0:T(8,128)(2,1)}), bf16[16,48,128]{2,1,0:T(8,128)(2,1)}, u32[]{:S(2)}, u32[]{:S(2)}) async-start(bf16[16,48,128]{2,1,0:T(8,128)(2,1)} %bitcast.95), calls=%async_computation.2 | async-start | bytes 393216 | tf_op jit(solution)/shard_map/all_to_all | solution.py:166
  122.1 20.8 %collective-permute-start.6 = (bf16[768,768]{1,0:T(8,128)(2,1)}, bf16[768,768]{1,0:T(8,128)(2,1)}, u32[]{:S(2)}, u32[]{:S(2)}) collective-permute-start(bf16[768,768]{1,0:T(8,128)(2,1)} %bitcast.89), channel_id=1, source_target_pairs={{0,1},{1,0},{2,3},{3,2},{4,5},{5,4},{6,7},{7,6},{8,9},{9,8},{10,11... | collective-permute-start | bytes 3538952 | tf_op jit(solution)/shard_map/ppermute | solution.py:154
  122.2 8.0 %collective-permute-start.7 = (bf16[768,128]{1,0:T(8,128)(2,1)}, bf16[768,128]{1,0:T(8,128)(2,1)}, u32[]{:S(2)}, u32[]{:S(2)}) collective-permute-start(bf16[768,128]{1,0:T(8,128)(2,1)} %copy-done.8), channel_id=1, source_target_pairs={{0,224},{1,33},{2,226},{3,35},{4,228},{5,37},{6,230},{7,39},{8,232... | collective-permute-start | bytes 589832 | tf_op jit(solution)/shard_map/ppermute | solution.py:163
  127.9 5.6 %collective-permute-start.5 = (bf16[24,128]{1,0:T(8,128)(2,1)S(1)}, bf16[24,128]{1,0:T(8,128)(2,1)S(1)}, u32[]{:S(2)}, u32[]{:S(2)}) collective-permute-start(bf16[24,128]{1,0:T(8,128)(2,1)S(1)} %slice_select_fusion), channel_id=1, source_target_pairs={{0,1},{1,0},{2,3},{3,2},{4,5},{5,4},{6,7},{7,6},{8,9},{9,8},{10,11... | collective-permute-start | bytes 18440 | tf_op jit(solution)/shard_map/ppermute | solution.py:154
  130.2 1.0 copy-start.2
  131.2 11.7 %copy-start.4 = (bf16[1,24,64,768]{3,2,1,0:T(8,128)(2,1)S(1)}, bf16[1,24,64,768]{3,2,1,0:T(8,128)(2,1)}, u32[]{:S(2)}) copy-start(bf16[1,24,64,768]{3,2,1,0:T(8,128)(2,1)} %param.8) | copy-start | bytes 7077892
  133.3 6.8 %collective-permute-start.8 = (bf16[768,128]{1,0:T(8,128)(2,1)S(1)}, bf16[768,128]{1,0:T(8,128)(2,1)S(1)}, u32[]{:S(2)}, u32[]{:S(2)}) collective-permute-start(bf16[768,128]{1,0:T(8,128)(2,1)S(1)} %second_back.1), channel_id=1, source_target_pairs={{0,224},{1,33},{2,226},{3,35},{4,228},{5,37},{6,230},{7,39},{8,232... | collective-permute-start | bytes 589832 | tf_op jit(solution)/shard_map/ppermute | solution.py:163
  140.2 2.7 %collective-permute-start.9 = (bf16[768,128]{1,0:T(8,128)(2,1)S(1)}, bf16[768,128]{1,0:T(8,128)(2,1)S(1)}, u32[]{:S(2)}, u32[]{:S(2)}) collective-permute-start(bf16[768,128]{1,0:T(8,128)(2,1)S(1)} %add_convert_fusion.w_ref), channel_id=1, source_target_pairs={{0,1},{1,0},{2,3},{3,2},{4,5},{5,4},{6,7},{7,6},{8,9},{9,8},{10,11... | collective-permute-start | bytes 589832 | tf_op jit(solution)/shard_map/ppermute | solution.py:154
  142.9 1.3 copy-start.7

commit v3 on v2

--- a/solution.py
+++ b/solution.py
@@ -4,6 +4,7 @@
 from jax.experimental import pallas as pl
 from jax.experimental.pallas import tpu as pltpu
 from jax.sharding import PartitionSpec as P
+
 
 SECTORS = 16
 FOLD = 128
@@ -34,11 +35,129 @@
     return max(0, i - 1), min(tiles, i + 2)
 
 
-def sum_kernel(got_ref, out_ref):
+def pack_kernel(
+    part_ref, other_ref, low_ref, high_ref, row_ref, corner_ref, cot_left_ref, cot_right_ref, own_ref,
+    out_ref, part_out_ref,
+):
+    chips, pair_rows = out_ref.shape[:2]
+    rows = pair_rows // 2
+    for q in range(chips):
+        at = slice(pair_rows * q, pair_rows * (q + 1))
+        part = part_ref[at, :] + other_ref[at, :].astype(F32)
+        part_out_ref[at, :] = part.astype(BF16)
+        label = row_ref[...]
+        part = jnp.where((label >= low_ref[at, :]) & (label <= high_ref[at, :]), part, 0.0)
+        out_ref[q, :, :WIDE] = (part[:, :WIDE] + part[:, WIDE:]).astype(BF16)
+    mask = own_ref[...] == row_ref[...]
+    for q in range(chips):
+        out_ref[q, :rows, WIDE : 2 * WIDE] = corner_ref[:, :WIDE]
+        out_ref[q, rows:, WIDE : 2 * WIDE] = corner_ref[:, WIDE:]
+    for n, cot_ref in enumerate((cot_left_ref, cot_right_ref)):
+        cot = fold_lanes(jnp.where(mask, cot_ref[...], 0.0), FOLD).astype(BF16)
+        for q in range(chips):
+            out_ref[q, rows * n : rows * (n + 1), 2 * WIDE :] = cot
+
+
+def sum_kernel(got_ref, out_ref, corner_ref, early_ref):
     total = got_ref[0, :, :WIDE].astype(F32)
     for q in range(1, got_ref.shape[0]):
         total = total + got_ref[q, :, :WIDE].astype(F32)
     out_ref[...] = jnp.broadcast_to(total.astype(BF16)[None], out_ref.shape)
+    corner_ref[...] = got_ref[:, :, WIDE : 2 * WIDE]
+    early_ref[...] = got_ref[:, :, 2 * WIDE :]
+
+
+def start_kernel(early_ref, other_ref, row_ref, col_ref, w_ref, cot_ref):
+    chips, pair_rows, _ = early_ref.shape
+    rows = pair_rows // 2
+    core = lax.rem(lax.axis_index("blk"), 2)
+
+    @pl.when(core == 0)
+    def _():
+        for q in range(chips):
+            w_ref[pair_rows * q : pair_rows * q + rows, :] = early_ref[q, :rows, :]
+            w_ref[pair_rows * q + rows : pair_rows * (q + 1), :] = other_ref[q, :rows, :]
+
+    @pl.when(core == 1)
+    def _():
+        for q in range(chips):
+            w_ref[pair_rows * q : pair_rows * q + rows, :] = other_ref[q, rows:, :]
+            w_ref[pair_rows * q + rows : pair_rows * (q + 1), :] = early_ref[q, rows:, :]
+
+    tiles = w_ref.shape[0] // FOLD
+    for i in range(tiles):
+        low, high = near_tiles(i, tiles)
+        lanes = slice(FOLD * i, FOLD * (i + 1))
+        total = jnp.zeros((FOLD, FOLD), F32)
+        for q in range(low, high):
+            at = slice(FOLD * q, FOLD * (q + 1))
+            same = col_ref[at, :] == row_ref[:, lanes]
+            total = total + jnp.where(same, w_ref[at, :].astype(F32), 0.0)
+        cot_ref[lanes, :] = total.T
+
+
+def weave_kernel(same_ref, cross_ref, out_ref):
+    chips, pair_rows, width = same_ref.shape
+    rows = pair_rows // 2
+    core = lax.rem(lax.axis_index("blk"), 2)
+
+    def put(low_ref, high_ref):
+        for q in range(chips):
+            for n, ref in enumerate((low_ref, high_ref)):
+                at = pair_rows * q + rows * n
+                out_ref[at : at + rows, :width] = ref[q, :rows, :]
+                out_ref[at : at + rows, width:] = ref[q, rows:, :]
+
+    @pl.when(core == 0)
+    def _():
+        put(same_ref, cross_ref)
+
+    @pl.when(core == 1)
+    def _():
+        put(cross_ref, same_ref)
+
+
+def new_kernel(near_ref, part_ref, row_ref, col_ref, out_ref):
+    tiles = near_ref.shape[0] // FOLD
+    for i in range(tiles):
+        low, high = near_tiles(i, tiles)
+        rows = slice(FOLD * i, FOLD * (i + 1))
+        product = jnp.dot(
+            near_ref[rows, :], part_ref[:, FOLD * low : FOLD * high], preferred_element_type=F32
+        )
+        total = jnp.zeros((FOLD, FOLD), F32)
+        for q in range(low, high):
+            same = col_ref[rows, :] == row_ref[:, FOLD * q : FOLD * (q + 1)]
+            total = total + jnp.where(same, product[:, FOLD * (q - low) : FOLD * (q - low + 1)], 0.0)
+        out_ref[rows, :] = total.astype(BF16)
+
+
+def total_kernel(got_ref, out_ref):
+    total = got_ref[0].astype(F32)
+    for q in range(1, got_ref.shape[0]):
+        total = total + got_ref[q].astype(F32)
+    out_ref[...] = total
+
+
+def open_kernel(own_ref, other_ref, label_ref, row_ref, left_ref, right_ref):
+    rows, chi = left_ref.shape
+    core = lax.rem(lax.axis_index("blk"), 2)
+    mask = label_ref[...] == row_ref[...]
+
+    def put(out_ref, x):
+        for q in range(chi // FOLD):
+            lanes = slice(FOLD * q, FOLD * (q + 1))
+            out_ref[:, lanes] = jnp.where(mask[:, lanes], x, 0.0).astype(BF16)
+
+    @pl.when(core == 0)
+    def _():
+        put(left_ref, own_ref[:rows, :])
+        put(right_ref, other_ref[:rows, :])
+
+    @pl.when(core == 1)
+    def _():
+        put(right_ref, own_ref[rows:, :])
+        put(left_ref, other_ref[rows:, :])
 
 
 def fold_back(enl_ref, operand, contract, to_row_ref, to_col_ref, out_ref):
@@ -126,14 +245,13 @@
         pltpu.make_async_copy(stage_ref.at[slot], left_ref.at[pl.ds(0, STEP)], sems.at[slot]).wait()
 
 
-def call(kernel, out_shape, in_specs, scratch, name, flops, moved, out_specs=VMEM):
+def call(kernel, out_shape, in_specs, scratch, flops, moved, out_specs=VMEM):
     return pl.pallas_call(
         kernel,
         out_shape=out_shape,
         in_specs=in_specs,
         out_specs=out_specs,
         scratch_shapes=scratch,
-        name=name,
         cost_estimate=pl.CostEstimate(flops=flops, bytes_accessed=moved, transcendentals=0),
         compiler_params=pltpu.CompilerParams(vmem_limit_bytes=24 << 20),
     )
@@ -165,36 +283,22 @@
     def exchange(x):
         return lax.all_to_all(x, "blk", 0, 0, tiled=True, axis_index_groups=groups)
 
-    def spread(x):
-        return jnp.broadcast_to(x[None], (chips,) + x.shape)
-
     def pick(a, b):
         return jnp.where(first, a, b)
 
-    def weave(own, other):
-        halves = jnp.stack([pick(own, other), pick(other, own)], axis=1)
-        return halves.reshape(chi, own.shape[-1])
-
-    row_label_all = charge
+    row = charge
     label = charge[0]
     to_row = site_move(charge, 1, False)
     label_to = to_row[0]
     col = label[:, None]
     to_col = label_to[:, None]
-    row_label = lax.dynamic_slice_in_dim(label, blk * rows, rows, 0)
-    row_mask = row_label[:, None] == label[None, :]
-    here = corner[0]
-    start_left = fold_lanes(jnp.where(row_mask, cot_left[0], 0.0), FOLD).astype(BF16)
-    start_right = fold_lanes(jnp.where(row_mask, cot_right[0], 0.0), FOLD).astype(BF16)
-    tall = jnp.concatenate([here[:, :WIDE], here[:, WIDE:]], axis=0)
-    start = jnp.concatenate([tall, jnp.concatenate([start_left, start_right], axis=0)], axis=1)
+    own_label = lax.dynamic_slice_in_dim(label, blk * rows, rows, 0)[:, None]
 
     edge_flat = edge[0].reshape(rows * depth, chi)
     part_left = contract_first(edge_flat, proj_left[0].reshape(rows * depth, chi))
     part_right = contract_first(edge_flat, proj_right[0].reshape(rows * depth, chi))
     other_part = swap_cores(pick(part_right, part_left).astype(BF16))
-    part = pick(part_left, part_right) + other_part.astype(F32)
-    part_bf = part.astype(BF16)
+    part = pick(part_left, part_right)
 
     sector = jnp.arange(SECTORS, dtype=jnp.int32)
     in_sector = label_to[None, :] == sector[:, None]
@@ -202,54 +306,60 @@
     most = jnp.max(jnp.where(in_sector, label[None, :], -1), axis=1)
     low = jnp.sum(jnp.where(label_to[:, None] == sector[None, :], least[None, :], 0), axis=1)
     high = jnp.sum(jnp.where(label_to[:, None] == sector[None, :], most[None, :], 0), axis=1)
-    reach = (label[None, :] >= low[:, None]) & (label[None, :] <= high[:, None])
-    narrow = fold_lanes(jnp.where(reach, part, 0.0), WIDE).astype(BF16)
-    got = exchange(jnp.concatenate([narrow.reshape(chips, pair_rows, WIDE), spread(start)], axis=2))
-
-    summed = call(
-        sum_kernel, jax.ShapeDtypeStruct((chips, pair_rows, WIDE), BF16), [VMEM], [], "sum_enl", 0, 2 << 20
+
+    def array(*shape, dtype=BF16):
+        return jax.ShapeDtypeStruct(shape, dtype)
+
+    packed, part_bf = call(
+        pack_kernel,
+        (array(chips, pair_rows, 2 * WIDE + FOLD), array(chi, chi)),
+        [VMEM] * 9,
+        [],
+        chi * chi * 8,
+        6 << 20,
+        (VMEM, VMEM),
+    )(part, other_part, low[:, None], high[:, None], row, corner[0], cot_left[0], cot_right[0], own_label)
+    got = exchange(packed)
+    summed, corner_half, early = call(
+        sum_kernel,
+        (array(chips, pair_rows, WIDE), array(chips, pair_rows, WIDE), array(chips, pair_rows, FOLD)),
+        [VMEM],
+        [],
+        0,
+        3 << 20,
+        (VMEM, VMEM, VMEM),
     )(got)
     enl = exchange(summed).reshape(chi, WIDE)
 
-    half = jnp.concatenate([got[:, :rows, WIDE : 2 * WIDE], got[:, rows:, WIDE : 2 * WIDE]], axis=2)
-    near = weave(site_move(half, 1, False), site_move(half, 1, True))
+    early_other = swap_cores(early)
+    w0, cot = call(
+        start_kernel, (array(chi, FOLD), array(chi, FOLD, dtype=F32)), [VMEM] * 4, [], 0, 1 << 20, (VMEM, VMEM)
+    )(early, early_other, row, col)
+    corner_same = site_move(corner_half, 1, False)
+    corner_cross = site_move(corner_half, 1, True)
+    near = call(weave_kernel, array(chi, chi), [VMEM] * 2, [], 0, 3 << 20)(corner_same, corner_cross)
     near_other = swap_cores(near)
-    early_left = got[:, :rows, 2 * WIDE :]
-    early_right = got[:, rows:, 2 * WIDE :]
-    w0 = weave(pick(early_left, early_right), swap_cores(pick(early_right, early_left)))
-
-    same = label[:, None] == label[None, :]
-    w0_open = jnp.where(same, jnp.concatenate([w0] * (chi // FOLD), axis=1), 0.0)
-    cot = jnp.transpose(jnp.sum(w0_open.reshape(chi // FOLD, FOLD, chi), axis=0))
-
-    packed = jax.ShapeDtypeStruct((chi, FOLD), BF16)
+
     back1 = call(
-        first_kernel, packed, [VMEM] * 6, [pltpu.VMEM((chi, WIDE), BF16)], "first_back", chi * chi * WIDE, 2 << 20
-    )(w0, enl, row_label_all, col, to_row, to_col)
+        first_kernel, array(chi, FOLD), [VMEM] * 6, [pltpu.VMEM((chi, WIDE), BF16)], chi * chi * WIDE, 2 << 20
+    )(w0, enl, row, col, to_row, to_col)
     back1_at = site_move(back1, -1, False)
-
-    near_part, back1_tie = lax.optimization_barrier((part_bf, back1))
-    new_part = jnp.dot(near, near_part, preferred_element_type=F32)
-    new_part = fold_lanes(jnp.where(same, new_part, 0.0), FOLD).astype(BF16)
+    back2 = call(
+        second_kernel, array(chi, FOLD), [VMEM] * 7, [pltpu.VMEM((WIDE, chi), BF16)], chi * chi * WIDE, 2 << 20
+    )(cot, back1_at, enl, row, col, to_row, to_col)
+    back2_at = site_move(back2, -1, False)
+    w2 = (cot + back2_at.astype(F32)).astype(BF16)
+    w2_other = swap_cores(w2)
+
+    new_part = call(new_kernel, array(chi, FOLD), [VMEM] * 4, [], chi * chi * chi, 3 << 20)(near, part_bf, row, col)
     new_got = exchange(new_part.reshape(chips, pair_rows, FOLD))
-
-    back2 = call(
-        second_kernel, packed, [VMEM] * 7, [pltpu.VMEM((WIDE, chi), BF16)], "second_back", chi * chi * WIDE, 2 << 20
-    )(cot, back1_at, enl, row_label_all, col, to_row, to_col)
-    w2 = (cot.astype(F32) + site_move(back2, -1, False).astype(F32)).astype(BF16)
-    w2_other = swap_cores(w2)
-
-    new_sum = jnp.sum(new_got.astype(F32), axis=0)
-    new_own = pick(new_sum[:rows], new_sum[rows:])
-    new_other = swap_cores(pick(new_sum[rows:], new_sum[:rows]))
-
-    def open_new(x):
-        return jnp.where(row_mask, jnp.concatenate([x] * (chi // FOLD), axis=1), 0.0).astype(BF16)
-
-    new_left = open_new(pick(new_own, new_other))
-    new_right = open_new(pick(new_other, new_own))
-
-    flat = jax.ShapeDtypeStruct((rows * depth, chi), BF16)
+    new_sum = call(total_kernel, array(pair_rows, FOLD, dtype=F32), [VMEM], [], 0, 1 << 18)(new_got)
+    new_other = swap_cores(new_sum)
+    new_left, new_right = call(
+        open_kernel, (array(rows, chi), array(rows, chi)), [VMEM] * 4, [], 0, 1 << 17, (VMEM, VMEM)
+    )(new_sum, new_other, own_label, row)
+
+    flat = array(rows * depth, chi)
     grad_left, grad_right = call(
         grad_kernel,
         (flat, flat),
@@ -260,11 +370,10 @@
             pltpu.VMEM((SLOTS, STEP, chi), BF16),
             pltpu.SemaphoreType.DMA((SLOTS,)),
         ],
-        "grads",
         4 * rows * depth * chi * chi,
         8 << 20,
         (ANY, ANY),
-    )(edge_flat, near, near_other, w2, w2_other, row_label_all, col)
+    )(edge_flat, near, near_other, w2, w2_other, row, col)
     return (
         new_left[None],
         new_right[None],
@@ -276,6 +385,7 @@
 def solution(mesh):
     row = P("site", "blk", None)
     flat = P("site", "blk", None, None)
+
     return jax.shard_map(
         body,
         mesh=mesh,

time: 156 us -> 173 us (1.11)
  blocking collectives: 0 us -> 44.2 us
  waiting for transfers between devices: 66.9 us -> 41.9 us
  other arithmetic: 14.8 us -> 5.75 us
  Pallas kernels: 13.8 us -> 20 us
  local copies, waits for them, and re-layouts: 10.8 us -> 15.3 us
  matrix products: 10.9 us -> 8.18 us
    all_to_all x0 -> x1, blocking collectives: none -> 44.2 us  [exchange(): return lax.all_to_all(x, 'blk', 0, 0, tiled=True, axis_index_groups=groups)]
    all_to_all x3 -> x2, waiting for transfers between devices: 35.7 us -> 3.67 us  [exchange(): return lax.all_to_all(x, 'blk', 0, 0, tiled=True, axis_index_groups=groups)]
    unnamed x43 -> x36, local copies, waits for them, and re-layouts: 5.48 us -> 11.9 us
    pallas_call x3 -> x9, Pallas kernels: 4.38 us -> 10.2 us  [the longest x1 2.63 us: body(): call(new_kernel, array(chi, FOLD), [VMEM] * 4, [], chi * chi * chi, 3 << 20)]
    ppermute x5, waiting for transfers between devices: 30.7 us -> 36.2 us  [site_move(): return lax.ppermute(x, ('site', 'blk'), route)]
    all_to_all x3 -> x2, starting transfers between devices: 20.5 us -> 15 us  [exchange(): return lax.all_to_all(x, 'blk', 0, 0, tiled=True, axis_index_groups=groups)]
    ppermute x5, starting transfers between devices: 8.67 us -> 13.5 us  [swap_cores(): return lax.ppermute(x, 'blk', [(i, i ^ 1) for i in range(members)])]
    convert_element_type x6 -> x2, other arithmetic: 5.66 us -> 2.26 us  [the longest x1 1.29 us: body(): other_part = swap_cores(pick(part_right, part_left).astype(BF16))]
  transfers between devices with their start and end apart: 13 -> 12, of which waited for: 8 -> 6; matrix products, arithmetic and copies ran while one was open for 9% -> 5% of each run, Pallas kernels for 2% -> 5%
where the time goes in v3:
time: 173 us; the launch traced here: 172 us
  blocking collectives  44.2 us (26%)
  waiting for transfers between devices  41.9 us (24%)
  starting transfers between devices  35.6 us (21%)
  Pallas kernels  20 us (12%)
  local copies, waits for them, and re-layouts  15.3 us (9%)
  matrix products  8.18 us (5%)
  other arithmetic  5.75 us (3%)
    all_to_all x1, blocking collectives, exchange(): return lax.all_to_all(x, 'blk', 0, 0, tiled=True, axis_index_groups=groups)  44.2 us
    ppermute x5, waiting for transfers between devices, site_move(): return lax.ppermute(x, ('site', 'blk'), route)  36.2 us
    all_to_all x2, starting transfers between devices, exchange(): return lax.all_to_all(x, 'blk', 0, 0, tiled=True, axis_index_groups=groups)  15 us
    ppermute x5, starting transfers between devices, swap_cores(): return lax.ppermute(x, 'blk', [(i, i ^ 1) for i in range(members)])  13.5 us
    unnamed x36, local copies, waits for them, and re-layouts  11.9 us
    pallas_call x1, Pallas kernels, body(): call(grad_kernel, (flat, flat), [VMEM] * 7, [pltpu.VMEM((FOLD, WIDE), BF1...  9.83 us
    dot_general x2, matrix products, contract_first(): lax.dot_general(left, right, (((0,), (0,)), ((), ())), preferred_element_...  8.18 us
    ppermute x5, starting transfers between devices, site_move(): return lax.ppermute(x, ('site', 'blk'), route)  6.99 us
  transfers between devices with their start and end apart: 12, of which 6 were waited for; matrix products, arithmetic and copies ran while one was open for 5% of the time, Pallas kernels for 5%

profile of v3, /device:TPU:1, one launch (start us, length us, event | category | flops | bytes accessed | tf_op | source)
XLA Modules:
  0.0 171.9 jit_solution(16911048583347397141)
XLA Ops:
  0.7 4.6 %fusion.3 = f32[768,768,1]{1,0,2:T(8,128)S(1)} fusion(bf16[1,24,64,768]{3,2,1,0:T(8,128)(2,1)} %param.9, bf16[1,24,64,768]{3,2,1,0:T(8,128)(2,1)} %param.8), kind=kOutput, calls=%fused_computation.5 | convolution fusion | flops 1811939328 | bytes 7077888 | tf_op jit(solution)/shard_map/dot_general | solution.py:19
  5.3 3.6 %bitcast_select_fusion.1 = (f32[768,768]{1,0:T(8,128)}, bf16[768,768,1]{1,0,2:T(8,128)(2,1)S(1)}) fusion(f32[768,768,1]{1,0,2:T(8,128)S(1)} %fusion.3, pred[]{:T(512)S(6)} %eq.18, bf16[1,24,64,768]{3,2,1,0:T(8,128)(2,1)S(1)} %copy-done, bf16[1,24,64,768]{3,2,1,0:T(8,128)(2,1)S(1)} %copy-done.2), kind=kOutput, calls=%fused_computation.1 | convolution fusion | flops 1813118976 | bytes 10616833 | tf_op jit(solution)/shard_map/dot_general | solution.py:19
  8.9 1.3 fusion
  10.2 3.2 %collective-permute-start = (bf16[768,768]{1,0:T(8,128)(2,1)}, bf16[768,768]{1,0:T(8,128)(2,1)S(1)}, u32[]{:S(2)}, u32[]{:S(2)}) collective-permute-start(bf16[768,768]{1,0:T(8,128)(2,1)} %fusion), channel_id=1, source_target_pairs={{0,1},{1,0},{2,3},{3,2},{4,5},{5,4},{6,7},{7,6},{8,9},{9,8},{10,11... | collective-permute-start | bytes 3538952 | tf_op jit(solution)/shard_map/ppermute | solution.py:272
  13.4 1.8 %collective-permute-start.1 = (s32[1,768]{1,0:T(1,128)S(1)}, s32[1,768]{1,0:T(1,128)}, u32[]{:S(2)}, u32[]{:S(2)}) collective-permute-start(s32[1,768]{1,0:T(1,128)S(1)} %copy-done.11), channel_id=1, source_target_pairs={{0,32},{1,225},{2,34},{3,227},{4,36},{5,229},{6,38},{7,231},{8,40}... | collective-permute-start | bytes 9224 | tf_op jit(solution)/shard_map/ppermute | solution.py:281
  17.1 1.3 reduce
  20.3 1.7 copy-done.4
  25.2 44.2 %all_to_all.15.got_ref = bf16[16,48,896]{2,1,0:T(8,128)(2,1)S(1)} all-to-all(bf16[16,48,896]{2,1,0:T(8,128)(2,1)S(1)} %get-tuple-element.15), channel_id=1, replica_groups={{0,2,4,6,8,10,12,14,16,18,20,22,24,26,28,30},{1,3,5,7,9,11,13,15,17,19,..., dimensions={0} | all-to-all | bytes 2752512 | tf_op jit(solution)/shard_map/all_to_all | solution.py:284
  71.2 5.9 %all-to-all-start.2 = ((bf16[16,48,384]{2,1,0:T(8,128)(2,1)}), bf16[16,48,384]{2,1,0:T(8,128)(2,1)S(1)}, u32[]{:S(2)}, u32[]{:S(2)}) async-start(bf16[16,48,384]{2,1,0:T(8,128)(2,1)} %copy-done.10), calls=%async_computation.2 | async-start | bytes 1179648 | tf_op jit(solution)/shard_map/all_to_all | solution.py:284
  77.1 2.7 %collective-permute-start.2 = (bf16[16,48,384]{2,1,0:T(8,128)(2,1)}, bf16[16,48,384]{2,1,0:T(8,128)(2,1)S(1)}, u32[]{:S(2)}, u32[]{:S(2)}) collective-permute-start(bf16[16,48,384]{2,1,0:T(8,128)(2,1)} %copy-done.17), channel_id=1, source_target_pairs={{0,32},{1,225},{2,34},{3,227},{4,36},{5,229},{6,38},{7,231},{8,40}... | collective-permute-start | bytes 1769480 | tf_op jit(solution)/shard_map/ppermute | solution.py:281
  79.8 28.5 %collective-permute-done.2.same_ref = bf16[16,48,384]{2,1,0:T(8,128)(2,1)S(1)} collective-permute-done((bf16[16,48,384]{2,1,0:T(8,128)(2,1)}, bf16[16,48,384]{2,1,0:T(8,128)(2,1)S(1)}, u32[]{:S(2)}, u32[]{:S(2)}) %collective-permute-start.2) | collective-permute-done | bytes 589856 | tf_op jit(solution)/shard_map/ppermute | solution.py:281
  108.3 2.1 %collective-permute-done.3.cross_ref = bf16[16,48,384]{2,1,0:T(8,128)(2,1)S(1)} collective-permute-done((bf16[16,48,384]{2,1,0:T(8,128)(2,1)}, bf16[16,48,384]{2,1,0:T(8,128)(2,1)S(1)}, u32[]{:S(2)}, u32[]{:S(2)}) %collective-permute-start.3) | collective-permute-done | bytes 589856 | tf_op jit(solution)/shard_map/ppermute | solution.py:281
  110.4 1.1 shard_map.104.near_ref
  112.2 1.6 copy.31.to_col_ref
  113.8 1.1 collective-permute-done.6.other_ref
  115.0 1.5 shard_map.108
  118.0 1.0 copy-done.1
  119.0 0.9 copy-done.13
  119.9 1.6 shard_map.109
  121.5 1.4 collective-permute-start.7
  122.9 5.6 %collective-permute-done.7.back_ref = bf16[768,128]{1,0:T(8,128)(2,1)S(1)} collective-permute-done((bf16[768,128]{1,0:T(8,128)(2,1)S(1)}, bf16[768,128]{1,0:T(8,128)(2,1)S(1)}, u32[]{:S(2)}, u32[]{:S(2)}) %collective-permute-start.7) | collective-permute-done | bytes 196640 | tf_op jit(solution)/shard_map/ppermute | solution.py:281
  128.5 1.0 copy-done.6
  129.5 1.7 shard_map.110
  131.2 1.1 collective-permute-start.8
  132.3 2.6 %shard_map.105 = bf16[768,128]{1,0:T(8,128)(2,1)} custom-call(bf16[768,768]{1,0:T(8,128)(2,1)} %shard_map.104.near_ref, bf16[768,768]{1,0:T(8,128)(2,1)S(1)} %copy-done.9, s32[1,768]{1,0:T(1,128)S(1)} %copy-done.11, s32[768,1]{1,0:T(8,128)S(1)} %copy.27.col_ref), custom_call_target="tpu_custom_call" | custom-call | flops 452984832 | bytes 3145728 | tf_op jit(solution)/shard_map/pallas_call | solution.py:354
  135.0 9.2 %all-to-all-start.1 = ((bf16[16,48,128]{2,1,0:T(8,128)(2,1)}), bf16[16,48,128]{2,1,0:T(8,128)(2,1)S(1)}, u32[]{:S(2)}, u32[]{:S(2)}) async-start(bf16[16,48,128]{2,1,0:T(8,128)(2,1)} %bitcast.10), calls=%async_computation.1 | async-start | bytes 393216 | tf_op jit(solution)/shard_map/all_to_all | solution.py:284
  144.1 1.0 add_convert_fusion.w_ref
  145.1 4.3 %collective-permute-start.9 = (bf16[768,128]{1,0:T(8,128)(2,1)S(1)}, bf16[768,128]{1,0:T(8,128)(2,1)S(1)}, u32[]{:S(2)}, u32[]{:S(2)}) collective-permute-start(bf16[768,128]{1,0:T(8,128)(2,1)S(1)} %add_convert_fusion.w_ref), channel_id=1, source_target_pairs={{0,1},{1,0},{2,3},{3,2},{4,5},{5,4},{6,7},{7,6},{8,9},{9,8},{10,11... | collective-permute-start | bytes 589832 | tf_op jit(solution)/shard_map/ppermute | solution.py:272
  149.5 3.7 %all-to-all-done.1.got_ref = bf16[16,48,128]{2,1,0:T(8,128)(2,1)S(1)} async-done(((bf16[16,48,128]{2,1,0:T(8,128)(2,1)}), bf16[16,48,128]{2,1,0:T(8,128)(2,1)S(1)}, u32[]{:S(2)}, u32[]{:S(2)}) %all-to-all-start.1) | async-done | bytes 196640 | tf_op jit(solution)/shard_map/all_to_all | solution.py:284
  153.2 5.5 %collective-permute-start.4 = (f32[48,128]{1,0:T(8,128)S(1)}, f32[48,128]{1,0:T(8,128)S(1)}, u32[]{:S(2)}, u32[]{:S(2)}) collective-permute-start(f32[48,128]{1,0:T(8,128)S(1)} %shard_map.106.own_ref), channel_id=1, source_target_pairs={{0,1},{1,0},{2,3},{3,2},{4,5},{5,4},{6,7},{7,6},{8,9},{9,8},{10,11... | collective-permute-start | bytes 73736 | tf_op jit(solution)/shard_map/ppermute | solution.py:272
  160.2 1.7 copy-done.3
  161.9 9.8 %shard_map.111 = (bf16[1536,768]{1,0:T(8,128)(2,1)}, bf16[1536,768]{1,0:T(8,128)(2,1)}) custom-call(bf16[1536,768]{1,0:T(8,128)(2,1)S(1)} %bitcast.39, bf16[768,768]{1,0:T(8,128)(2,1)} %shard_map.104.near_ref, bf16[768,768]{1,0:T(8,128)(2,1)} %collective-permute-done.5.near_other_ref, bf16[768,128]{1,0:T(8,128)(2,1)S(1)} %add_convert_fusion.w_ref, ...), custom_call_target="tpu_custom_call" | custom-call | flops 3623878656 | bytes 8388608 | tf_op jit(solution)/shard_map/pallas_call | solution.py:363
  (53 shorter events, 12.6 us)
Async XLA Ops:
  0.6 4.7 %copy-start = (bf16[1,24,64,768]{3,2,1,0:T(8,128)(2,1)S(1)}, bf16[1,24,64,768]{3,2,1,0:T(8,128)(2,1)}, u32[]{:S(2)}) copy-start(bf16[1,24,64,768]{3,2,1,0:T(8,128)(2,1)} %param.10) | copy-start | bytes 7077892
  0.7 4.6 %copy-start.2 = (bf16[1,24,64,768]{3,2,1,0:T(8,128)(2,1)S(1)}, bf16[1,24,64,768]{3,2,1,0:T(8,128)(2,1)}, u32[]{:S(2)}) copy-start(bf16[1,24,64,768]{3,2,1,0:T(8,128)(2,1)} %param.8) | copy-start | bytes 7077892
  8.9 4.5 %copy-start.11 = (s32[1,768]{1,0:T(1,128)S(1)}, s32[1,768]{1,0:T(1,128)}, u32[]{:S(2)}) copy-start(s32[1,768]{1,0:T(1,128)} %row_ref.13) | copy-start | bytes 9220
  10.2 10.1 %collective-permute-start = (bf16[768,768]{1,0:T(8,128)(2,1)}, bf16[768,768]{1,0:T(8,128)(2,1)S(1)}, u32[]{:S(2)}, u32[]{:S(2)}) collective-permute-start(bf16[768,768]{1,0:T(8,128)(2,1)} %fusion), channel_id=1, source_target_pairs={{0,1},{1,0},{2,3},{3,2},{4,5},{5,4},{6,7},{7,6},{8,9},{9,8},{10,11... | collective-permute-start | bytes 3538952 | tf_op jit(solution)/shard_map/ppermute | solution.py:272
  13.4 3.7 %collective-permute-start.1 = (s32[1,768]{1,0:T(1,128)S(1)}, s32[1,768]{1,0:T(1,128)}, u32[]{:S(2)}, u32[]{:S(2)}) collective-permute-start(s32[1,768]{1,0:T(1,128)S(1)} %copy-done.11), channel_id=1, source_target_pairs={{0,32},{1,225},{2,34},{3,227},{4,36},{5,229},{6,38},{7,231},{8,40}... | collective-permute-start | bytes 9224 | tf_op jit(solution)/shard_map/ppermute | solution.py:281
  20.3 1.7 copy-start.4
  22.0 0.9 copy-start.14
  22.9 0.9 copy-start.15
  23.8 0.8 copy-start.16
  25.2 44.3 %copy-start.8 = (bf16[768,768]{1,0:T(8,128)(2,1)}, bf16[768,768]{1,0:T(8,128)(2,1)S(1)}, u32[]{:S(2)}) copy-start(bf16[768,768]{1,0:T(8,128)(2,1)S(1)} %get-tuple-element.17.part_ref) | copy-start | bytes 3538948
  69.5 0.8 copy-start.10
  70.4 0.8 copy-start.17
  71.2 46.8 %all-to-all-start.2 = ((bf16[16,48,384]{2,1,0:T(8,128)(2,1)}), bf16[16,48,384]{2,1,0:T(8,128)(2,1)S(1)}, u32[]{:S(2)}, u32[]{:S(2)}) async-start(bf16[16,48,384]{2,1,0:T(8,128)(2,1)} %copy-done.10), calls=%async_computation.2 | async-start | bytes 1179648 | tf_op jit(solution)/shard_map/all_to_all | solution.py:284
  77.1 31.2 %collective-permute-start.2 = (bf16[16,48,384]{2,1,0:T(8,128)(2,1)}, bf16[16,48,384]{2,1,0:T(8,128)(2,1)S(1)}, u32[]{:S(2)}, u32[]{:S(2)}) collective-permute-start(bf16[16,48,384]{2,1,0:T(8,128)(2,1)} %copy-done.17), channel_id=1, source_target_pairs={{0,32},{1,225},{2,34},{3,227},{4,36},{5,229},{6,38},{7,231},{8,40}... | collective-permute-start | bytes 1769480 | tf_op jit(solution)/shard_map/ppermute | solution.py:281
  79.8 30.6 %collective-permute-start.3 = (bf16[16,48,384]{2,1,0:T(8,128)(2,1)}, bf16[16,48,384]{2,1,0:T(8,128)(2,1)S(1)}, u32[]{:S(2)}, u32[]{:S(2)}) collective-permute-start(bf16[16,48,384]{2,1,0:T(8,128)(2,1)} %copy-done.17), channel_id=1, source_target_pairs={{0,225},{1,32},{2,227},{3,34},{4,229},{5,36},{6,231},{7,38},{8,233... | collective-permute-start | bytes 1769480 | tf_op jit(solution)/shard_map/ppermute | solution.py:281
  111.5 48.7 %collective-permute-start.5 = (bf16[768,768]{1,0:T(8,128)(2,1)}, bf16[768,768]{1,0:T(8,128)(2,1)}, u32[]{:S(2)}, u32[]{:S(2)}) collective-permute-start(bf16[768,768]{1,0:T(8,128)(2,1)} %shard_map.104.near_ref), channel_id=1, source_target_pairs={{0,1},{1,0},{2,3},{3,2},{4,5},{5,4},{6,7},{7,6},{8,9},{9,8},{10,11... | collective-permute-start | bytes 3538952 | tf_op jit(solution)/shard_map/ppermute | solution.py:272
  111.5 3.5 %collective-permute-start.6 = (bf16[16,48,128]{2,1,0:T(8,128)(2,1)S(1)}, bf16[16,48,128]{2,1,0:T(8,128)(2,1)}, u32[]{:S(2)}, u32[]{:S(2)}) collective-permute-start(bf16[16,48,128]{2,1,0:T(8,128)(2,1)S(1)} %get-tuple-element.20.early_ref), channel_id=1, source_target_pairs={{0,1},{1,0},{2,3},{3,2},{4,5},{5,4},{6,7},{7,6},{8,9},{9,8},{10,11... | collective-permute-start | bytes 589832 | tf_op jit(solution)/shard_map/ppermute | solution.py:272
  116.5 0.8 copy-start.5
  117.3 0.7 copy-start.12
  118.0 1.0 copy-start.1
  119.0 0.9 copy-start.13
  119.9 12.4 %copy-start.9 = (bf16[768,768]{1,0:T(8,128)(2,1)S(1)}, bf16[768,768]{1,0:T(8,128)(2,1)}, u32[]{:S(2)}) copy-start(bf16[768,768]{1,0:T(8,128)(2,1)} %copy-done.8) | copy-start | bytes 3538948
  121.5 7.0 %collective-permute-start.7 = (bf16[768,128]{1,0:T(8,128)(2,1)S(1)}, bf16[768,128]{1,0:T(8,128)(2,1)S(1)}, u32[]{:S(2)}, u32[]{:S(2)}) collective-permute-start(bf16[768,128]{1,0:T(8,128)(2,1)S(1)} %shard_map.109), channel_id=1, source_target_pairs={{0,224},{1,33},{2,226},{3,35},{4,228},{5,37},{6,230},{7,39},{8,232... | collective-permute-start | bytes 589832 | tf_op jit(solution)/shard_map/ppermute | solution.py:281
  128.5 1.0 copy-start.6
  131.2 12.9 %copy-start.7 = (f32[768,128]{1,0:T(8,128)S(1)}, f32[768,128]{1,0:T(8,128)}, u32[]{:S(2)}) copy-start(f32[768,128]{1,0:T(8,128)} %copy-done.5) | copy-start | bytes 1179652
  131.2 12.9 %collective-permute-start.8 = (bf16[768,128]{1,0:T(8,128)(2,1)S(1)}, bf16[768,128]{1,0:T(8,128)(2,1)}, u32[]{:S(2)}, u32[]{:S(2)}) collective-permute-start(bf16[768,128]{1,0:T(8,128)(2,1)S(1)} %shard_map.110), channel_id=1, source_target_pairs={{0,224},{1,33},{2,226},{3,35},{4,228},{5,37},{6,230},{7,39},{8,232... | collective-permute-start | bytes 589832 | tf_op jit(solution)/shard_map/ppermute | solution.py:281
  135.0 18.2 %all-to-all-start.1 = ((bf16[16,48,128]{2,1,0:T(8,128)(2,1)}), bf16[16,48,128]{2,1,0:T(8,128)(2,1)S(1)}, u32[]{:S(2)}, u32[]{:S(2)}) async-start(bf16[16,48,128]{2,1,0:T(8,128)(2,1)} %bitcast.10), calls=%async_computation.1 | async-start | bytes 393216 | tf_op jit(solution)/shard_map/all_to_all | solution.py:284
  145.1 15.1 %collective-permute-start.9 = (bf16[768,128]{1,0:T(8,128)(2,1)S(1)}, bf16[768,128]{1,0:T(8,128)(2,1)S(1)}, u32[]{:S(2)}, u32[]{:S(2)}) collective-permute-start(bf16[768,128]{1,0:T(8,128)(2,1)S(1)} %add_convert_fusion.w_ref), channel_id=1, source_target_pairs={{0,1},{1,0},{2,3},{3,2},{4,5},{5,4},{6,7},{7,6},{8,9},{9,8},{10,11... | collective-permute-start | bytes 589832 | tf_op jit(solution)/shard_map/ppermute | solution.py:272
  153.2 6.3 %collective-permute-start.4 = (f32[48,128]{1,0:T(8,128)S(1)}, f32[48,128]{1,0:T(8,128)S(1)}, u32[]{:S(2)}, u32[]{:S(2)}) collective-permute-start(f32[48,128]{1,0:T(8,128)S(1)} %shard_map.106.own_ref), channel_id=1, source_target_pairs={{0,1},{1,0},{2,3},{3,2},{4,5},{5,4},{6,7},{7,6},{8,9},{9,8},{10,11... | collective-permute-start | bytes 73736 | tf_op jit(solution)/shard_map/ppermute | solution.py:272
  160.2 1.7 copy-start.3

commit v4 on v3

v4 whole, which is shorter than its diff:
```python
import jax
import jax.numpy as jnp
from jax import lax
from jax.experimental import pallas as pl
from jax.experimental.pallas import tpu as pltpu
from jax.sharding import PartitionSpec as P


SECTORS = 16
FOLD = 128
WIDE = 384
F32 = jnp.float32
BF16 = jnp.bfloat16
VMEM = pl.BlockSpec(memory_space=pltpu.VMEM)
ANY = pl.BlockSpec(memory_space=pl.ANY)
HBM = pl.BlockSpec(memory_space=pltpu.HBM)


def contract_first(left, right):
    return lax.dot_general(left, right, (((0,), (0,)), ((), ())), preferred_element_type=F32)


def contract_last(left, right):
    return lax.dot_general(left, right, (((1,), (1,)), ((), ())), preferred_element_type=F32)


def fold_lanes(x, width):
    pieces = [x[:, at : at + width] for at in range(0, x.shape[1], width)]
    total = pieces[0]
    for piece in pieces[1:]:
        total = total + piece
    return total


def near_tiles(i, tiles):
    return max(0, i - 1), min(tiles, i + 2)


def label_row(ref):
    return ref[...].astype(F32)


def column(row, i):
    return jnp.broadcast_to(row[:, FOLD * i : FOLD * (i + 1)], (FOLD, FOLD)).T


def lanes(q):
    return slice(FOLD * q, FOLD * (q + 1))


def pack_kernel(
    left_ref, right_ref, other_ref, row_ref, to_row_ref, cot_left_ref, cot_right_ref,
    out_ref, stage_ref, cot_ref, sems,
):
    chi = left_ref.shape[0]
    rows = cot_ref.shape[1]
    tiles = chi // FOLD
    wide = WIDE // FOLD
    blk = lax.axis_index("blk")
    copies = [
        pltpu.make_async_copy(ref, cot_ref.at[n], sems.at[n])
        for n, ref in enumerate((cot_left_ref, cot_right_ref))
    ]
    for copy in copies:
        copy.start()
    row, to_row = label_row(row_ref), label_row(to_row_ref)
    low, high = jnp.zeros_like(row), jnp.zeros_like(row)
    for n in range(SECTORS):
        member = to_row == float(n)
        least = jnp.min(jnp.where(member, row, float(SECTORS)), axis=1, keepdims=True)
        most = jnp.max(jnp.where(member, row, -1.0), axis=1, keepdims=True)
        low = low + jnp.where(member, least, 0.0)
        high = high + jnp.where(member, most, 0.0)

    def fold(own_ref):
        for i in range(tiles):
            at = lanes(i)
            low_col, high_col = column(low, i), column(high, i)
            totals = [None] * wide
            for q in range(tiles):
                part = own_ref[at, lanes(q)] + other_ref[at, lanes(q)].astype(F32)
                label = row[:, lanes(q)]
                part = jnp.where((label >= low_col) & (label <= high_col), part, 0.0)
                old = totals[q % wide]
                totals[q % wide] = part if old is None else old + part
            for q in range(wide):
                stage_ref[at, lanes(q)] = totals[q].astype(BF16)

    @pl.when(lax.rem(blk, 2) == 0)
    def _():
        fold(left_ref)

    @pl.when(lax.rem(blk, 2) == 1)
    def _():
        fold(right_ref)

    position = lax.broadcasted_iota(jnp.int32, (rows, chi), 1)
    wanted = blk * rows + lax.broadcasted_iota(jnp.int32, (rows, chi), 0)
    own = jnp.sum(jnp.where(position == wanted, row, 0.0), axis=1, keepdims=True)
    mask = own == row
    for n, copy in enumerate(copies):
        copy.wait()
        cot = fold_lanes(jnp.where(mask, cot_ref[n], 0.0), FOLD).astype(BF16)
        for q in range(chi // (2 * rows)):
            at = 2 * rows * q + rows * n
            stage_ref[at : at + rows, WIDE:] = cot
    copy = pltpu.make_async_copy(stage_ref, out_ref, sems.at[2])
    copy.start()
    copy.wait()


def sum_kernel(got_ref, out_ref, early_ref, held_ref, total_ref, sems):
    chips = got_ref.shape[0]
    part = chips // 4
    copies = [
        pltpu.make_async_copy(
            got_ref.at[pl.ds(part * n, part)], held_ref.at[pl.ds(part * n, part)], sems.at[n]
        )
        for n in range(4)
    ]
    for copy in copies:
        copy.start()
    total = jnp.zeros(total_ref.shape, F32)
    for n, copy in enumerate(copies):
        copy.wait()
        for q in range(part * n, part * (n + 1)):
            total = total + held_ref[q, :, :WIDE].astype(F32)
    total_ref[...] = total.astype(BF16)
    for q in range(chips):
        pltpu.make_async_copy(total_ref, out_ref.at[q], sems.at[q]).start()
    early_ref[...] = held_ref[:, :, WIDE:]
    for q in range(chips):
        pltpu.make_async_copy(total_ref, out_ref.at[q], sems.at[q]).wait()


def start_kernel(early_ref, other_ref, row_ref, open_ref, cot_ref, w_ref):
    chips, pair_rows, _ = early_ref.shape
    rows = pair_rows // 2
    core = lax.rem(lax.axis_index("blk"), 2)

    @pl.when(core == 0)
    def _():
        for q in range(chips):
            w_ref[pair_rows * q : pair_rows * q + rows, :] = early_ref[q, :rows, :]
            w_ref[pair_rows * q + rows : pair_rows * (q + 1), :] = other_ref[q, :rows, :]

    @pl.when(core == 1)
    def _():
        for q in range(chips):
            w_ref[pair_rows * q : pair_rows * q + rows, :] = other_ref[q, rows:, :]
            w_ref[pair_rows * q + rows : pair_rows * (q + 1), :] = early_ref[q, rows:, :]

    row = label_row(row_ref)
    tiles = w_ref.shape[0] // FOLD
    wide = WIDE // FOLD
    cols = [column(row, i) for i in range(tiles)]
    for i in range(tiles):
        low, high = near_tiles(i, tiles)
        total = jnp.zeros((FOLD, FOLD), F32)
        for q in range(low, high):
            total = total + jnp.where(cols[q] == row[:, lanes(i)], w_ref[lanes(q), :].astype(F32), 0.0)
        cot_ref[lanes(i), :] = total.T.astype(BF16)
        w = w_ref[lanes(i), :].astype(F32)
        for q in range(wide):
            same = (cols[i] == row[:, lanes(q)]) | (cols[i] == row[:, lanes(wide + q)])
            open_ref[lanes(i), lanes(q)] = jnp.where(same, w, 0.0).astype(BF16)


def weave_kernel(*refs):
    *piece_refs, out_ref, sems = refs
    ring = len(piece_refs)
    block = piece_refs[0].shape[0] // 2
    chip = lax.div(lax.axis_index("blk"), 2)
    y, z = lax.div(chip, ring), lax.rem(chip, ring)
    copies = []
    for n, ref in enumerate(piece_refs):
        step = -((n + 1) // 2) if n % 2 else n // 2
        for half in range(2):
            source = lax.rem(y + half, 2) * ring + lax.rem(z + step + ring, ring)
            at = pl.multiple_of(source * block, 16)
            copies.append(
                pltpu.make_async_copy(
                    ref.at[pl.ds(block * half, block)], out_ref.at[pl.ds(at, block)], sems.at[2 * n + half]
                )
            )
    for copy in copies:
        copy.start()
    for copy in copies:
        copy.wait()


def fold_tile(product, col, row, low, high):
    total = jnp.zeros((FOLD, FOLD), F32)
    for q in range(low, high):
        total = total + jnp.where(col == row[:, lanes(q)], product[:, lanes(q - low)], 0.0)
    return total.astype(BF16)


def new_kernel(near_ref, part_ref, row_ref, out_ref):
    tiles = near_ref.shape[0] // FOLD
    row = label_row(row_ref)
    for i in range(tiles):
        low, high = near_tiles(i, tiles)
        product = jnp.dot(
            near_ref[lanes(i), :], part_ref[:, FOLD * low : FOLD * high], preferred_element_type=F32
        )
        out_ref[lanes(i), :] = fold_tile(product, column(row, i), row, low, high)


def total_kernel(got_ref, out_ref):
    total = got_ref[0].astype(F32)
    for q in range(1, got_ref.shape[0]):
        total = total + got_ref[q].astype(F32)
    out_ref[...] = total


def open_kernel(own_ref, other_ref, row_ref, left_ref, right_ref):
    rows, chi = left_ref.shape
    blk = lax.axis_index("blk")
    core = lax.rem(blk, 2)
    row = label_row(row_ref)
    position = lax.broadcasted_iota(jnp.int32, (rows, chi), 1)
    wanted = blk * rows + lax.broadcasted_iota(jnp.int32, (rows, chi), 0)
    mask = jnp.sum(jnp.where(position == wanted, row, 0.0), axis=1, keepdims=True) == row

    def put(out_ref, x):
        wide = jnp.concatenate([x] * (chi // FOLD), axis=1)
        out_ref[...] = jnp.where(mask, wide, 0.0).astype(BF16)

    @pl.when(core == 0)
    def _():
        put(left_ref, own_ref[:rows, :])
        put(right_ref, other_ref[:rows, :])

    @pl.when(core == 1)
    def _():
        put(right_ref, own_ref[rows:, :])
        put(left_ref, other_ref[rows:, :])


def first_kernel(open_ref, enl_ref, to_row_ref, out_ref):
    to_row = label_row(to_row_ref)
    tiles = out_ref.shape[0] // FOLD
    for i in range(tiles):
        low, high = near_tiles(i, tiles)
        back = contract_last(enl_ref[lanes(i), :], open_ref[FOLD * low : FOLD * high, :])
        out_ref[lanes(i), :] = fold_tile(back, column(to_row, i), to_row, low, high)


def second_kernel(cot_ref, back_ref, enl_ref, row_ref, to_row_ref, out_ref, open_ref):
    row, to_row = label_row(row_ref), label_row(to_row_ref)
    tiles = out_ref.shape[0] // FOLD
    wide = WIDE // FOLD
    for i in range(wide):
        halves = []
        for at in (lanes(i), lanes(wide + i)):
            w = (cot_ref[at, :].astype(F32) + back_ref[at, :].astype(F32)).astype(BF16)
            halves.append(w.astype(F32))
        cols = column(row, i), column(row, wide + i)
        for q in range(tiles):
            total = jnp.where(cols[0] == row[:, lanes(q)], halves[0], 0.0)
            total = total + jnp.where(cols[1] == row[:, lanes(q)], halves[1], 0.0)
            open_ref[lanes(i), lanes(q)] = total.astype(BF16)
    for i in range(tiles):
        low, high = near_tiles(i, tiles)
        back = jnp.dot(
            enl_ref[lanes(i), :], open_ref[:, FOLD * low : FOLD * high], preferred_element_type=F32
        )
        out_ref[lanes(i), :] = fold_tile(back, column(to_row, i), to_row, low, high)


SLOTS = 4
STEP = 256


def grad_kernel(
    edge_hbm, near_hbm, other_hbm, w_ref, w_other_ref, row_ref, left_ref, right_ref,
    edge_ref, near_ref, open_ref, mid_ref, stage_ref, in_sems, sems,
):
    core = lax.rem(lax.axis_index("blk"), 2)
    chi = near_ref.shape[1]
    tiles = chi // FOLD
    steps = edge_ref.shape[0] // STEP
    row = label_row(row_ref)
    near_copies = [
        pltpu.make_async_copy(ref, near_ref.at[n], in_sems.at[steps + n])
        for n, ref in enumerate((near_hbm, other_hbm))
    ]
    edge_copies = [
        pltpu.make_async_copy(
            edge_hbm.at[pl.ds(STEP * n, STEP)], edge_ref.at[pl.ds(STEP * n, STEP)], in_sems.at[n]
        )
        for n in range(steps)
    ]
    near_copies[0].start()
    for copy in edge_copies:
        copy.start()
    near_copies[1].start()
    for side, w in enumerate((w_ref, w_other_ref)):
        near_copies[side].wait()
        for i in range(tiles):
            low, high = near_tiles(i, tiles)
            col = column(row, i)
            x = w[lanes(i), :].astype(F32)
            for q in range(low, high):
                open_ref[:, lanes(q - low)] = jnp.where(col == row[:, lanes(q)], x, 0.0).astype(BF16)
            mid = jnp.dot(
                open_ref[:, : FOLD * (high - low)],
                near_ref[side, FOLD * low : FOLD * high, :],
                preferred_element_type=F32,
            )
            mid_ref[:, lanes(i)] = mid.T.astype(BF16)
        for n in range(steps):
            at = side * steps + n
            slot = at % SLOTS
            rows = pl.ds(STEP * n, STEP)
            if side == 0:
                edge_copies[n].wait()
            if at >= SLOTS:
                pltpu.make_async_copy(stage_ref.at[slot], left_ref.at[rows], sems.at[slot]).wait()
            stage_ref[slot] = jnp.dot(
                edge_ref[STEP * n : STEP * (n + 1), :], mid_ref[...], preferred_element_type=F32
            ).astype(BF16)

            @pl.when(core == side)
            def _():
                pltpu.make_async_copy(stage_ref.at[slot], left_ref.at[rows], sems.at[slot]).start()

            @pl.when(core != side)
            def _():
                pltpu.make_async_copy(stage_ref.at[slot], right_ref.at[rows], sems.at[slot]).start()

    for slot in range(SLOTS):
        pltpu.make_async_copy(stage_ref.at[slot], left_ref.at[pl.ds(0, STEP)], sems.at[slot]).wait()


def call(kernel, out_shape, in_specs, scratch, flops, moved, out_specs=VMEM, limit=24 << 20):
    return pl.pallas_call(
        kernel,
        out_shape=out_shape,
        in_specs=in_specs,
        out_specs=out_specs,
        scratch_shapes=scratch,
        cost_estimate=pl.CostEstimate(flops=flops, bytes_accessed=moved, transcendentals=0),
        compiler_params=pltpu.CompilerParams(vmem_limit_bytes=limit),
    )


def body(corner, edge, proj_left, proj_right, charge, cot_left, cot_right):
    sites = lax.axis_size("site")
    members = lax.axis_size("blk")
    rows, chi = corner.shape[1], corner.shape[2]
    depth = edge.shape[2]
    chips = members // 2
    pair_rows = 2 * rows
    blk = lax.axis_index("blk")
    first = blk % 2 == 0
    groups = [[2 * q + core for q in range(chips)] for core in range(2)]

    def swap_cores(x):
        return lax.ppermute(x, "blk", [(i, i ^ 1) for i in range(members)])

    def site_move(x, distance, cross):
        route = []
        for s in range(sites):
            for i in range(members):
                target = i ^ 1 if cross else i
                sign = 1 if target % 2 == 0 else -1
                route.append((s * members + i, ((s + sign * distance) % sites) * members + target))
        return lax.ppermute(x, ("site", "blk"), route)

    def exchange(x):
        return lax.all_to_all(x, "blk", 0, 0, tiled=True, axis_index_groups=groups)

    def pick(a, b):
        return jnp.where(first, a, b)

    row = charge
    scale = jnp.broadcast_to(charge.astype(BF16), (8, chi))
    other_corner = swap_cores(corner[0])
    pair_corner = [pick(corner[0], other_corner), pick(other_corner, corner[0])]
    near = site_move(jnp.concatenate(pair_corner + [scale], axis=0), 1, False)
    to_row = near[pair_rows : pair_rows + 1].astype(jnp.int32)
    near = near[:pair_rows]

    def array(*shape, dtype=BF16):
        return jax.ShapeDtypeStruct(shape, dtype)

    edge_flat = edge[0].reshape(rows * depth, chi)
    part_left = contract_first(edge_flat, proj_left[0].reshape(rows * depth, chi))
    part_right = contract_first(edge_flat, proj_right[0].reshape(rows * depth, chi))
    other_part = swap_cores(pick(part_right, part_left).astype(BF16))
    part_bf = (pick(part_left, part_right) + other_part.astype(F32)).astype(BF16)
    packed = call(
        pack_kernel,
        array(chi, WIDE + FOLD),
        [VMEM] * 5 + [ANY] * 2,
        [pltpu.VMEM((chi, WIDE + FOLD), BF16), pltpu.VMEM((2, rows, chi), F32), pltpu.SemaphoreType.DMA((3,))],
        chi * chi * 8,
        6 << 20,
        HBM,
    )(part_left, part_right, other_part, row, to_row, cot_left[0], cot_right[0])
    got = exchange(packed.reshape(chips, pair_rows, WIDE + FOLD))
    summed, early = call(
        sum_kernel,
        (array(chips, pair_rows, WIDE), array(chips, pair_rows, FOLD)),
        [HBM],
        [
            pltpu.VMEM((chips, pair_rows, WIDE + FOLD), BF16),
            pltpu.VMEM((pair_rows, WIDE), BF16),
            pltpu.SemaphoreType.DMA((chips,)),
        ],
        0,
        3 << 20,
        (HBM, VMEM),
        63 << 20,
    )(got)
    enl = exchange(summed).reshape(chi, WIDE)

    rings = 2
    ring = chips // rings

    def turn(i, dy, dz):
        y, z, core = i // (2 * ring), i // 2 % ring, i % 2
        return (((y + dy) % rings) * ring + (z + dz) % ring) * 2 + core

    def ring_move(x, dy, dz):
        return lax.ppermute(x, "blk", [(i, turn(i, dy, dz)) for i in range(members)])

    near = jnp.concatenate([near, ring_move(near, 1, 0)], axis=0)
    up = down = near
    pieces = [near]
    for n in range(1, ring // 2 + 1):
        up = ring_move(up, 0, 1)
        pieces.append(up)
        if n < ring // 2:
            down = ring_move(down, 0, -1)
            pieces.append(down)
    near = call(weave_kernel, array(chi, chi), [ANY] * ring, [pltpu.SemaphoreType.DMA((chips,))], 0, 3 << 20, VMEM, 60 << 20)(*pieces)
    near_other = swap_cores(near)

    early_other = swap_cores(early)
    w_open, cot = call(
        start_kernel,
        (array(chi, WIDE), array(chi, FOLD)),
        [VMEM] * 3,
        [pltpu.VMEM((chi, FOLD), BF16)],
        0,
        1 << 20,
        (VMEM, VMEM),
    )(early, early_other, row)
    back1 = call(first_kernel, array(chi, FOLD), [VMEM] * 3, [], chi * chi * WIDE, 2 << 20)(w_open, enl, to_row)
    back1_at = site_move(back1, -1, False)
    back2 = call(
        second_kernel, array(chi, FOLD), [VMEM] * 5, [pltpu.VMEM((WIDE, chi), BF16)], chi * chi * WIDE, 2 << 20
    )(cot, back1_at, enl, row, to_row)
    back2_at = site_move(back2, -1, False)
    w2 = (cot.astype(F32) + back2_at.astype(F32)).astype(BF16)
    w2_other = swap_cores(w2)

    new_part = call(new_kernel, array(chi, FOLD), [VMEM] * 3, [], chi * chi * chi, 3 << 20)(near, part_bf, row)
    new_got = exchange(new_part.reshape(chips, pair_rows, FOLD))
    new_sum = call(total_kernel, array(pair_rows, FOLD, dtype=F32), [VMEM], [], 0, 1 << 18)(new_got)
    new_other = swap_cores(new_sum)
    new_left, new_right = call(
        open_kernel, (array(rows, chi), array(rows, chi)), [VMEM] * 3, [], 0, 1 << 17, (VMEM, VMEM)
    )(new_sum, new_other, row)

    flat = array(rows * depth, chi)
    grad_left, grad_right = call(
        grad_kernel,
        (flat, flat),
        [HBM] * 3 + [VMEM] * 3,
        [
            pltpu.VMEM((rows * depth, chi), BF16),
            pltpu.VMEM((2, chi, chi), BF16),
            pltpu.VMEM((FOLD, WIDE), BF16),
            pltpu.VMEM((chi, chi), BF16),
            pltpu.VMEM((SLOTS, STEP, chi), BF16),
            pltpu.SemaphoreType.DMA((rows * depth // STEP + 2,)),
            pltpu.SemaphoreType.DMA((SLOTS,)),
        ],
        4 * rows * depth * chi * chi,
        8 << 20,
        (HBM, HBM),
        62 << 20,
    )(edge_flat, near, near_other, w2, w2_other, row)
    return (
        new_left[None],
        new_right[None],
        grad_left.reshape(1, rows, depth, chi),
        grad_right.reshape(1, rows, depth, chi),
    )


def solution(mesh):
    row = P("site", "blk", None)
    flat = P("site", "blk", None, None)

    return jax.shard_map(
        body,
        mesh=mesh,
        in_specs=(row, flat, flat, flat, P("site", None), row, row),
        out_specs=(row, row, flat, flat),
        check_vma=False,
    )
```

time: 173 us -> 153 us (0.88)
  starting transfers between devices: 35.6 us -> 53.6 us
  blocking collectives: 44.2 us -> 29.6 us
  local copies, waits for them, and re-layouts: 15.3 us -> 3.48 us
  waiting for transfers between devices: 41.9 us -> 33.8 us
  other arithmetic: 5.75 us -> 1.86 us
  Pallas kernels: 20 us -> 22.5 us
    ppermute x5 -> x3, waiting for transfers between devices: 36.2 us -> 9 us  [site_move(): return lax.ppermute(x, ('site', 'blk'), route)]
    ppermute x0 -> x8, waiting for transfers between devices: none -> 17.9 us  [ring_move(): lax.ppermute(x, 'blk', [(i, turn(i, dy, dz)) for i in range(members)])]
    all_to_all x1, blocking collectives: 44.2 us -> 29.6 us  [exchange(): return lax.all_to_all(x, 'blk', 0, 0, tiled=True, axis_index_groups=groups)]
    ppermute x5 -> x6, starting transfers between devices: 13.5 us -> 24.9 us  [swap_cores(): return lax.ppermute(x, 'blk', [(i, i ^ 1) for i in range(members)])]
    ppermute x0 -> x8, starting transfers between devices: none -> 11 us  [ring_move(): lax.ppermute(x, 'blk', [(i, turn(i, dy, dz)) for i in range(members)])]
    unnamed x36 -> x48, local copies, waits for them, and re-layouts: 11.9 us -> 3.46 us
    ppermute x5 -> x3, starting transfers between devices: 6.99 us -> 2.38 us  [site_move(): return lax.ppermute(x, ('site', 'blk'), route)]
    pallas_call x1, Pallas kernels: 0.15 us -> 2.9 us  [body(): call(sum_kernel, (array(chips, pair_rows, WIDE), array(chips, pair_rows,...]
  transfers between devices with their start and end apart: 12 -> 19, of which waited for: 6 -> 10; matrix products, arithmetic and copies ran while one was open for 5% -> 1% of each run, Pallas kernels for 5% -> 4%
where the time goes in v4:
time: 153 us
  starting transfers between devices  53.6 us (35%)
  waiting for transfers between devices  33.8 us (22%)
  blocking collectives  29.6 us (19%)
  Pallas kernels  22.5 us (15%)
  matrix products  6.67 us (4%)
  local copies, waits for them, and re-layouts  3.48 us (2%)
  other arithmetic  1.86 us (1%)
    all_to_all x1, blocking collectives, exchange(): return lax.all_to_all(x, 'blk', 0, 0, tiled=True, axis_index_groups=groups)  29.6 us
    ppermute x6, starting transfers between devices, swap_cores(): return lax.ppermute(x, 'blk', [(i, i ^ 1) for i in range(members)])  24.9 us
    ppermute x8, waiting for transfers between devices, ring_move(): lax.ppermute(x, 'blk', [(i, turn(i, dy, dz)) for i in range(members)])  17.9 us
    all_to_all x2, starting transfers between devices, exchange(): return lax.all_to_all(x, 'blk', 0, 0, tiled=True, axis_index_groups=groups)  15.3 us
    pallas_call x1, Pallas kernels, body(): call(grad_kernel, (flat, flat), [HBM] * 3 + [VMEM] * 3, [pltpu.VMEM((rows...  11.6 us
    ppermute x8, starting transfers between devices, ring_move(): lax.ppermute(x, 'blk', [(i, turn(i, dy, dz)) for i in range(members)])  11 us
    ppermute x3, waiting for transfers between devices, site_move(): return lax.ppermute(x, ('site', 'blk'), route)  9 us
    dot_general x2, matrix products, contract_first(): lax.dot_general(left, right, (((0,), (0,)), ((), ())), preferred_element_...  6.67 us
  transfers between devices with their start and end apart: 19, of which 10 were waited for; matrix products, arithmetic and copies ran while one was open for 1% of the time, Pallas kernels for 4%

profile of v4, /device:TPU:1, one launch (start us, length us, event | category | flops | bytes accessed | tf_op | source)
XLA Modules:
  0.0 152.7 jit_solution(7930647093026668845)
XLA Ops:
  0.7 4.6 %fusion.6.left_ref = f32[768,768]{1,0:T(8,128)S(1)} fusion(bf16[1,24,64,768]{3,2,1,0:T(8,128)(2,1)} %param.9, bf16[1,24,64,768]{3,2,1,0:T(8,128)(2,1)} %param.8), kind=kOutput, calls=%fused_computation.8 | convolution fusion | flops 1811939328 | bytes 7077888 | tf_op jit(solution)/shard_map/dot_general | solution.py:20
  5.3 2.1 %select_convert_fusion = (bf16[768,768]{1,0:T(8,128)(2,1)S(1)}, f32[768,768]{1,0:T(8,128)S(1)}) fusion(f32[768,768]{1,0:T(8,128)S(1)} %fusion.6.left_ref, pred[]{:T(512)S(6)} %eq.5, bf16[1,24,64,768]{3,2,1,0:T(8,128)(2,1)S(1)} %copy-done.22, bf16[1,24,64,768]{3,2,1,0:T(8,128)(2,1)S(1)} %copy-done.12), kind=kOutput, calls=%fused_computation.7 | convolution fusion | flops 1812529152 | bytes 10616833 | tf_op jit(solution)/shard_map/dot_general | solution.py:20
  7.4 3.3 %collective-permute-start.10 = (bf16[768,768]{1,0:T(8,128)(2,1)S(1)}, bf16[768,768]{1,0:T(8,128)(2,1)S(1)}, u32[]{:S(2)}, u32[]{:S(2)}) collective-permute-start(bf16[768,768]{1,0:T(8,128)(2,1)S(1)} %get-tuple-element.22), channel_id=1, source_target_pairs={{0,1},{1,0},{2,3},{3,2},{4,5},{5,4},{6,7},{7,6},{8,9},{9,8},{10,11... | collective-permute-start | bytes 3538952 | tf_op jit(solution)/shard_map/ppermute | solution.py:361
  10.9 2.4 %collective-permute-done = bf16[24,768]{1,0:T(8,128)(2,1)S(1)} collective-permute-done((bf16[24,768]{1,0:T(8,128)(2,1)S(1)}, bf16[24,768]{1,0:T(8,128)(2,1)S(1)}, u32[]{:S(2)}, u32[]{:S(2)}) %collective-permute-start) | collective-permute-done | bytes 36896 | tf_op jit(solution)/shard_map/ppermute | solution.py:361
  13.3 1.9 %collective-permute-start.1 = (bf16[56,768]{1,0:T(8,128)(2,1)S(1)}, bf16[56,768]{1,0:T(8,128)(2,1)S(1)}, u32[]{:S(2)}, u32[]{:S(2)}) collective-permute-start(bf16[56,768]{1,0:T(8,128)(2,1)S(1)} %pad_maximum_fusion.1), channel_id=1, source_target_pairs={{0,32},{1,225},{2,34},{3,227},{4,36},{5,229},{6,38},{7,231},{8,40}... | collective-permute-start | bytes 258056 | tf_op jit(solution)/shard_map/ppermute | solution.py:370
  15.2 1.6 %collective-permute-done.1 = bf16[56,768]{1,0:T(8,128)(2,1)S(1)} collective-permute-done((bf16[56,768]{1,0:T(8,128)(2,1)S(1)}, bf16[56,768]{1,0:T(8,128)(2,1)S(1)}, u32[]{:S(2)}, u32[]{:S(2)}) %collective-permute-start.1) | collective-permute-done | bytes 86048 | tf_op jit(solution)/shard_map/ppermute | solution.py:370
  16.8 1.2 shard_map.106
  18.0 29.6 %all_to_all.15.got_ref = bf16[16,48,512]{2,1,0:T(8,128)(2,1)} all-to-all(bf16[16,48,512]{2,1,0:T(8,128)(2,1)S(1)} %bitcast.42), channel_id=1, replica_groups={{0,2,4,6,8,10,12,14,16,18,20,22,24,26,28,30},{1,3,5,7,9,11,13,15,17,19,..., dimensions={0} | all-to-all | bytes 1572864 | tf_op jit(solution)/shard_map/all_to_all | solution.py:373
  47.6 2.9 %shard_map.107 = (bf16[16,48,384]{2,1,0:T(8,128)(2,1)}, bf16[16,48,128]{2,1,0:T(8,128)(2,1)}) custom-call(bf16[16,48,512]{2,1,0:T(8,128)(2,1)} %all_to_all.15.got_ref), custom_call_target="tpu_custom_call" | custom-call | bytes 3145728 | tf_op jit(solution)/shard_map/pallas_call | solution.py:404
  50.5 7.3 %all-to-all-start.2 = ((bf16[16,48,384]{2,1,0:T(8,128)(2,1)}), bf16[16,48,384]{2,1,0:T(8,128)(2,1)S(1)}, u32[]{:S(2)}, u32[]{:S(2)}) async-start(bf16[16,48,384]{2,1,0:T(8,128)(2,1)} %get-tuple-element.17), calls=%async_computation.2 | async-start | bytes 1179648 | tf_op jit(solution)/shard_map/all_to_all | solution.py:373
  57.8 3.0 %collective-permute-start.2 = (bf16[48,768]{1,0:T(8,128)(2,1)S(1)}, bf16[48,768]{1,0:T(8,128)(2,1)S(1)}, u32[]{:S(2)}, u32[]{:S(2)}) collective-permute-start(bf16[48,768]{1,0:T(8,128)(2,1)S(1)} %slice.8), channel_id=1, source_target_pairs={{0,16},{1,17},{2,18},{3,19},{4,20},{5,21},{6,22},{7,23},{8,24},{9,... | collective-permute-start | bytes 221192 | tf_op jit(solution)/shard_map/ppermute | solution.py:428
  60.7 2.2 %collective-permute-done.2 = bf16[48,768]{1,0:T(8,128)(2,1)S(1)} collective-permute-done((bf16[48,768]{1,0:T(8,128)(2,1)S(1)}, bf16[48,768]{1,0:T(8,128)(2,1)S(1)}, u32[]{:S(2)}, u32[]{:S(2)}) %collective-permute-start.2) | collective-permute-done | bytes 73760 | tf_op jit(solution)/shard_map/ppermute | solution.py:428
  63.0 1.3 collective-permute-start.3
  64.3 1.5 collective-permute-start.4
  65.8 10.3 %collective-permute-done.3.refs_1_ = bf16[96,768]{1,0:T(8,128)(2,1)S(1)} collective-permute-done((bf16[96,768]{1,0:T(8,128)(2,1)S(1)}, bf16[96,768]{1,0:T(8,128)(2,1)S(1)}, u32[]{:S(2)}, u32[]{:S(2)}) %collective-permute-start.3) | collective-permute-done | bytes 147488 | tf_op jit(solution)/shard_map/ppermute | solution.py:428
  76.1 2.7 %collective-permute-start.6 = (bf16[96,768]{1,0:T(8,128)(2,1)S(1)}, bf16[96,768]{1,0:T(8,128)(2,1)S(1)}, u32[]{:S(2)}, u32[]{:S(2)}) collective-permute-start(bf16[96,768]{1,0:T(8,128)(2,1)S(1)} %collective-permute-done.4.refs_2_), channel_id=1, source_target_pairs={{0,14},{1,15},{2,0},{3,1},{4,2},{5,3},{6,4},{7,5},{8,6},{9,7},{10,... | collective-permute-start | bytes 442376 | tf_op jit(solution)/shard_map/ppermute | solution.py:428
  78.8 2.5 %collective-permute-done.5.refs_3_ = bf16[96,768]{1,0:T(8,128)(2,1)S(1)} collective-permute-done((bf16[96,768]{1,0:T(8,128)(2,1)S(1)}, bf16[96,768]{1,0:T(8,128)(2,1)S(1)}, u32[]{:S(2)}, u32[]{:S(2)}) %collective-permute-start.5) | collective-permute-done | bytes 147488 | tf_op jit(solution)/shard_map/ppermute | solution.py:428
  81.3 2.7 %collective-permute-start.8 = (bf16[96,768]{1,0:T(8,128)(2,1)S(1)}, bf16[96,768]{1,0:T(8,128)(2,1)S(1)}, u32[]{:S(2)}, u32[]{:S(2)}) collective-permute-start(bf16[96,768]{1,0:T(8,128)(2,1)S(1)} %collective-permute-done.6.refs_4_), channel_id=1, source_target_pairs={{0,14},{1,15},{2,0},{3,1},{4,2},{5,3},{6,4},{7,5},{8,6},{9,7},{10,... | collective-permute-start | bytes 442376 | tf_op jit(solution)/shard_map/ppermute | solution.py:428
  84.0 2.5 %collective-permute-done.7.refs_5_ = bf16[96,768]{1,0:T(8,128)(2,1)S(1)} collective-permute-done((bf16[96,768]{1,0:T(8,128)(2,1)S(1)}, bf16[96,768]{1,0:T(8,128)(2,1)S(1)}, u32[]{:S(2)}, u32[]{:S(2)}) %collective-permute-start.7) | collective-permute-done | bytes 147488 | tf_op jit(solution)/shard_map/ppermute | solution.py:428
  86.5 4.3 %collective-permute-start.13 = (bf16[16,48,128]{2,1,0:T(8,128)(2,1)}, bf16[16,48,128]{2,1,0:T(8,128)(2,1)S(1)}, u32[]{:S(2)}, u32[]{:S(2)}) collective-permute-start(bf16[16,48,128]{2,1,0:T(8,128)(2,1)} %get-tuple-element.14.early_ref), channel_id=1, source_target_pairs={{0,1},{1,0},{2,3},{3,2},{4,5},{5,4},{6,7},{7,6},{8,9},{9,8},{10,11... | collective-permute-start | bytes 589832 | tf_op jit(solution)/shard_map/ppermute | solution.py:361
  91.8 2.5 %shard_map.102.near_ref.near_hbm = bf16[768,768]{1,0:T(8,128)(2,1)} custom-call(bf16[96,768]{1,0:T(8,128)(2,1)} %copy-done.13, bf16[96,768]{1,0:T(8,128)(2,1)} %copy-done.15, bf16[96,768]{1,0:T(8,128)(2,1)} %copy-done.16, bf16[96,768]{1,0:T(8,128)(2,1)} %copy-done.17, bf16[96,768]{1,0:T(8,128)(2,1)} %copy-done.18, bf16[96,768]{1,0:T(8,128)(2,1)} %copy-done.19, ...), custom_call_target="tpu_custom_call" | custom-call | bytes 3145728 | tf_op jit(solution)/shard_map/pallas_call | solution.py:439
  94.4 5.4 %collective-permute-start.12 = (bf16[768,768]{1,0:T(8,128)(2,1)}, bf16[768,768]{1,0:T(8,128)(2,1)}, u32[]{:S(2)}, u32[]{:S(2)}) collective-permute-start(bf16[768,768]{1,0:T(8,128)(2,1)} %shard_map.102.near_ref.near_hbm), channel_id=1, source_target_pairs={{0,1},{1,0},{2,3},{3,2},{4,5},{5,4},{6,7},{7,6},{8,9},{9,8},{10,11... | collective-permute-start | bytes 3538952 | tf_op jit(solution)/shard_map/ppermute | solution.py:361
  101.0 1.2 copy-done.7
  103.4 7.5 %collective-permute-done.14.back_ref = bf16[768,128]{1,0:T(8,128)(2,1)S(1)} collective-permute-done((bf16[768,128]{1,0:T(8,128)(2,1)S(1)}, bf16[768,128]{1,0:T(8,128)(2,1)S(1)}, u32[]{:S(2)}, u32[]{:S(2)}) %collective-permute-start.14) | collective-permute-done | bytes 196640 | tf_op jit(solution)/shard_map/ppermute | solution.py:370
  111.8 1.7 %add_convert_fusion.part_ref = bf16[768,768]{1,0:T(8,128)(2,1)S(1)} fusion(bf16[768,768]{1,0:T(8,128)(2,1)} %copy-done.4, f32[768,768]{1,0:T(8,128)S(1)} %copy-done.1, f32[768,768]{1,0:T(8,128)S(1)} %copy-done.3, pred[]{:T(512)S(6)} %eq.5), kind=kLoop, calls=%fused_computation.6 | loop fusion | flops 2359296 | bytes 7077889 | tf_op jit(solution)/shard_map/convert_element_type | solution.py:393
  113.5 1.4 shard_map.103
  114.9 8.0 %all-to-all-start = ((bf16[16,48,128]{2,1,0:T(8,128)(2,1)}), bf16[16,48,128]{2,1,0:T(8,128)(2,1)S(1)}, u32[]{:S(2)}, u32[]{:S(2)}) async-start(bf16[16,48,128]{2,1,0:T(8,128)(2,1)} %bitcast.6), calls=%async_computation | async-start | bytes 393216 | tf_op jit(solution)/shard_map/all_to_all | solution.py:373
  123.0 5.3 %collective-permute-start.16 = (bf16[768,128]{1,0:T(8,128)(2,1)S(1)}, bf16[768,128]{1,0:T(8,128)(2,1)S(1)}, u32[]{:S(2)}, u32[]{:S(2)}) collective-permute-start(bf16[768,128]{1,0:T(8,128)(2,1)S(1)} %add_convert_fusion.1.w_ref), channel_id=1, source_target_pairs={{0,1},{1,0},{2,3},{3,2},{4,5},{5,4},{6,7},{7,6},{8,9},{9,8},{10,11... | collective-permute-start | bytes 589832 | tf_op jit(solution)/shard_map/ppermute | solution.py:361
  128.3 3.6 %all-to-all-done.got_ref = bf16[16,48,128]{2,1,0:T(8,128)(2,1)S(1)} async-done(((bf16[16,48,128]{2,1,0:T(8,128)(2,1)}), bf16[16,48,128]{2,1,0:T(8,128)(2,1)S(1)}, u32[]{:S(2)}, u32[]{:S(2)}) %all-to-all-start) | async-done | bytes 196640 | tf_op jit(solution)/shard_map/all_to_all | solution.py:373
  131.9 6.4 %collective-permute-start.11 = (f32[48,128]{1,0:T(8,128)S(1)}, f32[48,128]{1,0:T(8,128)S(1)}, u32[]{:S(2)}, u32[]{:S(2)}) collective-permute-start(f32[48,128]{1,0:T(8,128)S(1)} %shard_map.104.own_ref), channel_id=1, source_target_pairs={{0,1},{1,0},{2,3},{3,2},{4,5},{5,4},{6,7},{7,6},{8,9},{9,8},{10,11... | collective-permute-start | bytes 73736 | tf_op jit(solution)/shard_map/ppermute | solution.py:361
  139.2 0.9 shard_map.105
  140.9 11.6 %shard_map.111 = (bf16[1536,768]{1,0:T(8,128)(2,1)}, bf16[1536,768]{1,0:T(8,128)(2,1)}) custom-call(bf16[1536,768]{1,0:T(8,128)(2,1)} %bitcast.45, bf16[768,768]{1,0:T(8,128)(2,1)} %shard_map.102.near_ref.near_hbm, bf16[768,768]{1,0:T(8,128)(2,1)} %collective-permute-done.12.other_hbm, bf16[768,128]{1,0:T(8,128)(2,1)} %copy-done.14, ...), custom_call_target="tpu_custom_call" | custom-call | flops 3623878656 | bytes 8388608 | tf_op jit(solution)/shard_map/pallas_call | solution.py:470
  (76 shorter events, 6.1 us)
Async XLA Ops:
  5.3 11.5 %copy-start = (f32[768,768]{1,0:T(8,128)}, f32[768,768]{1,0:T(8,128)S(1)}, u32[]{:S(2)}) copy-start(f32[768,768]{1,0:T(8,128)S(1)} %fusion.6.left_ref) | copy-start | bytes 7077892
  5.3 5.5 %copy-start.9 = (s32[1,768]{1,0:T(1,128)S(1)}, s32[1,768]{1,0:T(1,128)}, u32[]{:S(2)}) copy-start(s32[1,768]{1,0:T(1,128)} %row_ref.11) | copy-start | bytes 9220
  5.3 11.4 %copy-start.10 = (f32[1,24,768]{2,1,0:T(8,128)S(1)}, f32[1,24,768]{2,1,0:T(8,128)}, u32[]{:S(2)}) copy-start(f32[1,24,768]{2,1,0:T(8,128)} %param.12) | copy-start | bytes 221188
  5.3 11.4 %copy-start.11 = (f32[1,24,768]{2,1,0:T(8,128)S(1)}, f32[1,24,768]{2,1,0:T(8,128)}, u32[]{:S(2)}) copy-start(f32[1,24,768]{2,1,0:T(8,128)} %param.13) | copy-start | bytes 221188
  7.4 10.5 %copy-start.2 = (f32[768,768]{1,0:T(8,128)}, f32[768,768]{1,0:T(8,128)S(1)}, u32[]{:S(2)}) copy-start(f32[768,768]{1,0:T(8,128)S(1)} %get-tuple-element.23.right_ref) | copy-start | bytes 7077892
  7.4 9.3 %collective-permute-start.10 = (bf16[768,768]{1,0:T(8,128)(2,1)S(1)}, bf16[768,768]{1,0:T(8,128)(2,1)S(1)}, u32[]{:S(2)}, u32[]{:S(2)}) collective-permute-start(bf16[768,768]{1,0:T(8,128)(2,1)S(1)} %get-tuple-element.22), channel_id=1, source_target_pairs={{0,1},{1,0},{2,3},{3,2},{4,5},{5,4},{6,7},{7,6},{8,9},{9,8},{10,11... | collective-permute-start | bytes 3538952 | tf_op jit(solution)/shard_map/ppermute | solution.py:361
  10.7 2.5 %collective-permute-start = (bf16[24,768]{1,0:T(8,128)(2,1)S(1)}, bf16[24,768]{1,0:T(8,128)(2,1)S(1)}, u32[]{:S(2)}, u32[]{:S(2)}) collective-permute-start(bf16[24,768]{1,0:T(8,128)(2,1)S(1)} %bitcast.46), channel_id=1, source_target_pairs={{0,1},{1,0},{2,3},{3,2},{4,5},{5,4},{6,7},{7,6},{8,9},{9,8},{10,11... | collective-permute-start | bytes 110600 | tf_op jit(solution)/shard_map/ppermute | solution.py:361
  13.3 3.4 %collective-permute-start.1 = (bf16[56,768]{1,0:T(8,128)(2,1)S(1)}, bf16[56,768]{1,0:T(8,128)(2,1)S(1)}, u32[]{:S(2)}, u32[]{:S(2)}) collective-permute-start(bf16[56,768]{1,0:T(8,128)(2,1)S(1)} %pad_maximum_fusion.1), channel_id=1, source_target_pairs={{0,32},{1,225},{2,34},{3,227},{4,36},{5,229},{6,38},{7,231},{8,40}... | collective-permute-start | bytes 258056 | tf_op jit(solution)/shard_map/ppermute | solution.py:370
  50.5 49.3 %copy-start.8 = (bf16[16,48,128]{2,1,0:T(8,128)(2,1)S(1)}, bf16[16,48,128]{2,1,0:T(8,128)(2,1)}, u32[]{:S(2)}) copy-start(bf16[16,48,128]{2,1,0:T(8,128)(2,1)} %get-tuple-element.14.early_ref) | copy-start | bytes 589828
  50.5 50.5 %all-to-all-start.2 = ((bf16[16,48,384]{2,1,0:T(8,128)(2,1)}), bf16[16,48,384]{2,1,0:T(8,128)(2,1)S(1)}, u32[]{:S(2)}, u32[]{:S(2)}) async-start(bf16[16,48,384]{2,1,0:T(8,128)(2,1)} %get-tuple-element.17), calls=%async_computation.2 | async-start | bytes 1179648 | tf_op jit(solution)/shard_map/all_to_all | solution.py:373
  57.8 5.2 %collective-permute-start.2 = (bf16[48,768]{1,0:T(8,128)(2,1)S(1)}, bf16[48,768]{1,0:T(8,128)(2,1)S(1)}, u32[]{:S(2)}, u32[]{:S(2)}) collective-permute-start(bf16[48,768]{1,0:T(8,128)(2,1)S(1)} %slice.8), channel_id=1, source_target_pairs={{0,16},{1,17},{2,18},{3,19},{4,20},{5,21},{6,22},{7,23},{8,24},{9,... | collective-permute-start | bytes 221192 | tf_op jit(solution)/shard_map/ppermute | solution.py:428
  63.0 28.8 %copy-start.13 = (bf16[96,768]{1,0:T(8,128)(2,1)}, bf16[96,768]{1,0:T(8,128)(2,1)S(1)}, u32[]{:S(2)}) copy-start(bf16[96,768]{1,0:T(8,128)(2,1)S(1)} %pad_maximum_fusion.refs_0_) | copy-start | bytes 442372
  63.0 13.1 %collective-permute-start.3 = (bf16[96,768]{1,0:T(8,128)(2,1)S(1)}, bf16[96,768]{1,0:T(8,128)(2,1)S(1)}, u32[]{:S(2)}, u32[]{:S(2)}) collective-permute-start(bf16[96,768]{1,0:T(8,128)(2,1)S(1)} %pad_maximum_fusion.refs_0_), channel_id=1, source_target_pairs={{0,2},{1,3},{2,4},{3,5},{4,6},{5,7},{6,8},{7,9},{8,10},{9,11},{10,... | collective-permute-start | bytes 442376 | tf_op jit(solution)/shard_map/ppermute | solution.py:428
  64.3 11.8 %collective-permute-start.4 = (bf16[96,768]{1,0:T(8,128)(2,1)S(1)}, bf16[96,768]{1,0:T(8,128)(2,1)S(1)}, u32[]{:S(2)}, u32[]{:S(2)}) collective-permute-start(bf16[96,768]{1,0:T(8,128)(2,1)S(1)} %pad_maximum_fusion.refs_0_), channel_id=1, source_target_pairs={{0,14},{1,15},{2,0},{3,1},{4,2},{5,3},{6,4},{7,5},{8,6},{9,7},{10,... | collective-permute-start | bytes 442376 | tf_op jit(solution)/shard_map/ppermute | solution.py:428
  76.1 15.7 %copy-start.15 = (bf16[96,768]{1,0:T(8,128)(2,1)}, bf16[96,768]{1,0:T(8,128)(2,1)S(1)}, u32[]{:S(2)}) copy-start(bf16[96,768]{1,0:T(8,128)(2,1)S(1)} %collective-permute-done.3.refs_1_) | copy-start | bytes 442372
  76.1 5.2 %collective-permute-start.5 = (bf16[96,768]{1,0:T(8,128)(2,1)S(1)}, bf16[96,768]{1,0:T(8,128)(2,1)S(1)}, u32[]{:S(2)}, u32[]{:S(2)}) collective-permute-start(bf16[96,768]{1,0:T(8,128)(2,1)S(1)} %collective-permute-done.3.refs_1_), channel_id=1, source_target_pairs={{0,2},{1,3},{2,4},{3,5},{4,6},{5,7},{6,8},{7,9},{8,10},{9,11},{10,... | collective-permute-start | bytes 442376 | tf_op jit(solution)/shard_map/ppermute | solution.py:428
  76.1 15.7 %copy-start.16 = (bf16[96,768]{1,0:T(8,128)(2,1)}, bf16[96,768]{1,0:T(8,128)(2,1)S(1)}, u32[]{:S(2)}) copy-start(bf16[96,768]{1,0:T(8,128)(2,1)S(1)} %collective-permute-done.4.refs_2_) | copy-start | bytes 442372
  76.1 5.2 %collective-permute-start.6 = (bf16[96,768]{1,0:T(8,128)(2,1)S(1)}, bf16[96,768]{1,0:T(8,128)(2,1)S(1)}, u32[]{:S(2)}, u32[]{:S(2)}) collective-permute-start(bf16[96,768]{1,0:T(8,128)(2,1)S(1)} %collective-permute-done.4.refs_2_), channel_id=1, source_target_pairs={{0,14},{1,15},{2,0},{3,1},{4,2},{5,3},{6,4},{7,5},{8,6},{9,7},{10,... | collective-permute-start | bytes 442376 | tf_op jit(solution)/shard_map/ppermute | solution.py:428
  81.3 10.5 %copy-start.17 = (bf16[96,768]{1,0:T(8,128)(2,1)}, bf16[96,768]{1,0:T(8,128)(2,1)S(1)}, u32[]{:S(2)}) copy-start(bf16[96,768]{1,0:T(8,128)(2,1)S(1)} %collective-permute-done.5.refs_3_) | copy-start | bytes 442372
  81.3 5.2 %collective-permute-start.7 = (bf16[96,768]{1,0:T(8,128)(2,1)S(1)}, bf16[96,768]{1,0:T(8,128)(2,1)S(1)}, u32[]{:S(2)}, u32[]{:S(2)}) collective-permute-start(bf16[96,768]{1,0:T(8,128)(2,1)S(1)} %collective-permute-done.5.refs_3_), channel_id=1, source_target_pairs={{0,2},{1,3},{2,4},{3,5},{4,6},{5,7},{6,8},{7,9},{8,10},{9,11},{10,... | collective-permute-start | bytes 442376 | tf_op jit(solution)/shard_map/ppermute | solution.py:428
  81.3 9.5 %collective-permute-start.8 = (bf16[96,768]{1,0:T(8,128)(2,1)S(1)}, bf16[96,768]{1,0:T(8,128)(2,1)S(1)}, u32[]{:S(2)}, u32[]{:S(2)}) collective-permute-start(bf16[96,768]{1,0:T(8,128)(2,1)S(1)} %collective-permute-done.6.refs_4_), channel_id=1, source_target_pairs={{0,14},{1,15},{2,0},{3,1},{4,2},{5,3},{6,4},{7,5},{8,6},{9,7},{10,... | collective-permute-start | bytes 442376 | tf_op jit(solution)/shard_map/ppermute | solution.py:428
  86.5 5.3 %collective-permute-start.9 = (bf16[96,768]{1,0:T(8,128)(2,1)S(1)}, bf16[96,768]{1,0:T(8,128)(2,1)}, u32[]{:S(2)}, u32[]{:S(2)}) collective-permute-start(bf16[96,768]{1,0:T(8,128)(2,1)S(1)} %collective-permute-done.7.refs_5_), channel_id=1, source_target_pairs={{0,2},{1,3},{2,4},{3,5},{4,6},{5,7},{6,8},{7,9},{8,10},{9,11},{10,... | collective-permute-start | bytes 442376 | tf_op jit(solution)/shard_map/ppermute | solution.py:428
  86.5 25.3 %copy-start.1 = (f32[768,768]{1,0:T(8,128)S(1)}, f32[768,768]{1,0:T(8,128)}, u32[]{:S(2)}) copy-start(f32[768,768]{1,0:T(8,128)} %copy-done) | copy-start | bytes 7077892
  86.5 13.3 %collective-permute-start.13 = (bf16[16,48,128]{2,1,0:T(8,128)(2,1)}, bf16[16,48,128]{2,1,0:T(8,128)(2,1)S(1)}, u32[]{:S(2)}, u32[]{:S(2)}) collective-permute-start(bf16[16,48,128]{2,1,0:T(8,128)(2,1)} %get-tuple-element.14.early_ref), channel_id=1, source_target_pairs={{0,1},{1,0},{2,3},{3,2},{4,5},{5,4},{6,7},{7,6},{8,9},{9,8},{10,11... | collective-permute-start | bytes 589832 | tf_op jit(solution)/shard_map/ppermute | solution.py:361
  94.4 45.8 %collective-permute-start.12 = (bf16[768,768]{1,0:T(8,128)(2,1)}, bf16[768,768]{1,0:T(8,128)(2,1)}, u32[]{:S(2)}, u32[]{:S(2)}) collective-permute-start(bf16[768,768]{1,0:T(8,128)(2,1)} %shard_map.102.near_ref.near_hbm), channel_id=1, source_target_pairs={{0,1},{1,0},{2,3},{3,2},{4,5},{5,4},{6,7},{7,6},{8,9},{9,8},{10,11... | collective-permute-start | bytes 3538952 | tf_op jit(solution)/shard_map/ppermute | solution.py:361
  101.0 10.7 %copy-start.3 = (f32[768,768]{1,0:T(8,128)S(1)}, f32[768,768]{1,0:T(8,128)}, u32[]{:S(2)}) copy-start(f32[768,768]{1,0:T(8,128)} %copy-done.2) | copy-start | bytes 7077892
  102.9 7.9 %collective-permute-start.14 = (bf16[768,128]{1,0:T(8,128)(2,1)S(1)}, bf16[768,128]{1,0:T(8,128)(2,1)S(1)}, u32[]{:S(2)}, u32[]{:S(2)}) collective-permute-start(bf16[768,128]{1,0:T(8,128)(2,1)S(1)} %shard_map.109), channel_id=1, source_target_pairs={{0,224},{1,33},{2,226},{3,35},{4,228},{5,37},{6,230},{7,39},{8,232... | collective-permute-start | bytes 589832 | tf_op jit(solution)/shard_map/ppermute | solution.py:370
  111.7 11.3 %collective-permute-start.15 = (bf16[768,128]{1,0:T(8,128)(2,1)S(1)}, bf16[768,128]{1,0:T(8,128)(2,1)S(1)}, u32[]{:S(2)}, u32[]{:S(2)}) collective-permute-start(bf16[768,128]{1,0:T(8,128)(2,1)S(1)} %shard_map.110), channel_id=1, source_target_pairs={{0,224},{1,33},{2,226},{3,35},{4,228},{5,37},{6,230},{7,39},{8,232... | collective-permute-start | bytes 589832 | tf_op jit(solution)/shard_map/ppermute | solution.py:370
  114.9 17.0 %all-to-all-start = ((bf16[16,48,128]{2,1,0:T(8,128)(2,1)}), bf16[16,48,128]{2,1,0:T(8,128)(2,1)S(1)}, u32[]{:S(2)}, u32[]{:S(2)}) async-start(bf16[16,48,128]{2,1,0:T(8,128)(2,1)} %bitcast.6), calls=%async_computation | async-start | bytes 393216 | tf_op jit(solution)/shard_map/all_to_all | solution.py:373
  123.0 17.2 %copy-start.14 = (bf16[768,128]{1,0:T(8,128)(2,1)}, bf16[768,128]{1,0:T(8,128)(2,1)S(1)}, u32[]{:S(2)}) copy-start(bf16[768,128]{1,0:T(8,128)(2,1)S(1)} %add_convert_fusion.1.w_ref) | copy-start | bytes 589828
  123.0 17.2 %collective-permute-start.16 = (bf16[768,128]{1,0:T(8,128)(2,1)S(1)}, bf16[768,128]{1,0:T(8,128)(2,1)S(1)}, u32[]{:S(2)}, u32[]{:S(2)}) collective-permute-start(bf16[768,128]{1,0:T(8,128)(2,1)S(1)} %add_convert_fusion.1.w_ref), channel_id=1, source_target_pairs={{0,1},{1,0},{2,3},{3,2},{4,5},{5,4},{6,7},{7,6},{8,9},{9,8},{10,11... | collective-permute-start | bytes 589832 | tf_op jit(solution)/shard_map/ppermute | solution.py:361
  131.9 7.3 %collective-permute-start.11 = (f32[48,128]{1,0:T(8,128)S(1)}, f32[48,128]{1,0:T(8,128)S(1)}, u32[]{:S(2)}, u32[]{:S(2)}) collective-permute-start(f32[48,128]{1,0:T(8,128)S(1)} %shard_map.104.own_ref), channel_id=1, source_target_pairs={{0,1},{1,0},{2,3},{3,2},{4,5},{5,4},{6,7},{7,6},{8,9},{9,8},{10,11... | collective-permute-start | bytes 73736 | tf_op jit(solution)/shard_map/ppermute | solution.py:361
  (11 other events, 30.7 us)

commit v5 on v4

--- a/solution.py
+++ b/solution.py
@@ -50,7 +50,7 @@
 
 def pack_kernel(
     left_ref, right_ref, other_ref, row_ref, to_row_ref, cot_left_ref, cot_right_ref,
-    out_ref, stage_ref, cot_ref, sems,
+    out_ref, cot_ref, sems,
 ):
     chi = left_ref.shape[0]
     rows = cot_ref.shape[1]
@@ -84,7 +84,7 @@
                 old = totals[q % wide]
                 totals[q % wide] = part if old is None else old + part
             for q in range(wide):
-                stage_ref[at, lanes(q)] = totals[q].astype(BF16)
+                out_ref[at, lanes(q)] = totals[q].astype(BF16)
 
     @pl.when(lax.rem(blk, 2) == 0)
     def _():
@@ -103,34 +103,30 @@
         cot = fold_lanes(jnp.where(mask, cot_ref[n], 0.0), FOLD).astype(BF16)
         for q in range(chi // (2 * rows)):
             at = 2 * rows * q + rows * n
-            stage_ref[at : at + rows, WIDE:] = cot
-    copy = pltpu.make_async_copy(stage_ref, out_ref, sems.at[2])
-    copy.start()
-    copy.wait()
-
-
-def sum_kernel(got_ref, out_ref, early_ref, held_ref, total_ref, sems):
-    chips = got_ref.shape[0]
-    part = chips // 4
-    copies = [
-        pltpu.make_async_copy(
-            got_ref.at[pl.ds(part * n, part)], held_ref.at[pl.ds(part * n, part)], sems.at[n]
-        )
-        for n in range(4)
-    ]
-    for copy in copies:
-        copy.start()
-    total = jnp.zeros(total_ref.shape, F32)
-    for n, copy in enumerate(copies):
-        copy.wait()
-        for q in range(part * n, part * (n + 1)):
-            total = total + held_ref[q, :, :WIDE].astype(F32)
-    total_ref[...] = total.astype(BF16)
-    for q in range(chips):
-        pltpu.make_async_copy(total_ref, out_ref.at[q], sems.at[q]).start()
-    early_ref[...] = held_ref[:, :, WIDE:]
-    for q in range(chips):
-        pltpu.make_async_copy(total_ref, out_ref.at[q], sems.at[q]).wait()
+            out_ref[at : at + rows, WIDE:] = cot
+
+
+def sum_kernel(got_ref, out_ref, early_ref):
+    total = got_ref[0, :, :WIDE].astype(F32)
+    for q in range(1, got_ref.shape[0]):
+        total = total + got_ref[q, :, :WIDE].astype(F32)
+    out_ref[...] = jnp.broadcast_to(total.astype(BF16)[None], out_ref.shape)
+    early_ref[...] = got_ref[:, :, WIDE:]
+
+
+def pair_kernel(own_ref, other_ref, out_ref):
+    rows = own_ref.shape[0]
+    core = lax.rem(lax.axis_index("blk"), 2)
+
+    @pl.when(core == 0)
+    def _():
+        out_ref[:rows, :] = own_ref[...]
+        out_ref[rows : 2 * rows, :] = other_ref[...]
+
+    @pl.when(core == 1)
+    def _():
+        out_ref[:rows, :] = other_ref[...]
+        out_ref[rows : 2 * rows, :] = own_ref[...]
 
 
 def start_kernel(early_ref, other_ref, row_ref, open_ref, cot_ref, w_ref):
@@ -166,13 +162,20 @@
             open_ref[lanes(i), lanes(q)] = jnp.where(same, w, 0.0).astype(BF16)
 
 
-def weave_kernel(*refs):
-    *piece_refs, out_ref, sems = refs
+def fold_tile(product, col, row, low, high):
+    total = jnp.zeros((FOLD, FOLD), F32)
+    for q in range(low, high):
+        total = total + jnp.where(col == row[:, lanes(q)], product[:, lanes(q - low)], 0.0)
+    return total.astype(BF16)
+
+
+def new_kernel(*refs):
+    *piece_refs, part_hbm, row_ref, turned_ref, out_ref, near_ref, part_ref, sems = refs
     ring = len(piece_refs)
     block = piece_refs[0].shape[0] // 2
     chip = lax.div(lax.axis_index("blk"), 2)
     y, z = lax.div(chip, ring), lax.rem(chip, ring)
-    copies = []
+    copies = [pltpu.make_async_copy(part_hbm, part_ref, sems.at[2 * ring])]
     for n, ref in enumerate(piece_refs):
         step = -((n + 1) // 2) if n % 2 else n // 2
         for half in range(2):
@@ -180,25 +183,17 @@
             at = pl.multiple_of(source * block, 16)
             copies.append(
                 pltpu.make_async_copy(
-                    ref.at[pl.ds(block * half, block)], out_ref.at[pl.ds(at, block)], sems.at[2 * n + half]
+                    ref.at[pl.ds(block * half, block)], near_ref.at[pl.ds(at, block)], sems.at[2 * n + half]
                 )
             )
     for copy in copies:
         copy.start()
     for copy in copies:
         copy.wait()
-
-
-def fold_tile(product, col, row, low, high):
-    total = jnp.zeros((FOLD, FOLD), F32)
-    for q in range(low, high):
-        total = total + jnp.where(col == row[:, lanes(q)], product[:, lanes(q - low)], 0.0)
-    return total.astype(BF16)
-
-
-def new_kernel(near_ref, part_ref, row_ref, out_ref):
     tiles = near_ref.shape[0] // FOLD
     row = label_row(row_ref)
+    for i in range(tiles):
+        turned_ref[:, lanes(i)] = near_ref[lanes(i), :].astype(F32).T.astype(BF16)
     for i in range(tiles):
         low, high = near_tiles(i, tiles)
         product = jnp.dot(
@@ -270,7 +265,7 @@
 
 
 SLOTS = 4
-STEP = 256
+STEP = 384
 
 
 def grad_kernel(
@@ -298,18 +293,19 @@
     near_copies[1].start()
     for side, w in enumerate((w_ref, w_other_ref)):
         near_copies[side].wait()
-        for i in range(tiles):
-            low, high = near_tiles(i, tiles)
-            col = column(row, i)
-            x = w[lanes(i), :].astype(F32)
-            for q in range(low, high):
-                open_ref[:, lanes(q - low)] = jnp.where(col == row[:, lanes(q)], x, 0.0).astype(BF16)
-            mid = jnp.dot(
-                open_ref[:, : FOLD * (high - low)],
-                near_ref[side, FOLD * low : FOLD * high, :],
+        cols = [column(row, q) for q in range(tiles)]
+        for i in range(0, tiles, 2):
+            low, high = max(0, i - 1), min(tiles, i + 3)
+            for half in range(2):
+                x = w[lanes(i + half), :].astype(F32).T
+                for q in range(low, high):
+                    same = cols[q] == row[:, lanes(i + half)]
+                    open_ref[lanes(q - low), lanes(half)] = jnp.where(same, x, 0.0).astype(BF16)
+            mid_ref[:, FOLD * i : FOLD * (i + 2)] = jnp.dot(
+                near_ref[side, :, FOLD * low : FOLD * high],
+                open_ref[: FOLD * (high - low), :],
                 preferred_element_type=F32,
-            )
-            mid_ref[:, lanes(i)] = mid.T.astype(BF16)
+            ).astype(BF16)
         for n in range(steps):
             at = side * steps + n
             slot = at % SLOTS
@@ -376,15 +372,16 @@
         return jnp.where(first, a, b)
 
     row = charge
-    scale = jnp.broadcast_to(charge.astype(BF16), (8, chi))
+    to_row = site_move(charge, 1, False)
     other_corner = swap_cores(corner[0])
-    pair_corner = [pick(corner[0], other_corner), pick(other_corner, corner[0])]
-    near = site_move(jnp.concatenate(pair_corner + [scale], axis=0), 1, False)
-    to_row = near[pair_rows : pair_rows + 1].astype(jnp.int32)
-    near = near[:pair_rows]
 
     def array(*shape, dtype=BF16):
         return jax.ShapeDtypeStruct(shape, dtype)
+
+    pair_corner = call(pair_kernel, array(pair_rows, chi), [VMEM] * 2, [], 0, 1 << 18)(
+        corner[0], other_corner
+    )
+    near = site_move(pair_corner, 1, False)
 
     edge_flat = edge[0].reshape(rows * depth, chi)
     part_left = contract_first(edge_flat, proj_left[0].reshape(rows * depth, chi))
@@ -395,25 +392,19 @@
         pack_kernel,
         array(chi, WIDE + FOLD),
         [VMEM] * 5 + [ANY] * 2,
-        [pltpu.VMEM((chi, WIDE + FOLD), BF16), pltpu.VMEM((2, rows, chi), F32), pltpu.SemaphoreType.DMA((3,))],
+        [pltpu.VMEM((2, rows, chi), F32), pltpu.SemaphoreType.DMA((2,))],
         chi * chi * 8,
         6 << 20,
-        HBM,
     )(part_left, part_right, other_part, row, to_row, cot_left[0], cot_right[0])
     got = exchange(packed.reshape(chips, pair_rows, WIDE + FOLD))
     summed, early = call(
         sum_kernel,
         (array(chips, pair_rows, WIDE), array(chips, pair_rows, FOLD)),
-        [HBM],
-        [
-            pltpu.VMEM((chips, pair_rows, WIDE + FOLD), BF16),
-            pltpu.VMEM((pair_rows, WIDE), BF16),
-            pltpu.SemaphoreType.DMA((chips,)),
-        ],
+        [VMEM],
+        [],
         0,
         3 << 20,
-        (HBM, VMEM),
-        63 << 20,
+        (VMEM, VMEM),
     )(got)
     enl = exchange(summed).reshape(chi, WIDE)
 
@@ -436,7 +427,16 @@
         if n < ring // 2:
             down = ring_move(down, 0, -1)
             pieces.append(down)
-    near = call(weave_kernel, array(chi, chi), [ANY] * ring, [pltpu.SemaphoreType.DMA((chips,))], 0, 3 << 20, VMEM, 60 << 20)(*pieces)
+    near, new_part = call(
+        new_kernel,
+        (array(chi, chi), array(chi, FOLD)),
+        [ANY] * (ring + 1) + [VMEM],
+        [pltpu.VMEM((chi, chi), BF16)] * 2 + [pltpu.SemaphoreType.DMA((chips + 1,))],
+        chi * chi * chi,
+        3 << 20,
+        (VMEM, VMEM),
+        60 << 20,
+    )(*pieces, part_bf, row)
     near_other = swap_cores(near)
 
     early_other = swap_cores(early)
@@ -449,7 +449,9 @@
         1 << 20,
         (VMEM, VMEM),
     )(early, early_other, row)
-    back1 = call(first_kernel, array(chi, FOLD), [VMEM] * 3, [], chi * chi * WIDE, 2 << 20)(w_open, enl, to_row)
+    back1 = call(first_kernel, array(chi, FOLD), [VMEM] * 3, [], chi * chi * WIDE, 2 << 20)(
+        w_open, enl, to_row
+    )
     back1_at = site_move(back1, -1, False)
     back2 = call(
         second_kernel, array(chi, FOLD), [VMEM] * 5, [pltpu.VMEM((WIDE, chi), BF16)], chi * chi * WIDE, 2 << 20
@@ -458,7 +460,6 @@
     w2 = (cot.astype(F32) + back2_at.astype(F32)).astype(BF16)
     w2_other = swap_cores(w2)
 
-    new_part = call(new_kernel, array(chi, FOLD), [VMEM] * 3, [], chi * chi * chi, 3 << 20)(near, part_bf, row)
     new_got = exchange(new_part.reshape(chips, pair_rows, FOLD))
     new_sum = call(total_kernel, array(pair_rows, FOLD, dtype=F32), [VMEM], [], 0, 1 << 18)(new_got)
     new_other = swap_cores(new_sum)
@@ -474,7 +475,7 @@
         [
             pltpu.VMEM((rows * depth, chi), BF16),
             pltpu.VMEM((2, chi, chi), BF16),
-            pltpu.VMEM((FOLD, WIDE), BF16),
+            pltpu.VMEM((4 * FOLD, 2 * FOLD), BF16),
             pltpu.VMEM((chi, chi), BF16),
             pltpu.VMEM((SLOTS, STEP, chi), BF16),
             pltpu.SemaphoreType.DMA((rows * depth // STEP + 2,)),
@@ -483,7 +484,7 @@
         4 * rows * depth * chi * chi,
         8 << 20,
         (HBM, HBM),
-        62 << 20,
+        60 << 20,
     )(edge_flat, near, near_other, w2, w2_other, row)
     return (
         new_left[None],

time: 153 us -> 145 us (0.948)
  blocking collectives: 29.6 us -> 0 us
  starting transfers between devices: 53.6 us -> 65.9 us
  waiting for transfers between devices: 33.8 us -> 43 us
  Pallas kernels: 22.5 us -> 19.5 us
  other arithmetic: 1.86 us -> 3.57 us
    all_to_all x1 -> x0, blocking collectives: 29.6 us -> none  [exchange(): return lax.all_to_all(x, 'blk', 0, 0, tiled=True, axis_index_groups=groups)]
    all_to_all x2 -> x3, starting transfers between devices: 15.3 us -> 26.4 us  [exchange(): return lax.all_to_all(x, 'blk', 0, 0, tiled=True, axis_index_groups=groups)]
    all_to_all x2 -> x3, waiting for transfers between devices: 3.6 us -> 7.59 us  [exchange(): return lax.all_to_all(x, 'blk', 0, 0, tiled=True, axis_index_groups=groups)]
    pallas_call x1, Pallas kernels: 2.9 us -> 0.11 us  [body(): call(sum_kernel, (array(chips, pair_rows, WIDE), array(chips, pair_rows,...]
    ppermute x3 -> x4, starting transfers between devices: 2.38 us -> 5.1 us  [site_move(): return lax.ppermute(x, ('site', 'blk'), route)]
    ppermute x8, waiting for transfers between devices: 17.9 us -> 20.2 us  [ring_move(): lax.ppermute(x, 'blk', [(i, turn(i, dy, dz)) for i in range(members)])]
    convert_element_type x1, other arithmetic: 1.74 us -> 3.51 us  [body(): (pick(part_left, part_right) + other_part.astype(F32)).astype(BF16)]
    ppermute x6, starting transfers between devices: 24.9 us -> 23.2 us  [swap_cores(): return lax.ppermute(x, 'blk', [(i, i ^ 1) for i in range(members)])]
  transfers between devices with their start and end apart: 19 -> 21, of which waited for: 10 -> 12; matrix products, arithmetic and copies ran while one was open for 1% -> 2% of each run, Pallas kernels for 4% -> 5%
where the time goes in v5:
time: 145 us
  starting transfers between devices  65.9 us (45%)
  waiting for transfers between devices  43 us (30%)
  Pallas kernels  19.5 us (13%)
  matrix products  6.66 us (5%)
  local copies, waits for them, and re-layouts  4.99 us (3%)
  other arithmetic  3.57 us (2%)
    all_to_all x3, starting transfers between devices, exchange(): return lax.all_to_all(x, 'blk', 0, 0, tiled=True, axis_index_groups=groups)  26.4 us
    ppermute x6, starting transfers between devices, swap_cores(): return lax.ppermute(x, 'blk', [(i, i ^ 1) for i in range(members)])  23.2 us
    ppermute x8, waiting for transfers between devices, ring_move(): lax.ppermute(x, 'blk', [(i, turn(i, dy, dz)) for i in range(members)])  20.2 us
    pallas_call x1, Pallas kernels, body(): call(grad_kernel, (flat, flat), [HBM] * 3 + [VMEM] * 3, [pltpu.VMEM((rows...  11.5 us
    ppermute x8, starting transfers between devices, ring_move(): lax.ppermute(x, 'blk', [(i, turn(i, dy, dz)) for i in range(members)])  11.2 us
    ppermute x4, waiting for transfers between devices, site_move(): return lax.ppermute(x, ('site', 'blk'), route)  10.6 us
    all_to_all x3, waiting for transfers between devices, exchange(): return lax.all_to_all(x, 'blk', 0, 0, tiled=True, axis_index_groups=groups)  7.59 us
    dot_general x2, matrix products, contract_first(): lax.dot_general(left, right, (((0,), (0,)), ((), ())), preferred_element_...  6.66 us
  transfers between devices with their start and end apart: 21, of which 12 were waited for; matrix products, arithmetic and copies ran while one was open for 2% of the time, Pallas kernels for 5%

profile of v5, /device:TPU:1, one launch (start us, length us, event | category | flops | bytes accessed | tf_op | source)
XLA Modules:
  0.0 144.8 jit_solution(610440773453958309)
XLA Ops:
  0.7 4.6 %fusion.6.left_ref = f32[768,768]{1,0:T(8,128)S(1)} fusion(bf16[1,24,64,768]{3,2,1,0:T(8,128)(2,1)} %param.9, bf16[1,24,64,768]{3,2,1,0:T(8,128)(2,1)} %param.8), kind=kOutput, calls=%fused_computation.8 | convolution fusion | flops 1811939328 | bytes 7077888 | tf_op jit(solution)/shard_map/dot_general | solution.py:20
  5.3 2.1 %select_convert_fusion = (bf16[768,768]{1,0:T(8,128)(2,1)S(1)}, f32[768,768]{1,0:T(8,128)S(1)}) fusion(f32[768,768]{1,0:T(8,128)S(1)} %fusion.6.left_ref, pred[]{:T(512)S(6)} %eq.5, bf16[1,24,64,768]{3,2,1,0:T(8,128)(2,1)S(1)} %copy-done, bf16[1,24,64,768]{3,2,1,0:T(8,128)(2,1)S(1)} %copy-done.13), kind=kOutput, calls=%fused_computation.7 | convolution fusion | flops 1812529152 | bytes 10616833 | tf_op jit(solution)/shard_map/dot_general | solution.py:20
  7.4 3.3 %collective-permute-start.10 = (bf16[768,768]{1,0:T(8,128)(2,1)S(1)}, bf16[768,768]{1,0:T(8,128)(2,1)S(1)}, u32[]{:S(2)}, u32[]{:S(2)}) collective-permute-start(bf16[768,768]{1,0:T(8,128)(2,1)S(1)} %get-tuple-element.24), channel_id=1, source_target_pairs={{0,1},{1,0},{2,3},{3,2},{4,5},{5,4},{6,7},{7,6},{8,9},{9,8},{10,11... | collective-permute-start | bytes 3538952 | tf_op jit(solution)/shard_map/ppermute | solution.py:357
  10.7 1.8 %collective-permute-start.13 = (s32[1,768]{1,0:T(1,128)S(1)}, s32[1,768]{1,0:T(1,128)S(1)}, u32[]{:S(2)}, u32[]{:S(2)}) collective-permute-start(s32[1,768]{1,0:T(1,128)S(1)} %copy-done.8), channel_id=1, source_target_pairs={{0,32},{1,225},{2,34},{3,227},{4,36},{5,229},{6,38},{7,231},{8,40}... | collective-permute-start | bytes 9224 | tf_op jit(solution)/shard_map/ppermute | solution.py:366
  13.3 1.1 shard_map.106
  15.3 10.6 %all-to-all-start.1 = ((bf16[16,48,512]{2,1,0:T(8,128)(2,1)}), bf16[16,48,512]{2,1,0:T(8,128)(2,1)S(1)}, u32[]{:S(2)}, u32[]{:S(2)}) async-start(bf16[16,48,512]{2,1,0:T(8,128)(2,1)} %bitcast.40), calls=%async_computation.1 | async-start | bytes 1572864 | tf_op jit(solution)/shard_map/all_to_all | solution.py:369
  26.0 2.2 %collective-permute-start = (bf16[24,768]{1,0:T(8,128)(2,1)S(1)}, bf16[24,768]{1,0:T(8,128)(2,1)S(1)}, u32[]{:S(2)}, u32[]{:S(2)}) collective-permute-start(bf16[24,768]{1,0:T(8,128)(2,1)S(1)} %bitcast.43), channel_id=1, source_target_pairs={{0,1},{1,0},{2,3},{3,2},{4,5},{5,4},{6,7},{7,6},{8,9},{9,8},{10,11... | collective-permute-start | bytes 110600 | tf_op jit(solution)/shard_map/ppermute | solution.py:357
  29.1 1.4 collective-permute-start.1
  30.5 3.4 %collective-permute-done.1 = bf16[48,768]{1,0:T(8,128)(2,1)S(1)} collective-permute-done((bf16[48,768]{1,0:T(8,128)(2,1)S(1)}, bf16[48,768]{1,0:T(8,128)(2,1)S(1)}, u32[]{:S(2)}, u32[]{:S(2)}) %collective-permute-start.1) | collective-permute-done | bytes 73760 | tf_op jit(solution)/shard_map/ppermute | solution.py:366
  33.9 3.0 %collective-permute-start.2 = (bf16[48,768]{1,0:T(8,128)(2,1)S(1)}, bf16[48,768]{1,0:T(8,128)(2,1)S(1)}, u32[]{:S(2)}, u32[]{:S(2)}) collective-permute-start(bf16[48,768]{1,0:T(8,128)(2,1)S(1)} %collective-permute-done.1), channel_id=1, source_target_pairs={{0,16},{1,17},{2,18},{3,19},{4,20},{5,21},{6,22},{7,23},{8,24},{9,... | collective-permute-start | bytes 221192 | tf_op jit(solution)/shard_map/ppermute | solution.py:419
  36.8 2.6 %collective-permute-done.2 = bf16[48,768]{1,0:T(8,128)(2,1)S(1)} collective-permute-done((bf16[48,768]{1,0:T(8,128)(2,1)S(1)}, bf16[48,768]{1,0:T(8,128)(2,1)S(1)}, u32[]{:S(2)}, u32[]{:S(2)}) %collective-permute-start.2) | collective-permute-done | bytes 73760 | tf_op jit(solution)/shard_map/ppermute | solution.py:419
  39.5 2.0 %collective-permute-start.3 = (bf16[96,768]{1,0:T(8,128)(2,1)S(1)}, bf16[96,768]{1,0:T(8,128)(2,1)}, u32[]{:S(2)}, u32[]{:S(2)}) collective-permute-start(bf16[96,768]{1,0:T(8,128)(2,1)S(1)} %constant_dynamic-update-slice_fusion.refs_0_), channel_id=1, source_target_pairs={{0,2},{1,3},{2,4},{3,5},{4,6},{5,7},{6,8},{7,9},{8,10},{9,11},{10,... | collective-permute-start | bytes 442376 | tf_op jit(solution)/shard_map/ppermute | solution.py:419
  41.4 4.2 %all-to-all-done.1.got_ref = bf16[16,48,512]{2,1,0:T(8,128)(2,1)S(1)} async-done(((bf16[16,48,512]{2,1,0:T(8,128)(2,1)}), bf16[16,48,512]{2,1,0:T(8,128)(2,1)S(1)}, u32[]{:S(2)}, u32[]{:S(2)}) %all-to-all-start.1) | async-done | bytes 786464 | tf_op jit(solution)/shard_map/all_to_all | solution.py:369
  46.6 6.1 %all-to-all-start.2 = ((bf16[16,48,384]{2,1,0:T(8,128)(2,1)}), bf16[16,48,384]{2,1,0:T(8,128)(2,1)S(1)}, u32[]{:S(2)}, u32[]{:S(2)}) async-start(bf16[16,48,384]{2,1,0:T(8,128)(2,1)} %copy-done.5), calls=%async_computation.2 | async-start | bytes 1179648 | tf_op jit(solution)/shard_map/all_to_all | solution.py:369
  52.7 2.6 %collective-permute-start.4 = (bf16[96,768]{1,0:T(8,128)(2,1)S(1)}, bf16[96,768]{1,0:T(8,128)(2,1)S(1)}, u32[]{:S(2)}, u32[]{:S(2)}) collective-permute-start(bf16[96,768]{1,0:T(8,128)(2,1)S(1)} %constant_dynamic-update-slice_fusion.refs_0_), channel_id=1, source_target_pairs={{0,14},{1,15},{2,0},{3,1},{4,2},{5,3},{6,4},{7,5},{8,6},{9,7},{10,... | collective-permute-start | bytes 442376 | tf_op jit(solution)/shard_map/ppermute | solution.py:419
  55.3 13.7 %collective-permute-done.4.refs_2_ = bf16[96,768]{1,0:T(8,128)(2,1)S(1)} collective-permute-done((bf16[96,768]{1,0:T(8,128)(2,1)S(1)}, bf16[96,768]{1,0:T(8,128)(2,1)S(1)}, u32[]{:S(2)}, u32[]{:S(2)}) %collective-permute-start.4) | collective-permute-done | bytes 147488 | tf_op jit(solution)/shard_map/ppermute | solution.py:419
  68.9 1.0 collective-permute-start.6
  70.4 2.8 %collective-permute-done.6.refs_4_ = bf16[96,768]{1,0:T(8,128)(2,1)S(1)} collective-permute-done((bf16[96,768]{1,0:T(8,128)(2,1)S(1)}, bf16[96,768]{1,0:T(8,128)(2,1)S(1)}, u32[]{:S(2)}, u32[]{:S(2)}) %collective-permute-start.6) | collective-permute-done | bytes 147488 | tf_op jit(solution)/shard_map/ppermute | solution.py:419
  73.2 2.2 %collective-permute-start.8 = (bf16[96,768]{1,0:T(8,128)(2,1)S(1)}, bf16[96,768]{1,0:T(8,128)(2,1)S(1)}, u32[]{:S(2)}, u32[]{:S(2)}) collective-permute-start(bf16[96,768]{1,0:T(8,128)(2,1)S(1)} %collective-permute-done.6.refs_4_), channel_id=1, source_target_pairs={{0,14},{1,15},{2,0},{3,1},{4,2},{5,3},{6,4},{7,5},{8,6},{9,7},{10,... | collective-permute-start | bytes 442376 | tf_op jit(solution)/shard_map/ppermute | solution.py:419
  75.5 3.5 %add_convert_fusion.refs_8_ = bf16[768,768]{1,0:T(8,128)(2,1)} fusion(bf16[768,768]{1,0:T(8,128)(2,1)} %copy-done.3, f32[768,768]{1,0:T(8,128)} %copy-done.1, f32[768,768]{1,0:T(8,128)} %copy-done.2, pred[]{:T(512)S(6)} %eq.5), kind=kLoop, calls=%fused_computation.6 | loop fusion | flops 2359296 | bytes 7077889 | tf_op jit(solution)/shard_map/convert_element_type | solution.py:390
  79.7 1.1 collective-permute-done.9.refs_7_
  80.8 3.9 %shard_map.103 = (bf16[768,768]{1,0:T(8,128)(2,1)}, bf16[768,128]{1,0:T(8,128)(2,1)}) custom-call(bf16[96,768]{1,0:T(8,128)(2,1)} %copy-done.14, bf16[96,768]{1,0:T(8,128)(2,1)} %collective-permute-done.3.refs_1_, bf16[96,768]{1,0:T(8,128)(2,1)} %copy-done.16, bf16[96,768]{1,0:T(8,128)(2,1)} %copy-done.17, bf16[96,768]{1,0:T(8,128)(2,1)} %copy-done.18, ...), custom_call_target="tpu_custom_call" | custom-call | flops 452984832 | bytes 3145728 | tf_op jit(solution)/shard_map/pallas_call | solution.py:430
  84.7 5.3 %collective-permute-start.12 = (bf16[768,768]{1,0:T(8,128)(2,1)}, bf16[768,768]{1,0:T(8,128)(2,1)}, u32[]{:S(2)}, u32[]{:S(2)}) collective-permute-start(bf16[768,768]{1,0:T(8,128)(2,1)} %get-tuple-element.17.near_hbm), channel_id=1, source_target_pairs={{0,1},{1,0},{2,3},{3,2},{4,5},{5,4},{6,7},{7,6},{8,9},{9,8},{10,11... | collective-permute-start | bytes 3538952 | tf_op jit(solution)/shard_map/ppermute | solution.py:357
  90.1 2.9 %collective-permute-done.14.other_ref = bf16[16,48,128]{2,1,0:T(8,128)(2,1)S(1)} collective-permute-done((bf16[16,48,128]{2,1,0:T(8,128)(2,1)S(1)}, bf16[16,48,128]{2,1,0:T(8,128)(2,1)S(1)}, u32[]{:S(2)}, u32[]{:S(2)}) %collective-permute-start.14) | collective-permute-done | bytes 196640 | tf_op jit(solution)/shard_map/ppermute | solution.py:357
  94.2 1.1 copy-done.7
  95.9 1.6 %collective-permute-start.15 = (bf16[768,128]{1,0:T(8,128)(2,1)S(1)}, bf16[768,128]{1,0:T(8,128)(2,1)S(1)}, u32[]{:S(2)}, u32[]{:S(2)}) collective-permute-start(bf16[768,128]{1,0:T(8,128)(2,1)S(1)} %shard_map.109), channel_id=1, source_target_pairs={{0,224},{1,33},{2,226},{3,35},{4,228},{5,37},{6,230},{7,39},{8,232... | collective-permute-start | bytes 589832 | tf_op jit(solution)/shard_map/ppermute | solution.py:366
  97.6 6.4 %collective-permute-done.15.back_ref = bf16[768,128]{1,0:T(8,128)(2,1)S(1)} collective-permute-done((bf16[768,128]{1,0:T(8,128)(2,1)S(1)}, bf16[768,128]{1,0:T(8,128)(2,1)S(1)}, u32[]{:S(2)}, u32[]{:S(2)}) %collective-permute-start.15) | collective-permute-done | bytes 196640 | tf_op jit(solution)/shard_map/ppermute | solution.py:366
  105.1 9.8 %all-to-all-start = ((bf16[16,48,128]{2,1,0:T(8,128)(2,1)}), bf16[16,48,128]{2,1,0:T(8,128)(2,1)S(1)}, u32[]{:S(2)}, u32[]{:S(2)}) async-start(bf16[16,48,128]{2,1,0:T(8,128)(2,1)} %bitcast.6), calls=%async_computation | async-start | bytes 393216 | tf_op jit(solution)/shard_map/all_to_all | solution.py:369
  115.0 5.6 %collective-permute-start.17 = (bf16[768,128]{1,0:T(8,128)(2,1)S(1)}, bf16[768,128]{1,0:T(8,128)(2,1)S(1)}, u32[]{:S(2)}, u32[]{:S(2)}) collective-permute-start(bf16[768,128]{1,0:T(8,128)(2,1)S(1)} %add_convert_fusion.1.w_ref), channel_id=1, source_target_pairs={{0,1},{1,0},{2,3},{3,2},{4,5},{5,4},{6,7},{7,6},{8,9},{9,8},{10,11... | collective-permute-start | bytes 589832 | tf_op jit(solution)/shard_map/ppermute | solution.py:357
  120.5 3.3 %all-to-all-done.got_ref = bf16[16,48,128]{2,1,0:T(8,128)(2,1)S(1)} async-done(((bf16[16,48,128]{2,1,0:T(8,128)(2,1)}), bf16[16,48,128]{2,1,0:T(8,128)(2,1)S(1)}, u32[]{:S(2)}, u32[]{:S(2)}) %all-to-all-start) | async-done | bytes 196640 | tf_op jit(solution)/shard_map/all_to_all | solution.py:369
  123.9 6.7 %collective-permute-start.11 = (f32[48,128]{1,0:T(8,128)S(1)}, f32[48,128]{1,0:T(8,128)S(1)}, u32[]{:S(2)}, u32[]{:S(2)}) collective-permute-start(f32[48,128]{1,0:T(8,128)S(1)} %shard_map.104.own_ref), channel_id=1, source_target_pairs={{0,1},{1,0},{2,3},{3,2},{4,5},{5,4},{6,7},{7,6},{8,9},{9,8},{10,11... | collective-permute-start | bytes 73736 | tf_op jit(solution)/shard_map/ppermute | solution.py:357
  133.1 11.5 %shard_map.111 = (bf16[1536,768]{1,0:T(8,128)(2,1)}, bf16[1536,768]{1,0:T(8,128)(2,1)}) custom-call(bf16[1536,768]{1,0:T(8,128)(2,1)} %bitcast.45, bf16[768,768]{1,0:T(8,128)(2,1)} %get-tuple-element.17.near_hbm, bf16[768,768]{1,0:T(8,128)(2,1)} %collective-permute-done.12.other_hbm, bf16[768,128]{1,0:T(8,128)(2,1)} %copy-done.15, ...), custom_call_target="tpu_custom_call" | custom-call | flops 3623878656 | bytes 8388608 | tf_op jit(solution)/shard_map/pallas_call | solution.py:471
  (70 shorter events, 10.3 us)
Async XLA Ops:
  5.3 8.0 %copy-start.1 = (f32[768,768]{1,0:T(8,128)}, f32[768,768]{1,0:T(8,128)S(1)}, u32[]{:S(2)}) copy-start(f32[768,768]{1,0:T(8,128)S(1)} %fusion.6.left_ref) | copy-start | bytes 7077892
  5.3 8.0 %copy-start.10 = (f32[1,24,768]{2,1,0:T(8,128)S(1)}, f32[1,24,768]{2,1,0:T(8,128)}, u32[]{:S(2)}) copy-start(f32[1,24,768]{2,1,0:T(8,128)} %param.12) | copy-start | bytes 221188
  5.3 8.0 %copy-start.11 = (f32[1,24,768]{2,1,0:T(8,128)S(1)}, f32[1,24,768]{2,1,0:T(8,128)}, u32[]{:S(2)}) copy-start(f32[1,24,768]{2,1,0:T(8,128)} %param.13) | copy-start | bytes 221188
  7.4 7.0 %copy-start.2 = (f32[768,768]{1,0:T(8,128)}, f32[768,768]{1,0:T(8,128)S(1)}, u32[]{:S(2)}) copy-start(f32[768,768]{1,0:T(8,128)S(1)} %get-tuple-element.25.right_ref) | copy-start | bytes 7077892
  7.4 5.8 %collective-permute-start.10 = (bf16[768,768]{1,0:T(8,128)(2,1)S(1)}, bf16[768,768]{1,0:T(8,128)(2,1)S(1)}, u32[]{:S(2)}, u32[]{:S(2)}) collective-permute-start(bf16[768,768]{1,0:T(8,128)(2,1)S(1)} %get-tuple-element.24), channel_id=1, source_target_pairs={{0,1},{1,0},{2,3},{3,2},{4,5},{5,4},{6,7},{7,6},{8,9},{9,8},{10,11... | collective-permute-start | bytes 3538952 | tf_op jit(solution)/shard_map/ppermute | solution.py:357
  10.7 2.5 %collective-permute-start.13 = (s32[1,768]{1,0:T(1,128)S(1)}, s32[1,768]{1,0:T(1,128)S(1)}, u32[]{:S(2)}, u32[]{:S(2)}) collective-permute-start(s32[1,768]{1,0:T(1,128)S(1)} %copy-done.8), channel_id=1, source_target_pairs={{0,32},{1,225},{2,34},{3,227},{4,36},{5,229},{6,38},{7,231},{8,40}... | collective-permute-start | bytes 9224 | tf_op jit(solution)/shard_map/ppermute | solution.py:366
  13.3 12.7 %copy-start.12 = (bf16[1,24,768]{2,1,0:T(8,128)(2,1)S(1)}, bf16[1,24,768]{2,1,0:T(8,128)(2,1)}, u32[]{:S(2)}) copy-start(bf16[1,24,768]{2,1,0:T(8,128)(2,1)} %param.7) | copy-start | bytes 110596
  15.3 30.4 %all-to-all-start.1 = ((bf16[16,48,512]{2,1,0:T(8,128)(2,1)}), bf16[16,48,512]{2,1,0:T(8,128)(2,1)S(1)}, u32[]{:S(2)}, u32[]{:S(2)}) async-start(bf16[16,48,512]{2,1,0:T(8,128)(2,1)} %bitcast.40), calls=%async_computation.1 | async-start | bytes 1572864 | tf_op jit(solution)/shard_map/all_to_all | solution.py:369
  26.0 3.1 %collective-permute-start = (bf16[24,768]{1,0:T(8,128)(2,1)S(1)}, bf16[24,768]{1,0:T(8,128)(2,1)S(1)}, u32[]{:S(2)}, u32[]{:S(2)}) collective-permute-start(bf16[24,768]{1,0:T(8,128)(2,1)S(1)} %bitcast.43), channel_id=1, source_target_pairs={{0,1},{1,0},{2,3},{3,2},{4,5},{5,4},{6,7},{7,6},{8,9},{9,8},{10,11... | collective-permute-start | bytes 110600 | tf_op jit(solution)/shard_map/ppermute | solution.py:357
  29.1 4.8 %collective-permute-start.1 = (bf16[48,768]{1,0:T(8,128)(2,1)S(1)}, bf16[48,768]{1,0:T(8,128)(2,1)S(1)}, u32[]{:S(2)}, u32[]{:S(2)}) collective-permute-start(bf16[48,768]{1,0:T(8,128)(2,1)S(1)} %shard_map.102), channel_id=1, source_target_pairs={{0,32},{1,225},{2,34},{3,227},{4,36},{5,229},{6,38},{7,231},{8,40}... | collective-permute-start | bytes 221192 | tf_op jit(solution)/shard_map/ppermute | solution.py:366
  33.9 5.6 %collective-permute-start.2 = (bf16[48,768]{1,0:T(8,128)(2,1)S(1)}, bf16[48,768]{1,0:T(8,128)(2,1)S(1)}, u32[]{:S(2)}, u32[]{:S(2)}) collective-permute-start(bf16[48,768]{1,0:T(8,128)(2,1)S(1)} %collective-permute-done.1), channel_id=1, source_target_pairs={{0,16},{1,17},{2,18},{3,19},{4,20},{5,21},{6,22},{7,23},{8,24},{9,... | collective-permute-start | bytes 221192 | tf_op jit(solution)/shard_map/ppermute | solution.py:419
  39.5 39.5 %copy-start.14 = (bf16[96,768]{1,0:T(8,128)(2,1)}, bf16[96,768]{1,0:T(8,128)(2,1)S(1)}, u32[]{:S(2)}) copy-start(bf16[96,768]{1,0:T(8,128)(2,1)S(1)} %constant_dynamic-update-slice_fusion.refs_0_) | copy-start | bytes 442372
  39.5 15.8 %collective-permute-start.3 = (bf16[96,768]{1,0:T(8,128)(2,1)S(1)}, bf16[96,768]{1,0:T(8,128)(2,1)}, u32[]{:S(2)}, u32[]{:S(2)}) collective-permute-start(bf16[96,768]{1,0:T(8,128)(2,1)S(1)} %constant_dynamic-update-slice_fusion.refs_0_), channel_id=1, source_target_pairs={{0,2},{1,3},{2,4},{3,5},{4,6},{5,7},{6,8},{7,9},{8,10},{9,11},{10,... | collective-permute-start | bytes 442376 | tf_op jit(solution)/shard_map/ppermute | solution.py:419
  46.6 47.6 %all-to-all-start.2 = ((bf16[16,48,384]{2,1,0:T(8,128)(2,1)}), bf16[16,48,384]{2,1,0:T(8,128)(2,1)S(1)}, u32[]{:S(2)}, u32[]{:S(2)}) async-start(bf16[16,48,384]{2,1,0:T(8,128)(2,1)} %copy-done.5), calls=%async_computation.2 | async-start | bytes 1179648 | tf_op jit(solution)/shard_map/all_to_all | solution.py:369
  52.7 16.3 %collective-permute-start.4 = (bf16[96,768]{1,0:T(8,128)(2,1)S(1)}, bf16[96,768]{1,0:T(8,128)(2,1)S(1)}, u32[]{:S(2)}, u32[]{:S(2)}) collective-permute-start(bf16[96,768]{1,0:T(8,128)(2,1)S(1)} %constant_dynamic-update-slice_fusion.refs_0_), channel_id=1, source_target_pairs={{0,14},{1,15},{2,0},{3,1},{4,2},{5,3},{6,4},{7,5},{8,6},{9,7},{10,... | collective-permute-start | bytes 442376 | tf_op jit(solution)/shard_map/ppermute | solution.py:419
  55.2 14.7 %collective-permute-start.5 = (bf16[96,768]{1,0:T(8,128)(2,1)}, bf16[96,768]{1,0:T(8,128)(2,1)S(1)}, u32[]{:S(2)}, u32[]{:S(2)}) collective-permute-start(bf16[96,768]{1,0:T(8,128)(2,1)} %collective-permute-done.3.refs_1_), channel_id=1, source_target_pairs={{0,2},{1,3},{2,4},{3,5},{4,6},{5,7},{6,8},{7,9},{8,10},{9,11},{10,... | collective-permute-start | bytes 442376 | tf_op jit(solution)/shard_map/ppermute | solution.py:419
  68.9 10.0 %copy-start.16 = (bf16[96,768]{1,0:T(8,128)(2,1)}, bf16[96,768]{1,0:T(8,128)(2,1)S(1)}, u32[]{:S(2)}) copy-start(bf16[96,768]{1,0:T(8,128)(2,1)S(1)} %collective-permute-done.4.refs_2_) | copy-start | bytes 442372
  68.9 4.3 %collective-permute-start.6 = (bf16[96,768]{1,0:T(8,128)(2,1)S(1)}, bf16[96,768]{1,0:T(8,128)(2,1)S(1)}, u32[]{:S(2)}, u32[]{:S(2)}) collective-permute-start(bf16[96,768]{1,0:T(8,128)(2,1)S(1)} %collective-permute-done.4.refs_2_), channel_id=1, source_target_pairs={{0,14},{1,15},{2,0},{3,1},{4,2},{5,3},{6,4},{7,5},{8,6},{9,7},{10,... | collective-permute-start | bytes 442376 | tf_op jit(solution)/shard_map/ppermute | solution.py:419
  69.9 9.0 %copy-start.17 = (bf16[96,768]{1,0:T(8,128)(2,1)}, bf16[96,768]{1,0:T(8,128)(2,1)S(1)}, u32[]{:S(2)}) copy-start(bf16[96,768]{1,0:T(8,128)(2,1)S(1)} %collective-permute-done.5.refs_3_) | copy-start | bytes 442372
  69.9 5.5 %collective-permute-start.7 = (bf16[96,768]{1,0:T(8,128)(2,1)S(1)}, bf16[96,768]{1,0:T(8,128)(2,1)S(1)}, u32[]{:S(2)}, u32[]{:S(2)}) collective-permute-start(bf16[96,768]{1,0:T(8,128)(2,1)S(1)} %collective-permute-done.5.refs_3_), channel_id=1, source_target_pairs={{0,2},{1,3},{2,4},{3,5},{4,6},{5,7},{6,8},{7,9},{8,10},{9,11},{10,... | collective-permute-start | bytes 442376 | tf_op jit(solution)/shard_map/ppermute | solution.py:419
  73.2 5.7 %copy-start.18 = (bf16[96,768]{1,0:T(8,128)(2,1)}, bf16[96,768]{1,0:T(8,128)(2,1)S(1)}, u32[]{:S(2)}) copy-start(bf16[96,768]{1,0:T(8,128)(2,1)S(1)} %collective-permute-done.6.refs_4_) | copy-start | bytes 442372
  73.2 5.8 %collective-permute-start.8 = (bf16[96,768]{1,0:T(8,128)(2,1)S(1)}, bf16[96,768]{1,0:T(8,128)(2,1)S(1)}, u32[]{:S(2)}, u32[]{:S(2)}) collective-permute-start(bf16[96,768]{1,0:T(8,128)(2,1)S(1)} %collective-permute-done.6.refs_4_), channel_id=1, source_target_pairs={{0,14},{1,15},{2,0},{3,1},{4,2},{5,3},{6,4},{7,5},{8,6},{9,7},{10,... | collective-permute-start | bytes 442376 | tf_op jit(solution)/shard_map/ppermute | solution.py:419
  75.5 5.3 %collective-permute-start.9 = (bf16[96,768]{1,0:T(8,128)(2,1)S(1)}, bf16[96,768]{1,0:T(8,128)(2,1)}, u32[]{:S(2)}, u32[]{:S(2)}) collective-permute-start(bf16[96,768]{1,0:T(8,128)(2,1)S(1)} %collective-permute-done.7.refs_5_), channel_id=1, source_target_pairs={{0,2},{1,3},{2,4},{3,5},{4,6},{5,7},{6,8},{7,9},{8,10},{9,11},{10,... | collective-permute-start | bytes 442376 | tf_op jit(solution)/shard_map/ppermute | solution.py:419
  79.0 14.0 %copy-start.9 = (s32[1,768]{1,0:T(1,128)S(1)}, s32[1,768]{1,0:T(1,128)}, u32[]{:S(2)}) copy-start(s32[1,768]{1,0:T(1,128)} %row_ref.9) | copy-start | bytes 9220
  84.7 47.7 %collective-permute-start.12 = (bf16[768,768]{1,0:T(8,128)(2,1)}, bf16[768,768]{1,0:T(8,128)(2,1)}, u32[]{:S(2)}, u32[]{:S(2)}) collective-permute-start(bf16[768,768]{1,0:T(8,128)(2,1)} %get-tuple-element.17.near_hbm), channel_id=1, source_target_pairs={{0,1},{1,0},{2,3},{3,2},{4,5},{5,4},{6,7},{7,6},{8,9},{9,8},{10,11... | collective-permute-start | bytes 3538952 | tf_op jit(solution)/shard_map/ppermute | solution.py:357
  90.0 3.0 %collective-permute-start.14 = (bf16[16,48,128]{2,1,0:T(8,128)(2,1)S(1)}, bf16[16,48,128]{2,1,0:T(8,128)(2,1)S(1)}, u32[]{:S(2)}, u32[]{:S(2)}) collective-permute-start(bf16[16,48,128]{2,1,0:T(8,128)(2,1)S(1)} %get-tuple-element.18.early_ref), channel_id=1, source_target_pairs={{0,1},{1,0},{2,3},{3,2},{4,5},{5,4},{6,7},{7,6},{8,9},{9,8},{10,11... | collective-permute-start | bytes 589832 | tf_op jit(solution)/shard_map/ppermute | solution.py:357
  95.9 8.1 %collective-permute-start.15 = (bf16[768,128]{1,0:T(8,128)(2,1)S(1)}, bf16[768,128]{1,0:T(8,128)(2,1)S(1)}, u32[]{:S(2)}, u32[]{:S(2)}) collective-permute-start(bf16[768,128]{1,0:T(8,128)(2,1)S(1)} %shard_map.109), channel_id=1, source_target_pairs={{0,224},{1,33},{2,226},{3,35},{4,228},{5,37},{6,230},{7,39},{8,232... | collective-permute-start | bytes 589832 | tf_op jit(solution)/shard_map/ppermute | solution.py:366
  104.8 10.0 %collective-permute-start.16 = (bf16[768,128]{1,0:T(8,128)(2,1)S(1)}, bf16[768,128]{1,0:T(8,128)(2,1)S(1)}, u32[]{:S(2)}, u32[]{:S(2)}) collective-permute-start(bf16[768,128]{1,0:T(8,128)(2,1)S(1)} %shard_map.110), channel_id=1, source_target_pairs={{0,224},{1,33},{2,226},{3,35},{4,228},{5,37},{6,230},{7,39},{8,232... | collective-permute-start | bytes 589832 | tf_op jit(solution)/shard_map/ppermute | solution.py:366
  105.1 18.7 %all-to-all-start = ((bf16[16,48,128]{2,1,0:T(8,128)(2,1)}), bf16[16,48,128]{2,1,0:T(8,128)(2,1)S(1)}, u32[]{:S(2)}, u32[]{:S(2)}) async-start(bf16[16,48,128]{2,1,0:T(8,128)(2,1)} %bitcast.6), calls=%async_computation | async-start | bytes 393216 | tf_op jit(solution)/shard_map/all_to_all | solution.py:369
  115.0 17.5 %copy-start.15 = (bf16[768,128]{1,0:T(8,128)(2,1)}, bf16[768,128]{1,0:T(8,128)(2,1)S(1)}, u32[]{:S(2)}) copy-start(bf16[768,128]{1,0:T(8,128)(2,1)S(1)} %add_convert_fusion.1.w_ref) | copy-start | bytes 589828
  115.0 17.4 %collective-permute-start.17 = (bf16[768,128]{1,0:T(8,128)(2,1)S(1)}, bf16[768,128]{1,0:T(8,128)(2,1)S(1)}, u32[]{:S(2)}, u32[]{:S(2)}) collective-permute-start(bf16[768,128]{1,0:T(8,128)(2,1)S(1)} %add_convert_fusion.1.w_ref), channel_id=1, source_target_pairs={{0,1},{1,0},{2,3},{3,2},{4,5},{5,4},{6,7},{7,6},{8,9},{9,8},{10,11... | collective-permute-start | bytes 589832 | tf_op jit(solution)/shard_map/ppermute | solution.py:357
  123.9 7.6 %collective-permute-start.11 = (f32[48,128]{1,0:T(8,128)S(1)}, f32[48,128]{1,0:T(8,128)S(1)}, u32[]{:S(2)}, u32[]{:S(2)}) collective-permute-start(f32[48,128]{1,0:T(8,128)S(1)} %shard_map.104.own_ref), channel_id=1, source_target_pairs={{0,1},{1,0},{2,3},{3,2},{4,5},{5,4},{6,7},{7,6},{8,9},{9,8},{10,11... | collective-permute-start | bytes 73736 | tf_op jit(solution)/shard_map/ppermute | solution.py:357
  (11 other events, 24.3 us)

commit v6 on v5

--- a/solution.py
+++ b/solution.py
@@ -202,35 +202,19 @@
         out_ref[lanes(i), :] = fold_tile(product, column(row, i), row, low, high)
 
 
-def total_kernel(got_ref, out_ref):
-    total = got_ref[0].astype(F32)
-    for q in range(1, got_ref.shape[0]):
-        total = total + got_ref[q].astype(F32)
-    out_ref[...] = total
-
-
-def open_kernel(own_ref, other_ref, row_ref, left_ref, right_ref):
+def open_kernel(got_ref, row_ref, left_ref, right_ref):
     rows, chi = left_ref.shape
     blk = lax.axis_index("blk")
-    core = lax.rem(blk, 2)
     row = label_row(row_ref)
     position = lax.broadcasted_iota(jnp.int32, (rows, chi), 1)
     wanted = blk * rows + lax.broadcasted_iota(jnp.int32, (rows, chi), 0)
     mask = jnp.sum(jnp.where(position == wanted, row, 0.0), axis=1, keepdims=True) == row
-
-    def put(out_ref, x):
-        wide = jnp.concatenate([x] * (chi // FOLD), axis=1)
+    for side, out_ref in enumerate((left_ref, right_ref)):
+        total = got_ref[side].astype(F32)
+        for q in range(side + 2, got_ref.shape[0], 2):
+            total = total + got_ref[q].astype(F32)
+        wide = jnp.concatenate([total] * (chi // FOLD), axis=1)
         out_ref[...] = jnp.where(mask, wide, 0.0).astype(BF16)
-
-    @pl.when(core == 0)
-    def _():
-        put(left_ref, own_ref[:rows, :])
-        put(right_ref, other_ref[:rows, :])
-
-    @pl.when(core == 1)
-    def _():
-        put(right_ref, own_ref[rows:, :])
-        put(left_ref, other_ref[rows:, :])
 
 
 def first_kernel(open_ref, enl_ref, to_row_ref, out_ref):
@@ -460,12 +444,10 @@
     w2 = (cot.astype(F32) + back2_at.astype(F32)).astype(BF16)
     w2_other = swap_cores(w2)
 
-    new_got = exchange(new_part.reshape(chips, pair_rows, FOLD))
-    new_sum = call(total_kernel, array(pair_rows, FOLD, dtype=F32), [VMEM], [], 0, 1 << 18)(new_got)
-    new_other = swap_cores(new_sum)
+    new_got = lax.all_to_all(new_part.reshape(members, rows, FOLD), "blk", 0, 0, tiled=True)
     new_left, new_right = call(
-        open_kernel, (array(rows, chi), array(rows, chi)), [VMEM] * 3, [], 0, 1 << 17, (VMEM, VMEM)
-    )(new_sum, new_other, row)
+        open_kernel, (array(rows, chi), array(rows, chi)), [VMEM] * 2, [], 0, 1 << 18, (VMEM, VMEM)
+    )(new_got, row)
 
     flat = array(rows * depth, chi)
     grad_left, grad_right = call(

time: 145 us -> 146 us (level)
  waiting for transfers between devices: 43 us -> 49.8 us
  starting transfers between devices: 65.9 us -> 59.7 us
    all_to_all x0 -> x1, starting transfers between devices: none -> 15.3 us  [body(): lax.all_to_all(new_part.reshape(members, rows, FOLD), 'blk', 0, 0, tiled=...]
    ppermute x6 -> x5, starting transfers between devices: 23.2 us -> 11.5 us  [swap_cores(): return lax.ppermute(x, 'blk', [(i, i ^ 1) for i in range(members)])]
    all_to_all x0 -> x1, waiting for transfers between devices: none -> 11 us  [body(): lax.all_to_all(new_part.reshape(members, rows, FOLD), 'blk', 0, 0, tiled=...]
    all_to_all x3 -> x2, starting transfers between devices: 26.4 us -> 16.7 us  [exchange(): return lax.all_to_all(x, 'blk', 0, 0, tiled=True, axis_index_groups=groups)]
    all_to_all x3 -> x2, waiting for transfers between devices: 7.59 us -> 4.25 us  [exchange(): return lax.all_to_all(x, 'blk', 0, 0, tiled=True, axis_index_groups=groups)]
    ppermute x6 -> x5, waiting for transfers between devices: 4.59 us -> 3.74 us  [swap_cores(): return lax.ppermute(x, 'blk', [(i, i ^ 1) for i in range(members)])]
  transfers between devices with their start and end apart: 21 -> 20, of which waited for: 12 -> 11; matrix products, arithmetic and copies ran while one was open for 2% -> 2% of each run, Pallas kernels for 5% -> 5%
where the time goes in v6:
time: 146 us; the launch traced here: 145 us
  starting transfers between devices  59.7 us (41%)
  waiting for transfers between devices  49.8 us (34%)
  Pallas kernels  19.2 us (13%)
  matrix products  6.66 us (5%)
  local copies, waits for them, and re-layouts  4.98 us (3%)
  other arithmetic  3.57 us (2%)
    ppermute x8, waiting for transfers between devices, ring_move(): lax.ppermute(x, 'blk', [(i, turn(i, dy, dz)) for i in range(members)])  20.2 us
    all_to_all x2, starting transfers between devices, exchange(): return lax.all_to_all(x, 'blk', 0, 0, tiled=True, axis_index_groups=groups)  16.7 us
    all_to_all x1, starting transfers between devices, body(): lax.all_to_all(new_part.reshape(members, rows, FOLD), 'blk', 0, 0, tiled=...  15.3 us
    pallas_call x1, Pallas kernels, body(): call(grad_kernel, (flat, flat), [HBM] * 3 + [VMEM] * 3, [pltpu.VMEM((rows...  11.5 us
    ppermute x5, starting transfers between devices, swap_cores(): return lax.ppermute(x, 'blk', [(i, i ^ 1) for i in range(members)])  11.5 us
    ppermute x8, starting transfers between devices, ring_move(): lax.ppermute(x, 'blk', [(i, turn(i, dy, dz)) for i in range(members)])  11.2 us
    all_to_all x1, waiting for transfers between devices, body(): lax.all_to_all(new_part.reshape(members, rows, FOLD), 'blk', 0, 0, tiled=...  11 us
    ppermute x4, waiting for transfers between devices, site_move(): return lax.ppermute(x, ('site', 'blk'), route)  10.6 us
  transfers between devices with their start and end apart: 20, of which 11 were waited for; matrix products, arithmetic and copies ran while one was open for 2% of the time, Pallas kernels for 5%

profile of v6, /device:TPU:1, one launch (start us, length us, event | category | flops | bytes accessed | tf_op | source)
XLA Modules:
  0.0 145.1 jit_solution(3329918885668906815)
XLA Ops:
  0.7 4.6 %fusion.6.left_ref = f32[768,768]{1,0:T(8,128)S(1)} fusion(bf16[1,24,64,768]{3,2,1,0:T(8,128)(2,1)} %param.9, bf16[1,24,64,768]{3,2,1,0:T(8,128)(2,1)} %param.8), kind=kOutput, calls=%fused_computation.8 | convolution fusion | flops 1811939328 | bytes 7077888 | tf_op jit(solution)/shard_map/dot_general | solution.py:20
  5.3 2.1 %select_convert_fusion = (bf16[768,768]{1,0:T(8,128)(2,1)S(1)}, f32[768,768]{1,0:T(8,128)S(1)}) fusion(f32[768,768]{1,0:T(8,128)S(1)} %fusion.6.left_ref, pred[]{:T(512)S(6)} %eq.5, bf16[1,24,64,768]{3,2,1,0:T(8,128)(2,1)S(1)} %copy-done, bf16[1,24,64,768]{3,2,1,0:T(8,128)(2,1)S(1)} %copy-done.13), kind=kOutput, calls=%fused_computation.7 | convolution fusion | flops 1812529152 | bytes 10616833 | tf_op jit(solution)/shard_map/dot_general | solution.py:20
  7.4 3.3 %collective-permute-start.10 = (bf16[768,768]{1,0:T(8,128)(2,1)S(1)}, bf16[768,768]{1,0:T(8,128)(2,1)S(1)}, u32[]{:S(2)}, u32[]{:S(2)}) collective-permute-start(bf16[768,768]{1,0:T(8,128)(2,1)S(1)} %get-tuple-element.24), channel_id=1, source_target_pairs={{0,1},{1,0},{2,3},{3,2},{4,5},{5,4},{6,7},{7,6},{8,9},{9,8},{10,11... | collective-permute-start | bytes 3538952 | tf_op jit(solution)/shard_map/ppermute | solution.py:341
  10.7 1.8 %collective-permute-start.12 = (s32[1,768]{1,0:T(1,128)S(1)}, s32[1,768]{1,0:T(1,128)S(1)}, u32[]{:S(2)}, u32[]{:S(2)}) collective-permute-start(s32[1,768]{1,0:T(1,128)S(1)} %copy-done.8), channel_id=1, source_target_pairs={{0,32},{1,225},{2,34},{3,227},{4,36},{5,229},{6,38},{7,231},{8,40}... | collective-permute-start | bytes 9224 | tf_op jit(solution)/shard_map/ppermute | solution.py:350
  13.3 1.1 shard_map.105
  14.4 0.9 copy-done.4
  15.3 10.6 %all-to-all-start.1 = ((bf16[16,48,512]{2,1,0:T(8,128)(2,1)}), bf16[16,48,512]{2,1,0:T(8,128)(2,1)S(1)}, u32[]{:S(2)}, u32[]{:S(2)}) async-start(bf16[16,48,512]{2,1,0:T(8,128)(2,1)} %bitcast.40), calls=%async_computation.1 | async-start | bytes 1572864 | tf_op jit(solution)/shard_map/all_to_all | solution.py:353
  25.9 2.2 %collective-permute-start = (bf16[24,768]{1,0:T(8,128)(2,1)S(1)}, bf16[24,768]{1,0:T(8,128)(2,1)S(1)}, u32[]{:S(2)}, u32[]{:S(2)}) collective-permute-start(bf16[24,768]{1,0:T(8,128)(2,1)S(1)} %bitcast.43), channel_id=1, source_target_pairs={{0,1},{1,0},{2,3},{3,2},{4,5},{5,4},{6,7},{7,6},{8,9},{9,8},{10,11... | collective-permute-start | bytes 110600 | tf_op jit(solution)/shard_map/ppermute | solution.py:341
  28.2 0.9 collective-permute-done.other_ref
  29.1 1.4 collective-permute-start.1
  30.5 3.4 %collective-permute-done.1 = bf16[48,768]{1,0:T(8,128)(2,1)S(1)} collective-permute-done((bf16[48,768]{1,0:T(8,128)(2,1)S(1)}, bf16[48,768]{1,0:T(8,128)(2,1)S(1)}, u32[]{:S(2)}, u32[]{:S(2)}) %collective-permute-start.1) | collective-permute-done | bytes 73760 | tf_op jit(solution)/shard_map/ppermute | solution.py:350
  33.9 3.0 %collective-permute-start.2 = (bf16[48,768]{1,0:T(8,128)(2,1)S(1)}, bf16[48,768]{1,0:T(8,128)(2,1)S(1)}, u32[]{:S(2)}, u32[]{:S(2)}) collective-permute-start(bf16[48,768]{1,0:T(8,128)(2,1)S(1)} %collective-permute-done.1), channel_id=1, source_target_pairs={{0,16},{1,17},{2,18},{3,19},{4,20},{5,21},{6,22},{7,23},{8,24},{9,... | collective-permute-start | bytes 221192 | tf_op jit(solution)/shard_map/ppermute | solution.py:403
  36.8 2.6 %collective-permute-done.2 = bf16[48,768]{1,0:T(8,128)(2,1)S(1)} collective-permute-done((bf16[48,768]{1,0:T(8,128)(2,1)S(1)}, bf16[48,768]{1,0:T(8,128)(2,1)S(1)}, u32[]{:S(2)}, u32[]{:S(2)}) %collective-permute-start.2) | collective-permute-done | bytes 73760 | tf_op jit(solution)/shard_map/ppermute | solution.py:403
  39.5 2.0 %collective-permute-start.3 = (bf16[96,768]{1,0:T(8,128)(2,1)S(1)}, bf16[96,768]{1,0:T(8,128)(2,1)}, u32[]{:S(2)}, u32[]{:S(2)}) collective-permute-start(bf16[96,768]{1,0:T(8,128)(2,1)S(1)} %constant_dynamic-update-slice_fusion.refs_0_), channel_id=1, source_target_pairs={{0,2},{1,3},{2,4},{3,5},{4,6},{5,7},{6,8},{7,9},{8,10},{9,11},{10,... | collective-permute-start | bytes 442376 | tf_op jit(solution)/shard_map/ppermute | solution.py:403
  41.4 4.2 %all-to-all-done.1.got_ref = bf16[16,48,512]{2,1,0:T(8,128)(2,1)S(1)} async-done(((bf16[16,48,512]{2,1,0:T(8,128)(2,1)}), bf16[16,48,512]{2,1,0:T(8,128)(2,1)S(1)}, u32[]{:S(2)}, u32[]{:S(2)}) %all-to-all-start.1) | async-done | bytes 786464 | tf_op jit(solution)/shard_map/all_to_all | solution.py:353
  46.6 6.1 %all-to-all-start.2 = ((bf16[16,48,384]{2,1,0:T(8,128)(2,1)}), bf16[16,48,384]{2,1,0:T(8,128)(2,1)S(1)}, u32[]{:S(2)}, u32[]{:S(2)}) async-start(bf16[16,48,384]{2,1,0:T(8,128)(2,1)} %copy-done.5), calls=%async_computation.2 | async-start | bytes 1179648 | tf_op jit(solution)/shard_map/all_to_all | solution.py:353
  52.7 2.6 %collective-permute-start.4 = (bf16[96,768]{1,0:T(8,128)(2,1)S(1)}, bf16[96,768]{1,0:T(8,128)(2,1)S(1)}, u32[]{:S(2)}, u32[]{:S(2)}) collective-permute-start(bf16[96,768]{1,0:T(8,128)(2,1)S(1)} %constant_dynamic-update-slice_fusion.refs_0_), channel_id=1, source_target_pairs={{0,14},{1,15},{2,0},{3,1},{4,2},{5,3},{6,4},{7,5},{8,6},{9,7},{10,... | collective-permute-start | bytes 442376 | tf_op jit(solution)/shard_map/ppermute | solution.py:403
  55.2 13.7 %collective-permute-done.4.refs_2_ = bf16[96,768]{1,0:T(8,128)(2,1)S(1)} collective-permute-done((bf16[96,768]{1,0:T(8,128)(2,1)S(1)}, bf16[96,768]{1,0:T(8,128)(2,1)S(1)}, u32[]{:S(2)}, u32[]{:S(2)}) %collective-permute-start.4) | collective-permute-done | bytes 147488 | tf_op jit(solution)/shard_map/ppermute | solution.py:403
  68.9 1.0 collective-permute-start.6
  70.4 2.8 %collective-permute-done.6.refs_4_ = bf16[96,768]{1,0:T(8,128)(2,1)S(1)} collective-permute-done((bf16[96,768]{1,0:T(8,128)(2,1)S(1)}, bf16[96,768]{1,0:T(8,128)(2,1)S(1)}, u32[]{:S(2)}, u32[]{:S(2)}) %collective-permute-start.6) | collective-permute-done | bytes 147488 | tf_op jit(solution)/shard_map/ppermute | solution.py:403
  73.2 2.2 %collective-permute-start.8 = (bf16[96,768]{1,0:T(8,128)(2,1)S(1)}, bf16[96,768]{1,0:T(8,128)(2,1)S(1)}, u32[]{:S(2)}, u32[]{:S(2)}) collective-permute-start(bf16[96,768]{1,0:T(8,128)(2,1)S(1)} %collective-permute-done.6.refs_4_), channel_id=1, source_target_pairs={{0,14},{1,15},{2,0},{3,1},{4,2},{5,3},{6,4},{7,5},{8,6},{9,7},{10,... | collective-permute-start | bytes 442376 | tf_op jit(solution)/shard_map/ppermute | solution.py:403
  75.5 3.5 %add_convert_fusion.refs_8_ = bf16[768,768]{1,0:T(8,128)(2,1)} fusion(bf16[768,768]{1,0:T(8,128)(2,1)} %copy-done.3, f32[768,768]{1,0:T(8,128)} %copy-done.1, f32[768,768]{1,0:T(8,128)} %copy-done.2, pred[]{:T(512)S(6)} %eq.5), kind=kLoop, calls=%fused_computation.6 | loop fusion | flops 2359296 | bytes 7077889 | tf_op jit(solution)/shard_map/convert_element_type | solution.py:374
  79.7 1.1 collective-permute-done.9.refs_7_
  80.8 3.9 %shard_map.103 = (bf16[768,768]{1,0:T(8,128)(2,1)}, bf16[768,128]{1,0:T(8,128)(2,1)}) custom-call(bf16[96,768]{1,0:T(8,128)(2,1)} %copy-done.14, bf16[96,768]{1,0:T(8,128)(2,1)} %collective-permute-done.3.refs_1_, bf16[96,768]{1,0:T(8,128)(2,1)} %copy-done.16, bf16[96,768]{1,0:T(8,128)(2,1)} %copy-done.17, bf16[96,768]{1,0:T(8,128)(2,1)} %copy-done.18, ...), custom_call_target="tpu_custom_call" | custom-call | flops 452984832 | bytes 3145728 | tf_op jit(solution)/shard_map/pallas_call | solution.py:414
  84.7 5.3 %collective-permute-start.11 = (bf16[768,768]{1,0:T(8,128)(2,1)}, bf16[768,768]{1,0:T(8,128)(2,1)}, u32[]{:S(2)}, u32[]{:S(2)}) collective-permute-start(bf16[768,768]{1,0:T(8,128)(2,1)} %get-tuple-element.17.near_hbm), channel_id=1, source_target_pairs={{0,1},{1,0},{2,3},{3,2},{4,5},{5,4},{6,7},{7,6},{8,9},{9,8},{10,11... | collective-permute-start | bytes 3538952 | tf_op jit(solution)/shard_map/ppermute | solution.py:341
  90.1 2.9 %collective-permute-done.13.other_ref = bf16[16,48,128]{2,1,0:T(8,128)(2,1)S(1)} collective-permute-done((bf16[16,48,128]{2,1,0:T(8,128)(2,1)S(1)}, bf16[16,48,128]{2,1,0:T(8,128)(2,1)S(1)}, u32[]{:S(2)}, u32[]{:S(2)}) %collective-permute-start.13) | collective-permute-done | bytes 196640 | tf_op jit(solution)/shard_map/ppermute | solution.py:341
  94.2 1.1 copy-done.7
  95.9 1.6 %collective-permute-start.14 = (bf16[768,128]{1,0:T(8,128)(2,1)S(1)}, bf16[768,128]{1,0:T(8,128)(2,1)S(1)}, u32[]{:S(2)}, u32[]{:S(2)}) collective-permute-start(bf16[768,128]{1,0:T(8,128)(2,1)S(1)} %shard_map.108), channel_id=1, source_target_pairs={{0,224},{1,33},{2,226},{3,35},{4,228},{5,37},{6,230},{7,39},{8,232... | collective-permute-start | bytes 589832 | tf_op jit(solution)/shard_map/ppermute | solution.py:350
  97.6 6.4 %collective-permute-done.14.back_ref = bf16[768,128]{1,0:T(8,128)(2,1)S(1)} collective-permute-done((bf16[768,128]{1,0:T(8,128)(2,1)S(1)}, bf16[768,128]{1,0:T(8,128)(2,1)S(1)}, u32[]{:S(2)}, u32[]{:S(2)}) %collective-permute-start.14) | collective-permute-done | bytes 196640 | tf_op jit(solution)/shard_map/ppermute | solution.py:350
  105.1 15.3 %all-to-all-start = ((bf16[32,24,128]{2,1,0:T(8,128)(2,1)}), bf16[32,24,128]{2,1,0:T(8,128)(2,1)S(1)}, u32[]{:S(2)}, u32[]{:S(2)}) async-start(bf16[32,24,128]{2,1,0:T(8,128)(2,1)} %bitcast.6), calls=%async_computation | async-start | bytes 393216 | tf_op jit(solution)/shard_map/all_to_all | solution.py:447
  121.0 11.0 %all-to-all-done.got_ref = bf16[32,24,128]{2,1,0:T(8,128)(2,1)S(1)} async-done(((bf16[32,24,128]{2,1,0:T(8,128)(2,1)}), bf16[32,24,128]{2,1,0:T(8,128)(2,1)S(1)}, u32[]{:S(2)}, u32[]{:S(2)}) %all-to-all-start) | async-done | bytes 196640 | tf_op jit(solution)/shard_map/all_to_all | solution.py:447
  133.4 11.5 %shard_map.110 = (bf16[1536,768]{1,0:T(8,128)(2,1)}, bf16[1536,768]{1,0:T(8,128)(2,1)}) custom-call(bf16[1536,768]{1,0:T(8,128)(2,1)} %bitcast.45, bf16[768,768]{1,0:T(8,128)(2,1)} %get-tuple-element.17.near_hbm, bf16[768,768]{1,0:T(8,128)(2,1)} %collective-permute-done.11.other_hbm, bf16[768,128]{1,0:T(8,128)(2,1)} %copy-done.15, ...), custom_call_target="tpu_custom_call" | custom-call | flops 3623878656 | bytes 8388608 | tf_op jit(solution)/shard_map/pallas_call | solution.py:453
  (67 shorter events, 8.0 us)
Async XLA Ops:
  5.3 8.0 %copy-start.1 = (f32[768,768]{1,0:T(8,128)}, f32[768,768]{1,0:T(8,128)S(1)}, u32[]{:S(2)}) copy-start(f32[768,768]{1,0:T(8,128)S(1)} %fusion.6.left_ref) | copy-start | bytes 7077892
  5.3 5.4 %copy-start.8 = (s32[1,768]{1,0:T(1,128)S(1)}, s32[1,768]{1,0:T(1,128)}, u32[]{:S(2)}) copy-start(s32[1,768]{1,0:T(1,128)} %row_ref.9) | copy-start | bytes 9220
  5.3 8.0 %copy-start.10 = (f32[1,24,768]{2,1,0:T(8,128)S(1)}, f32[1,24,768]{2,1,0:T(8,128)}, u32[]{:S(2)}) copy-start(f32[1,24,768]{2,1,0:T(8,128)} %param.12) | copy-start | bytes 221188
  5.3 8.0 %copy-start.11 = (f32[1,24,768]{2,1,0:T(8,128)S(1)}, f32[1,24,768]{2,1,0:T(8,128)}, u32[]{:S(2)}) copy-start(f32[1,24,768]{2,1,0:T(8,128)} %param.13) | copy-start | bytes 221188
  7.4 7.0 %copy-start.2 = (f32[768,768]{1,0:T(8,128)}, f32[768,768]{1,0:T(8,128)S(1)}, u32[]{:S(2)}) copy-start(f32[768,768]{1,0:T(8,128)S(1)} %get-tuple-element.25.right_ref) | copy-start | bytes 7077892
  7.4 5.8 %collective-permute-start.10 = (bf16[768,768]{1,0:T(8,128)(2,1)S(1)}, bf16[768,768]{1,0:T(8,128)(2,1)S(1)}, u32[]{:S(2)}, u32[]{:S(2)}) collective-permute-start(bf16[768,768]{1,0:T(8,128)(2,1)S(1)} %get-tuple-element.24), channel_id=1, source_target_pairs={{0,1},{1,0},{2,3},{3,2},{4,5},{5,4},{6,7},{7,6},{8,9},{9,8},{10,11... | collective-permute-start | bytes 3538952 | tf_op jit(solution)/shard_map/ppermute | solution.py:341
  10.7 2.5 %collective-permute-start.12 = (s32[1,768]{1,0:T(1,128)S(1)}, s32[1,768]{1,0:T(1,128)S(1)}, u32[]{:S(2)}, u32[]{:S(2)}) collective-permute-start(s32[1,768]{1,0:T(1,128)S(1)} %copy-done.8), channel_id=1, source_target_pairs={{0,32},{1,225},{2,34},{3,227},{4,36},{5,229},{6,38},{7,231},{8,40}... | collective-permute-start | bytes 9224 | tf_op jit(solution)/shard_map/ppermute | solution.py:350
  13.3 12.7 %copy-start.12 = (bf16[1,24,768]{2,1,0:T(8,128)(2,1)S(1)}, bf16[1,24,768]{2,1,0:T(8,128)(2,1)}, u32[]{:S(2)}) copy-start(bf16[1,24,768]{2,1,0:T(8,128)(2,1)} %param.7) | copy-start | bytes 110596
  15.3 30.4 %all-to-all-start.1 = ((bf16[16,48,512]{2,1,0:T(8,128)(2,1)}), bf16[16,48,512]{2,1,0:T(8,128)(2,1)S(1)}, u32[]{:S(2)}, u32[]{:S(2)}) async-start(bf16[16,48,512]{2,1,0:T(8,128)(2,1)} %bitcast.40), calls=%async_computation.1 | async-start | bytes 1572864 | tf_op jit(solution)/shard_map/all_to_all | solution.py:353
  25.9 3.1 %collective-permute-start = (bf16[24,768]{1,0:T(8,128)(2,1)S(1)}, bf16[24,768]{1,0:T(8,128)(2,1)S(1)}, u32[]{:S(2)}, u32[]{:S(2)}) collective-permute-start(bf16[24,768]{1,0:T(8,128)(2,1)S(1)} %bitcast.43), channel_id=1, source_target_pairs={{0,1},{1,0},{2,3},{3,2},{4,5},{5,4},{6,7},{7,6},{8,9},{9,8},{10,11... | collective-permute-start | bytes 110600 | tf_op jit(solution)/shard_map/ppermute | solution.py:341
  29.1 4.8 %collective-permute-start.1 = (bf16[48,768]{1,0:T(8,128)(2,1)S(1)}, bf16[48,768]{1,0:T(8,128)(2,1)S(1)}, u32[]{:S(2)}, u32[]{:S(2)}) collective-permute-start(bf16[48,768]{1,0:T(8,128)(2,1)S(1)} %shard_map.102), channel_id=1, source_target_pairs={{0,32},{1,225},{2,34},{3,227},{4,36},{5,229},{6,38},{7,231},{8,40}... | collective-permute-start | bytes 221192 | tf_op jit(solution)/shard_map/ppermute | solution.py:350
  33.9 5.6 %collective-permute-start.2 = (bf16[48,768]{1,0:T(8,128)(2,1)S(1)}, bf16[48,768]{1,0:T(8,128)(2,1)S(1)}, u32[]{:S(2)}, u32[]{:S(2)}) collective-permute-start(bf16[48,768]{1,0:T(8,128)(2,1)S(1)} %collective-permute-done.1), channel_id=1, source_target_pairs={{0,16},{1,17},{2,18},{3,19},{4,20},{5,21},{6,22},{7,23},{8,24},{9,... | collective-permute-start | bytes 221192 | tf_op jit(solution)/shard_map/ppermute | solution.py:403
  39.4 39.5 %copy-start.14 = (bf16[96,768]{1,0:T(8,128)(2,1)}, bf16[96,768]{1,0:T(8,128)(2,1)S(1)}, u32[]{:S(2)}) copy-start(bf16[96,768]{1,0:T(8,128)(2,1)S(1)} %constant_dynamic-update-slice_fusion.refs_0_) | copy-start | bytes 442372
  39.5 15.8 %collective-permute-start.3 = (bf16[96,768]{1,0:T(8,128)(2,1)S(1)}, bf16[96,768]{1,0:T(8,128)(2,1)}, u32[]{:S(2)}, u32[]{:S(2)}) collective-permute-start(bf16[96,768]{1,0:T(8,128)(2,1)S(1)} %constant_dynamic-update-slice_fusion.refs_0_), channel_id=1, source_target_pairs={{0,2},{1,3},{2,4},{3,5},{4,6},{5,7},{6,8},{7,9},{8,10},{9,11},{10,... | collective-permute-start | bytes 442376 | tf_op jit(solution)/shard_map/ppermute | solution.py:403
  46.6 47.6 %all-to-all-start.2 = ((bf16[16,48,384]{2,1,0:T(8,128)(2,1)}), bf16[16,48,384]{2,1,0:T(8,128)(2,1)S(1)}, u32[]{:S(2)}, u32[]{:S(2)}) async-start(bf16[16,48,384]{2,1,0:T(8,128)(2,1)} %copy-done.5), calls=%async_computation.2 | async-start | bytes 1179648 | tf_op jit(solution)/shard_map/all_to_all | solution.py:353
  52.7 16.3 %collective-permute-start.4 = (bf16[96,768]{1,0:T(8,128)(2,1)S(1)}, bf16[96,768]{1,0:T(8,128)(2,1)S(1)}, u32[]{:S(2)}, u32[]{:S(2)}) collective-permute-start(bf16[96,768]{1,0:T(8,128)(2,1)S(1)} %constant_dynamic-update-slice_fusion.refs_0_), channel_id=1, source_target_pairs={{0,14},{1,15},{2,0},{3,1},{4,2},{5,3},{6,4},{7,5},{8,6},{9,7},{10,... | collective-permute-start | bytes 442376 | tf_op jit(solution)/shard_map/ppermute | solution.py:403
  55.2 14.7 %collective-permute-start.5 = (bf16[96,768]{1,0:T(8,128)(2,1)}, bf16[96,768]{1,0:T(8,128)(2,1)S(1)}, u32[]{:S(2)}, u32[]{:S(2)}) collective-permute-start(bf16[96,768]{1,0:T(8,128)(2,1)} %collective-permute-done.3.refs_1_), channel_id=1, source_target_pairs={{0,2},{1,3},{2,4},{3,5},{4,6},{5,7},{6,8},{7,9},{8,10},{9,11},{10,... | collective-permute-start | bytes 442376 | tf_op jit(solution)/shard_map/ppermute | solution.py:403
  68.9 10.0 %copy-start.16 = (bf16[96,768]{1,0:T(8,128)(2,1)}, bf16[96,768]{1,0:T(8,128)(2,1)S(1)}, u32[]{:S(2)}) copy-start(bf16[96,768]{1,0:T(8,128)(2,1)S(1)} %collective-permute-done.4.refs_2_) | copy-start | bytes 442372
  68.9 4.3 %collective-permute-start.6 = (bf16[96,768]{1,0:T(8,128)(2,1)S(1)}, bf16[96,768]{1,0:T(8,128)(2,1)S(1)}, u32[]{:S(2)}, u32[]{:S(2)}) collective-permute-start(bf16[96,768]{1,0:T(8,128)(2,1)S(1)} %collective-permute-done.4.refs_2_), channel_id=1, source_target_pairs={{0,14},{1,15},{2,0},{3,1},{4,2},{5,3},{6,4},{7,5},{8,6},{9,7},{10,... | collective-permute-start | bytes 442376 | tf_op jit(solution)/shard_map/ppermute | solution.py:403
  69.9 9.0 %copy-start.17 = (bf16[96,768]{1,0:T(8,128)(2,1)}, bf16[96,768]{1,0:T(8,128)(2,1)S(1)}, u32[]{:S(2)}) copy-start(bf16[96,768]{1,0:T(8,128)(2,1)S(1)} %collective-permute-done.5.refs_3_) | copy-start | bytes 442372
  69.9 5.5 %collective-permute-start.7 = (bf16[96,768]{1,0:T(8,128)(2,1)S(1)}, bf16[96,768]{1,0:T(8,128)(2,1)S(1)}, u32[]{:S(2)}, u32[]{:S(2)}) collective-permute-start(bf16[96,768]{1,0:T(8,128)(2,1)S(1)} %collective-permute-done.5.refs_3_), channel_id=1, source_target_pairs={{0,2},{1,3},{2,4},{3,5},{4,6},{5,7},{6,8},{7,9},{8,10},{9,11},{10,... | collective-permute-start | bytes 442376 | tf_op jit(solution)/shard_map/ppermute | solution.py:403
  73.2 5.7 %copy-start.18 = (bf16[96,768]{1,0:T(8,128)(2,1)}, bf16[96,768]{1,0:T(8,128)(2,1)S(1)}, u32[]{:S(2)}) copy-start(bf16[96,768]{1,0:T(8,128)(2,1)S(1)} %collective-permute-done.6.refs_4_) | copy-start | bytes 442372
  73.2 5.8 %collective-permute-start.8 = (bf16[96,768]{1,0:T(8,128)(2,1)S(1)}, bf16[96,768]{1,0:T(8,128)(2,1)S(1)}, u32[]{:S(2)}, u32[]{:S(2)}) collective-permute-start(bf16[96,768]{1,0:T(8,128)(2,1)S(1)} %collective-permute-done.6.refs_4_), channel_id=1, source_target_pairs={{0,14},{1,15},{2,0},{3,1},{4,2},{5,3},{6,4},{7,5},{8,6},{9,7},{10,... | collective-permute-start | bytes 442376 | tf_op jit(solution)/shard_map/ppermute | solution.py:403
  75.4 5.3 %collective-permute-start.9 = (bf16[96,768]{1,0:T(8,128)(2,1)S(1)}, bf16[96,768]{1,0:T(8,128)(2,1)}, u32[]{:S(2)}, u32[]{:S(2)}) collective-permute-start(bf16[96,768]{1,0:T(8,128)(2,1)S(1)} %collective-permute-done.7.refs_5_), channel_id=1, source_target_pairs={{0,2},{1,3},{2,4},{3,5},{4,6},{5,7},{6,8},{7,9},{8,10},{9,11},{10,... | collective-permute-start | bytes 442376 | tf_op jit(solution)/shard_map/ppermute | solution.py:403
  79.0 14.0 %copy-start.9 = (s32[1,768]{1,0:T(1,128)S(1)}, s32[1,768]{1,0:T(1,128)}, u32[]{:S(2)}) copy-start(s32[1,768]{1,0:T(1,128)} %row_ref.9) | copy-start | bytes 9220
  84.7 48.1 %collective-permute-start.11 = (bf16[768,768]{1,0:T(8,128)(2,1)}, bf16[768,768]{1,0:T(8,128)(2,1)}, u32[]{:S(2)}, u32[]{:S(2)}) collective-permute-start(bf16[768,768]{1,0:T(8,128)(2,1)} %get-tuple-element.17.near_hbm), channel_id=1, source_target_pairs={{0,1},{1,0},{2,3},{3,2},{4,5},{5,4},{6,7},{7,6},{8,9},{9,8},{10,11... | collective-permute-start | bytes 3538952 | tf_op jit(solution)/shard_map/ppermute | solution.py:341
  90.0 3.0 %collective-permute-start.13 = (bf16[16,48,128]{2,1,0:T(8,128)(2,1)S(1)}, bf16[16,48,128]{2,1,0:T(8,128)(2,1)S(1)}, u32[]{:S(2)}, u32[]{:S(2)}) collective-permute-start(bf16[16,48,128]{2,1,0:T(8,128)(2,1)S(1)} %get-tuple-element.18.early_ref), channel_id=1, source_target_pairs={{0,1},{1,0},{2,3},{3,2},{4,5},{5,4},{6,7},{7,6},{8,9},{9,8},{10,11... | collective-permute-start | bytes 589832 | tf_op jit(solution)/shard_map/ppermute | solution.py:341
  95.9 8.1 %collective-permute-start.14 = (bf16[768,128]{1,0:T(8,128)(2,1)S(1)}, bf16[768,128]{1,0:T(8,128)(2,1)S(1)}, u32[]{:S(2)}, u32[]{:S(2)}) collective-permute-start(bf16[768,128]{1,0:T(8,128)(2,1)S(1)} %shard_map.108), channel_id=1, source_target_pairs={{0,224},{1,33},{2,226},{3,35},{4,228},{5,37},{6,230},{7,39},{8,232... | collective-permute-start | bytes 589832 | tf_op jit(solution)/shard_map/ppermute | solution.py:350
  104.8 15.6 %collective-permute-start.15 = (bf16[768,128]{1,0:T(8,128)(2,1)S(1)}, bf16[768,128]{1,0:T(8,128)(2,1)S(1)}, u32[]{:S(2)}, u32[]{:S(2)}) collective-permute-start(bf16[768,128]{1,0:T(8,128)(2,1)S(1)} %shard_map.109), channel_id=1, source_target_pairs={{0,224},{1,33},{2,226},{3,35},{4,228},{5,37},{6,230},{7,39},{8,232... | collective-permute-start | bytes 589832 | tf_op jit(solution)/shard_map/ppermute | solution.py:350
  105.1 26.9 %all-to-all-start = ((bf16[32,24,128]{2,1,0:T(8,128)(2,1)}), bf16[32,24,128]{2,1,0:T(8,128)(2,1)S(1)}, u32[]{:S(2)}, u32[]{:S(2)}) async-start(bf16[32,24,128]{2,1,0:T(8,128)(2,1)} %bitcast.6), calls=%async_computation | async-start | bytes 393216 | tf_op jit(solution)/shard_map/all_to_all | solution.py:447
  120.5 12.3 %copy-start.15 = (bf16[768,128]{1,0:T(8,128)(2,1)}, bf16[768,128]{1,0:T(8,128)(2,1)S(1)}, u32[]{:S(2)}) copy-start(bf16[768,128]{1,0:T(8,128)(2,1)S(1)} %add_convert_fusion.1.w_ref) | copy-start | bytes 589828
  120.5 12.3 %collective-permute-start.16 = (bf16[768,128]{1,0:T(8,128)(2,1)S(1)}, bf16[768,128]{1,0:T(8,128)(2,1)S(1)}, u32[]{:S(2)}, u32[]{:S(2)}) collective-permute-start(bf16[768,128]{1,0:T(8,128)(2,1)S(1)} %add_convert_fusion.1.w_ref), channel_id=1, source_target_pairs={{0,1},{1,0},{2,3},{3,2},{4,5},{5,4},{6,7},{7,6},{8,9},{9,8},{10,11... | collective-permute-start | bytes 589832 | tf_op jit(solution)/shard_map/ppermute | solution.py:341
  (10 other events, 18.8 us)
